TPU v7x, 512 devices: a whole 4x8x8 slice. The times are simulated.
512 devices in a mesh: row: 32 (over z, y_hi), mem: 8 (over x, core), lev: 2 (over y_lo).
Axes of the slice: x: 4, y: 8 (y_hi: 4, y_lo: 2; y = y_hi * 2 + y_lo), z: 8, core: 2. Of those that a mesh axis runs over, the one named last changes fastest.
Arguments:
- control_fields: bfloat16 [16, 6, 1024, 2048], P('mem', 'lev', 'row'), may hold values from -6 to 6
- perturbations: bfloat16 [3, 16, 6, 1024, 2048], P(None, 'mem', 'lev', 'row'), may hold values from -1.5 to 1.5
- column_taper: bfloat16 [2048, 2048], P('row'), may hold values from -1 to 2, as said below
- row_taper: bfloat16 [1024, 1024], P('row'), may hold values from -1 to 2, as said below
- courant_numbers: float32 [3, 6, 1024, 2048], P(None, 'lev', 'row', 'mem'), may hold values from -0.3 to 0.3
- tracer_slope: float32 [2, 6, 1024, 2048], P(None, 'lev', 'row', 'mem'), may hold values from -3 to 3
Outputs:
- increment: float32 [3, 6, 1024, 2048], P(None, 'lev', 'row', 'mem')
Inputs may be any that keep to these rules, and one draw needn't show every extreme that they name: `column_taper`: A square matrix. `row_taper`: A square matrix.
All inputs are finite; a program needn't handle non-finite values.
Results may differ from a plain program's by a relative error of at most 0.0048.
Values may be sent and summed in bfloat16 or wider, within the bound.
No kernel may reach another device: no remote copies, remote signals or barrier semaphores. Data moves between devices by JAX's collectives and lax.ppermute only.
A program may use at most 64 MiB of HBM per device.

v0:
```python
import jax
import jax.numpy as jnp
from jax import lax
from jax.sharding import Mesh
from jax.sharding import PartitionSpec as P

STEPS = 4
ROW = ("row_0", "row_1")


def gather_axes(x, axes, dim):
    if not axes:
        return x
    nearer = lax.all_gather(x, axes[-1], axis=dim, tiled=True)
    return gather_axes(nearer, axes[:-1], dim)


def split_up(x, dim, length):
    before, after = (x.shape[:dim], x.shape[dim + 1 :])
    return jnp.moveaxis(x.reshape(*before, length, -1, *after), dim, 0)


def summed_on_arrival(x, axis, dim):
    parts = split_up(x, dim, lax.axis_size(axis))
    arrived = lax.all_to_all(parts, axis, split_axis=0, concat_axis=0, tiled=True)
    return arrived.astype(jnp.float32).sum(axis=0)


def padded_2(x, sides, width):
    edges = {}
    for axis, dim in sides:
        size, length = (lax.axis_size(axis), x.shape[dim])
        up = [(i, (i + 1) % size) for i in range(size - 1)]
        last = lax.slice_in_dim(x, length - width, length, axis=dim)
        first = lax.slice_in_dim(x, 0, width, axis=dim)
        edges[dim] = (
            lax.ppermute(last, axis, up),
            lax.ppermute(first, axis, [(b, a) for a, b in up]),
        )
    done = []
    for _, dim in sides:
        low, high = edges[dim]
        around = [(width, width) if d in done else (0, 0) for d in range(x.ndim)]
        x = jnp.concatenate([jnp.pad(low, around), x, jnp.pad(high, around)], axis=dim)
        done.append(dim)
    return x


def upwind(middle, behind, forward, velocity):
    return jnp.maximum(velocity, 0.0) * (middle - behind) + jnp.minimum(velocity, 0.0) * (
        forward - middle
    )


def advance(present, courant_numbers, tracer_slope, padded):
    middle = padded[:, 1:-1, 1:-1, 1:-1]
    change = upwind(
        middle, padded[:, :-2, 1:-1, 1:-1], padded[:, 2:, 1:-1, 1:-1], courant_numbers[0]
    )
    change = change + upwind(
        middle, padded[:, 1:-1, :-2, 1:-1], padded[:, 1:-1, 2:, 1:-1], courant_numbers[1]
    )
    change = change + upwind(
        middle, padded[:, 1:-1, 1:-1, :-2], padded[:, 1:-1, 1:-1, 2:], courant_numbers[2]
    )
    shifted = present - change
    source = present[0] * tracer_slope[0] + present[1] * tracer_slope[1]
    return jnp.concatenate([shifted[:2], shifted[2:] - source[None]], axis=0)


def on_device(
    control_fields, perturbations, column_taper, row_taper, courant_numbers, tracer_slope
):
    member_count, level_count, row_count, column_count = control_fields.shape
    field_count = member_count * level_count
    flattened = control_fields.reshape(field_count * row_count, column_count)
    first_pass = jnp.dot(
        flattened,
        lax.all_gather(column_taper, ROW, axis=0, tiled=True),
        preferred_element_type=jnp.float32,
    )
    first_pass = first_pass.astype(jnp.bfloat16).reshape(field_count, row_count, column_count)
    row_whole = gather_axes(row_taper, ROW, 0)
    tapered = jnp.einsum(
        "ij,fjc->fic",
        row_whole,
        lax.all_to_all(first_pass, ROW, split_axis=2, concat_axis=1, tiled=True),
        preferred_element_type=jnp.float32,
    )
    localized = lax.all_to_all(
        tapered.astype(jnp.bfloat16), ROW, split_axis=1, concat_axis=2, tiled=True
    )
    localized = localized.reshape(member_count, level_count, row_count, column_count)
    weighted = jnp.einsum(
        "kmlrc,mlrc->klrc", perturbations, localized, preferred_element_type=jnp.float32
    )
    present = summed_on_arrival(weighted.astype(jnp.bfloat16), "mem", 3)
    for advect_step in range(STEPS):
        padded = padded_2(
            present.astype(jnp.bfloat16), ((ROW, 2), ("mem", 3), ("lev", 1)), 1
        ).astype(present.dtype)
        present = advance(present, courant_numbers, tracer_slope, padded)
    return present


def solution(mesh):
    torus = Mesh(
        mesh.devices.reshape(8, 4, mesh.shape["mem"], mesh.shape["lev"]),
        ("row_0", "row_1", "mem", "lev"),
    )
    placed = (
        P("mem", "lev", ROW, None),
        P(None, "mem", "lev", ROW, None),
        P(ROW, None),
        P(ROW, None),
        P(None, "lev", ROW, "mem"),
        P(None, "lev", ROW, "mem"),
    )
    return jax.shard_map(
        on_device,
        mesh=torus,
        in_specs=placed,
        out_specs=P(None, "lev", ROW, "mem"),
        check_vma=False,
    )
```

profile of v0, /device:TPU:73, one launch (start us, length us, event | category | flops | bytes accessed | tf_op | source)
XLA Modules:
  0.0 396.5 jit_solution(15193475571621653589)
XLA Ops:
  7.3 13.9 %all_gather.10 = bf16[128,1024]{1,0:T(8,128)(2,1)} all-gather(bf16[32,1024]{1,0:T(8,128)(2,1)} %param.9), channel_id=1, replica_groups=mesh['row_0'=8,'row_1'=4,'mem'=8,'lev'=2] {'row_1'}, dimensions={0}, use_global_device_ids=true | all-gather | bytes 327680 | tf_op jit(solution)/shard_map/all_gather | solution.py:14
  21.2 129.4 %all-gather.3.cloned.1.call-done = bf16[2048,2048]{1,0:T(8,128)(2,1)} async-done(((bf16[64,2048]{1,0:T(8,128)(2,1)}), bf16[2048,2048]{1,0:T(8,128)(2,1)}) %all-gather.3.cloned.1.call-update) | async-done | bytes 8388624 | tf_op jit(solution)/shard_map/all_gather | solution.py:79
  150.6 5.2 %convolution_convert_fusion = bf16[192,2048]{1,0:T(8,128)(2,1)S(1)} fusion(bf16[192,2048]{1,0:T(8,128)(2,1)S(1)} %bitcast.52, bf16[2048,2048]{1,0:T(8,128)(2,1)} %all-gather.3.cloned.1.call-done), kind=kOutput, calls=%fused_computation.1 | convolution fusion | flops 1611005952 | bytes 9961472 | tf_op jit(solution)/shard_map/dot_general | solution.py:77
  155.8 4.2 %copy.22 = bf16[6,32,2048]{1,0,2:T(8,128)(2,1)} copy(bf16[6,32,2048]{2,1,0:T(8,128)(2,1)S(1)} %bitcast.60) | data formatting | bytes 1572864 | tf_op jit(solution)/shard_map/reshape | solution.py:82
  160.0 5.8 %reshape.20 = bf16[32,2,6144]{2,1,0:T(2,128)(2,1)S(1)} reshape(bf16[2048,6,32]{2,1,0:T(8,128)(2,1)} %bitcast.53) | data formatting | bytes 1572864
  165.8 34.5 %all_to_all.38 = bf16[32,2,6144]{2,1,0:T(2,128)(2,1)S(1)} all-to-all(bf16[32,2,6144]{2,1,0:T(2,128)(2,1)S(1)} %reshape.20), channel_id=1, replica_groups=mesh['row_0'=8,'row_1'=4,'mem'=8,'lev'=2] {'row_0','row_1'}, dimensions={0} | all-to-all | bytes 1572864 | tf_op jit(solution)/shard_map/all_to_all | solution.py:87
  200.3 4.1 %reshape.21 = bf16[2048,6,32]{2,1,0:T(8,128)(2,1)} reshape(bf16[32,2,6144]{2,1,0:T(2,128)(2,1)S(1)} %all_to_all.38) | data formatting | bytes 1572864
  204.5 4.2 %copy.24 = bf16[6,32,32,64]{3,2,1,0:T(8,128)(2,1)S(1)} copy(bf16[6,32,32,64]{2,0,3,1:T(8,128)(2,1)} %bitcast.54) | data formatting | bytes 1572864 | tf_op jit(solution)/shard_map/all_to_all | solution.py:87
  208.7 4.3 %fusion.5 = bf16[6,1024,64]{1,2,0:T(8,128)(2,1)} fusion(bf16[6,1024,64]{2,1,0:T(8,128)(2,1)S(1)} %bitcast.59, bf16[1024,1024]{1,0:T(8,128)(2,1)} %all-gather.5.cloned.1.call-done), kind=kOutput, calls=%fused_computation.8 | convolution fusion | flops 805699584 | bytes 3670016 | tf_op jit(solution)/shard_map/ij,fjc->fic/dot_general | solution.py:84
  213.1 2.6 copy.26
  217.8 26.1 %all_to_all.39 = bf16[32,2,6144]{2,1,0:T(2,128)(2,1)} all-to-all(bf16[32,2,6144]{2,1,0:T(2,128)(2,1)} %reshape.22), channel_id=1, replica_groups=mesh['row_0'=8,'row_1'=4,'mem'=8,'lev'=2] {'row_0','row_1'}, dimensions={0} | all-to-all | bytes 1572864 | tf_op jit(solution)/shard_map/all_to_all | solution.py:90
  243.9 3.3 reshape.23
  249.4 2.8 reshape.15
  255.1 26.8 %all_to_all.40 = bf16[8,3,3,32,256]{4,3,2,1,0:T(8,128)(2,1)S(1)} all-to-all(bf16[8,3,3,32,256]{4,3,2,1,0:T(8,128)(2,1)S(1)} %copy.29), channel_id=1, replica_groups=mesh['row_0'=8,'row_1'=4,'mem'=8,'lev'=2] {'mem'}, dimensions={0} | all-to-all | bytes 2359296 | tf_op jit(solution)/shard_map/all_to_all | solution.py:25
  282.2 2.9 collective-permute-start.1
  285.2 3.5 collective-permute-start.2
  288.7 4.8 %collective-permute-start.3 = (bf16[3,3,1,256]{3,2,1,0:T(2,128)(2,1)S(1)}, bf16[3,3,1,256]{3,2,1,0:T(2,128)(2,1)S(1)}, u32[]{:S(2)}, u32[]{:S(2)}) collective-permute-start(bf16[3,3,1,256]{3,2,1,0:T(2,128)(2,1)S(1)} %get-tuple-element.30), channel_id=1, source_target_pairs={{16,0},{32,16},{48,32},{64,48},{80,64},{96,80},{112,96},{128,112},... | collective-permute-start | bytes 13832 | tf_op jit(solution)/shard_map/ppermute | solution.py:38
  294.8 10.6 %collective-permute-start.5 = (bf16[3,1,32,256]{3,2,1,0:T(8,128)(2,1)S(1)}, bf16[3,1,32,256]{3,2,1,0:T(8,128)(2,1)S(1)}, u32[]{:S(2)}, u32[]{:S(2)}) collective-permute-start(bf16[3,1,32,256]{3,2,1,0:T(8,128)(2,1)S(1)} %get-tuple-element.32), channel_id=1, source_target_pairs={{1,0},{3,2},{5,4},{7,6},{9,8},{11,10},{13,12},{15,14},{17,16},{19,... | collective-permute-start | bytes 147464 | tf_op jit(solution)/shard_map/ppermute | solution.py:38
  305.4 2.2 collective-permute-start.4
  307.7 3.4 collective-permute-done.4
  314.4 6.4 %collective-permute-start.9 = (bf16[3,3,1,256]{3,2,1,0:T(2,128)(2,1)S(1)}, bf16[3,3,1,256]{3,2,1,0:T(2,128)(2,1)S(1)}, u32[]{:S(2)}, u32[]{:S(2)}) collective-permute-start(bf16[3,3,1,256]{3,2,1,0:T(2,128)(2,1)S(1)} %get-tuple-element.24), channel_id=1, source_target_pairs={{16,0},{32,16},{48,32},{64,48},{80,64},{96,80},{112,96},{128,112},... | collective-permute-start | bytes 13832 | tf_op jit(solution)/shard_map/ppermute | solution.py:38
  322.1 4.0 %collective-permute-start.11 = (bf16[3,1,32,256]{3,2,1,0:T(8,128)(2,1)S(1)}, bf16[3,1,32,256]{3,2,1,0:T(8,128)(2,1)S(1)}, u32[]{:S(2)}, u32[]{:S(2)}) collective-permute-start(bf16[3,1,32,256]{3,2,1,0:T(8,128)(2,1)S(1)} %get-tuple-element.26), channel_id=1, source_target_pairs={{1,0},{3,2},{5,4},{7,6},{9,8},{11,10},{13,12},{15,14},{17,16},{19,... | collective-permute-start | bytes 147464 | tf_op jit(solution)/shard_map/ppermute | solution.py:38
  326.2 3.0 collective-permute-start.7
  332.5 4.4 %collective-permute-done.10 = bf16[3,3,32,1]{3,2,1,0:T(8,128)(2,1)S(1)} collective-permute-done((bf16[3,3,32,1]{3,2,1,0:T(8,128)(2,1)S(1)}, bf16[3,3,32,1]{3,2,1,0:T(8,128)(2,1)S(1)}, u32[]{:S(2)}, u32[]{:S(2)}) %collective-permute-start.10) | collective-permute-done | bytes 608 | tf_op jit(solution)/shard_map/ppermute | solution.py:38
  339.9 6.4 %collective-permute-start.15 = (bf16[3,3,1,256]{3,2,1,0:T(2,128)(2,1)S(1)}, bf16[3,3,1,256]{3,2,1,0:T(2,128)(2,1)S(1)}, u32[]{:S(2)}, u32[]{:S(2)}) collective-permute-start(bf16[3,3,1,256]{3,2,1,0:T(2,128)(2,1)S(1)} %get-tuple-element.18), channel_id=1, source_target_pairs={{16,0},{32,16},{48,32},{64,48},{80,64},{96,80},{112,96},{128,112},... | collective-permute-start | bytes 13832 | tf_op jit(solution)/shard_map/ppermute | solution.py:38
  347.6 4.0 %collective-permute-start.17 = (bf16[3,1,32,256]{3,2,1,0:T(8,128)(2,1)S(1)}, bf16[3,1,32,256]{3,2,1,0:T(8,128)(2,1)S(1)}, u32[]{:S(2)}, u32[]{:S(2)}) collective-permute-start(bf16[3,1,32,256]{3,2,1,0:T(8,128)(2,1)S(1)} %get-tuple-element.20), channel_id=1, source_target_pairs={{1,0},{3,2},{5,4},{7,6},{9,8},{11,10},{13,12},{15,14},{17,16},{19,... | collective-permute-start | bytes 147464 | tf_op jit(solution)/shard_map/ppermute | solution.py:38
  351.7 3.0 collective-permute-start.13
  358.0 4.4 %collective-permute-done.16 = bf16[3,3,32,1]{3,2,1,0:T(8,128)(2,1)S(1)} collective-permute-done((bf16[3,3,32,1]{3,2,1,0:T(8,128)(2,1)S(1)}, bf16[3,3,32,1]{3,2,1,0:T(8,128)(2,1)S(1)}, u32[]{:S(2)}, u32[]{:S(2)}) %collective-permute-start.16) | collective-permute-done | bytes 608 | tf_op jit(solution)/shard_map/ppermute | solution.py:38
  365.4 6.4 %collective-permute-start.21 = (bf16[3,3,1,256]{3,2,1,0:T(2,128)(2,1)S(1)}, bf16[3,3,1,256]{3,2,1,0:T(2,128)(2,1)S(1)}, u32[]{:S(2)}, u32[]{:S(2)}) collective-permute-start(bf16[3,3,1,256]{3,2,1,0:T(2,128)(2,1)S(1)} %get-tuple-element.12), channel_id=1, source_target_pairs={{16,0},{32,16},{48,32},{64,48},{80,64},{96,80},{112,96},{128,112},... | collective-permute-start | bytes 13832 | tf_op jit(solution)/shard_map/ppermute | solution.py:38
  373.1 4.0 %collective-permute-start.23 = (bf16[3,1,32,256]{3,2,1,0:T(8,128)(2,1)S(1)}, bf16[3,1,32,256]{3,2,1,0:T(8,128)(2,1)S(1)}, u32[]{:S(2)}, u32[]{:S(2)}) collective-permute-start(bf16[3,1,32,256]{3,2,1,0:T(8,128)(2,1)S(1)} %get-tuple-element.14), channel_id=1, source_target_pairs={{1,0},{3,2},{5,4},{7,6},{9,8},{11,10},{13,12},{15,14},{17,16},{19,... | collective-permute-start | bytes 147464 | tf_op jit(solution)/shard_map/ppermute | solution.py:38
  377.2 3.0 collective-permute-start.19
  383.5 4.4 %collective-permute-done.22 = bf16[3,3,32,1]{3,2,1,0:T(8,128)(2,1)S(1)} collective-permute-done((bf16[3,3,32,1]{3,2,1,0:T(8,128)(2,1)S(1)}, bf16[3,3,32,1]{3,2,1,0:T(8,128)(2,1)S(1)}, u32[]{:S(2)}, u32[]{:S(2)}) %collective-permute-start.22) | collective-permute-done | bytes 608 | tf_op jit(solution)/shard_map/ppermute | solution.py:38
  (84 shorter events, 34.7 us)
Async XLA Ops:
  6.5 144.1 %copy-start = (bf16[2,3,32,2048]{3,2,1,0:T(8,128)(2,1)S(1)}, bf16[2,3,32,2048]{3,2,1,0:T(8,128)(2,1)}, u32[]{:S(2)}) copy-start(bf16[2,3,32,2048]{3,2,1,0:T(8,128)(2,1)} %param.6) | copy-start | bytes 2359300
  6.5 144.1 %all-gather.3.cloned.1.call-start = ((), (), s32[]{:S(2)}) async-start(), calls=%async_computation.3 | async-start | bytes 8650752 | tf_op jit(solution)/shard_map/all_gather | solution.py:79
  7.3 201.5 %all-gather.5.cloned.1.call-start = ((), (), s32[]{:S(2)}) async-start(), calls=%async_computation.4 | async-start | bytes 2359296 | tf_op jit(solution)/shard_map/all_gather | solution.py:14
  252.2 1.7 copy-start.2
  255.1 52.5 %copy-start.3 = (f32[3,3,32,256]{3,2,1,0:T(8,128)S(1)}, f32[3,3,32,256]{3,2,1,0:T(8,128)}, u32[]{:S(2)}) copy-start(f32[3,3,32,256]{3,2,1,0:T(8,128)} %param.10) | copy-start | bytes 884740
  282.2 23.1 %collective-permute-start.1 = (bf16[3,3,32,1]{3,2,1,0:T(8,128)(2,1)S(1)}, bf16[3,3,32,1]{3,2,1,0:T(8,128)(2,1)S(1)}, u32[]{:S(2)}, u32[]{:S(2)}) collective-permute-start(bf16[3,3,32,1]{3,2,1,0:T(8,128)(2,1)S(1)} %get-tuple-element.33), channel_id=1, source_target_pairs={{0,2},{2,4},{4,6},{6,8},{8,10},{10,12},{12,14},{1,3},{3,5},{5,7},{... | collective-permute-start | bytes 1736 | tf_op jit(solution)/shard_map/ppermute | solution.py:37
  285.2 25.9 %collective-permute-start.2 = (bf16[3,3,1,256]{3,2,1,0:T(2,128)(2,1)S(1)}, bf16[3,3,1,256]{3,2,1,0:T(2,128)(2,1)S(1)}, u32[]{:S(2)}, u32[]{:S(2)}) collective-permute-start(bf16[3,3,1,256]{3,2,1,0:T(2,128)(2,1)S(1)} %get-tuple-element.29), channel_id=1, source_target_pairs={{0,16},{16,32},{32,48},{48,64},{64,80},{80,96},{96,112},{112,128},... | collective-permute-start | bytes 13832 | tf_op jit(solution)/shard_map/ppermute | solution.py:37
  288.7 22.3 %collective-permute-start.3 = (bf16[3,3,1,256]{3,2,1,0:T(2,128)(2,1)S(1)}, bf16[3,3,1,256]{3,2,1,0:T(2,128)(2,1)S(1)}, u32[]{:S(2)}, u32[]{:S(2)}) collective-permute-start(bf16[3,3,1,256]{3,2,1,0:T(2,128)(2,1)S(1)} %get-tuple-element.30), channel_id=1, source_target_pairs={{16,0},{32,16},{48,32},{64,48},{80,64},{96,80},{112,96},{128,112},... | collective-permute-start | bytes 13832 | tf_op jit(solution)/shard_map/ppermute | solution.py:38
  293.5 17.6 %collective-permute-start = (bf16[3,1,32,256]{3,2,1,0:T(8,128)(2,1)S(1)}, bf16[3,1,32,256]{3,2,1,0:T(8,128)(2,1)S(1)}, u32[]{:S(2)}, u32[]{:S(2)}) collective-permute-start(bf16[3,1,32,256]{3,2,1,0:T(8,128)(2,1)S(1)} %get-tuple-element.31), channel_id=1, source_target_pairs={{0,1},{2,3},{4,5},{6,7},{8,9},{10,11},{12,13},{14,15},{16,17},{18,... | collective-permute-start | bytes 147464 | tf_op jit(solution)/shard_map/ppermute | solution.py:37
  294.8 16.3 %collective-permute-start.5 = (bf16[3,1,32,256]{3,2,1,0:T(8,128)(2,1)S(1)}, bf16[3,1,32,256]{3,2,1,0:T(8,128)(2,1)S(1)}, u32[]{:S(2)}, u32[]{:S(2)}) collective-permute-start(bf16[3,1,32,256]{3,2,1,0:T(8,128)(2,1)S(1)} %get-tuple-element.32), channel_id=1, source_target_pairs={{1,0},{3,2},{5,4},{7,6},{9,8},{11,10},{13,12},{15,14},{17,16},{19,... | collective-permute-start | bytes 147464 | tf_op jit(solution)/shard_map/ppermute | solution.py:38
  305.4 5.7 %collective-permute-start.4 = (bf16[3,3,32,1]{3,2,1,0:T(8,128)(2,1)S(1)}, bf16[3,3,32,1]{3,2,1,0:T(8,128)(2,1)S(1)}, u32[]{:S(2)}, u32[]{:S(2)}) collective-permute-start(bf16[3,3,32,1]{3,2,1,0:T(8,128)(2,1)S(1)} %get-tuple-element.34), channel_id=1, source_target_pairs={{2,0},{4,2},{6,4},{8,6},{10,8},{12,10},{14,12},{3,1},{5,3},{7,5},{... | collective-permute-start | bytes 1736 | tf_op jit(solution)/shard_map/ppermute | solution.py:38
  311.5 0.9 copy-start.1
  312.5 24.4 %collective-permute-start.8 = (bf16[3,3,1,256]{3,2,1,0:T(2,128)(2,1)S(1)}, bf16[3,3,1,256]{3,2,1,0:T(2,128)(2,1)S(1)}, u32[]{:S(2)}, u32[]{:S(2)}) collective-permute-start(bf16[3,3,1,256]{3,2,1,0:T(2,128)(2,1)S(1)} %get-tuple-element.23), channel_id=1, source_target_pairs={{0,16},{16,32},{32,48},{48,64},{64,80},{80,96},{96,112},{112,128},... | collective-permute-start | bytes 13832 | tf_op jit(solution)/shard_map/ppermute | solution.py:37
  314.4 22.5 %collective-permute-start.9 = (bf16[3,3,1,256]{3,2,1,0:T(2,128)(2,1)S(1)}, bf16[3,3,1,256]{3,2,1,0:T(2,128)(2,1)S(1)}, u32[]{:S(2)}, u32[]{:S(2)}) collective-permute-start(bf16[3,3,1,256]{3,2,1,0:T(2,128)(2,1)S(1)} %get-tuple-element.24), channel_id=1, source_target_pairs={{16,0},{32,16},{48,32},{64,48},{80,64},{96,80},{112,96},{128,112},... | collective-permute-start | bytes 13832 | tf_op jit(solution)/shard_map/ppermute | solution.py:38
  320.8 16.1 %collective-permute-start.6 = (bf16[3,1,32,256]{3,2,1,0:T(8,128)(2,1)S(1)}, bf16[3,1,32,256]{3,2,1,0:T(8,128)(2,1)S(1)}, u32[]{:S(2)}, u32[]{:S(2)}) collective-permute-start(bf16[3,1,32,256]{3,2,1,0:T(8,128)(2,1)S(1)} %get-tuple-element.25), channel_id=1, source_target_pairs={{0,1},{2,3},{4,5},{6,7},{8,9},{10,11},{12,13},{14,15},{16,17},{18,... | collective-permute-start | bytes 147464 | tf_op jit(solution)/shard_map/ppermute | solution.py:37
  322.1 14.8 %collective-permute-start.11 = (bf16[3,1,32,256]{3,2,1,0:T(8,128)(2,1)S(1)}, bf16[3,1,32,256]{3,2,1,0:T(8,128)(2,1)S(1)}, u32[]{:S(2)}, u32[]{:S(2)}) collective-permute-start(bf16[3,1,32,256]{3,2,1,0:T(8,128)(2,1)S(1)} %get-tuple-element.26), channel_id=1, source_target_pairs={{1,0},{3,2},{5,4},{7,6},{9,8},{11,10},{13,12},{15,14},{17,16},{19,... | collective-permute-start | bytes 147464 | tf_op jit(solution)/shard_map/ppermute | solution.py:38
  326.2 4.4 %collective-permute-start.7 = (bf16[3,3,32,1]{3,2,1,0:T(8,128)(2,1)S(1)}, bf16[3,3,32,1]{3,2,1,0:T(8,128)(2,1)S(1)}, u32[]{:S(2)}, u32[]{:S(2)}) collective-permute-start(bf16[3,3,32,1]{3,2,1,0:T(8,128)(2,1)S(1)} %get-tuple-element.27), channel_id=1, source_target_pairs={{0,2},{2,4},{4,6},{6,8},{8,10},{10,12},{12,14},{1,3},{3,5},{5,7},{... | collective-permute-start | bytes 1736 | tf_op jit(solution)/shard_map/ppermute | solution.py:37
  330.6 6.3 %collective-permute-start.10 = (bf16[3,3,32,1]{3,2,1,0:T(8,128)(2,1)S(1)}, bf16[3,3,32,1]{3,2,1,0:T(8,128)(2,1)S(1)}, u32[]{:S(2)}, u32[]{:S(2)}) collective-permute-start(bf16[3,3,32,1]{3,2,1,0:T(8,128)(2,1)S(1)} %get-tuple-element.28), channel_id=1, source_target_pairs={{2,0},{4,2},{6,4},{8,6},{10,8},{12,10},{14,12},{3,1},{5,3},{7,5},{... | collective-permute-start | bytes 1736 | tf_op jit(solution)/shard_map/ppermute | solution.py:38
  338.0 24.4 %collective-permute-start.14 = (bf16[3,3,1,256]{3,2,1,0:T(2,128)(2,1)S(1)}, bf16[3,3,1,256]{3,2,1,0:T(2,128)(2,1)S(1)}, u32[]{:S(2)}, u32[]{:S(2)}) collective-permute-start(bf16[3,3,1,256]{3,2,1,0:T(2,128)(2,1)S(1)} %get-tuple-element.17), channel_id=1, source_target_pairs={{0,16},{16,32},{32,48},{48,64},{64,80},{80,96},{96,112},{112,128},... | collective-permute-start | bytes 13832 | tf_op jit(solution)/shard_map/ppermute | solution.py:37
  339.9 22.5 %collective-permute-start.15 = (bf16[3,3,1,256]{3,2,1,0:T(2,128)(2,1)S(1)}, bf16[3,3,1,256]{3,2,1,0:T(2,128)(2,1)S(1)}, u32[]{:S(2)}, u32[]{:S(2)}) collective-permute-start(bf16[3,3,1,256]{3,2,1,0:T(2,128)(2,1)S(1)} %get-tuple-element.18), channel_id=1, source_target_pairs={{16,0},{32,16},{48,32},{64,48},{80,64},{96,80},{112,96},{128,112},... | collective-permute-start | bytes 13832 | tf_op jit(solution)/shard_map/ppermute | solution.py:38
  346.3 16.1 %collective-permute-start.12 = (bf16[3,1,32,256]{3,2,1,0:T(8,128)(2,1)S(1)}, bf16[3,1,32,256]{3,2,1,0:T(8,128)(2,1)S(1)}, u32[]{:S(2)}, u32[]{:S(2)}) collective-permute-start(bf16[3,1,32,256]{3,2,1,0:T(8,128)(2,1)S(1)} %get-tuple-element.19), channel_id=1, source_target_pairs={{0,1},{2,3},{4,5},{6,7},{8,9},{10,11},{12,13},{14,15},{16,17},{18,... | collective-permute-start | bytes 147464 | tf_op jit(solution)/shard_map/ppermute | solution.py:37
  347.6 14.8 %collective-permute-start.17 = (bf16[3,1,32,256]{3,2,1,0:T(8,128)(2,1)S(1)}, bf16[3,1,32,256]{3,2,1,0:T(8,128)(2,1)S(1)}, u32[]{:S(2)}, u32[]{:S(2)}) collective-permute-start(bf16[3,1,32,256]{3,2,1,0:T(8,128)(2,1)S(1)} %get-tuple-element.20), channel_id=1, source_target_pairs={{1,0},{3,2},{5,4},{7,6},{9,8},{11,10},{13,12},{15,14},{17,16},{19,... | collective-permute-start | bytes 147464 | tf_op jit(solution)/shard_map/ppermute | solution.py:38
  351.7 4.4 %collective-permute-start.13 = (bf16[3,3,32,1]{3,2,1,0:T(8,128)(2,1)S(1)}, bf16[3,3,32,1]{3,2,1,0:T(8,128)(2,1)S(1)}, u32[]{:S(2)}, u32[]{:S(2)}) collective-permute-start(bf16[3,3,32,1]{3,2,1,0:T(8,128)(2,1)S(1)} %get-tuple-element.21), channel_id=1, source_target_pairs={{0,2},{2,4},{4,6},{6,8},{8,10},{10,12},{12,14},{1,3},{3,5},{5,7},{... | collective-permute-start | bytes 1736 | tf_op jit(solution)/shard_map/ppermute | solution.py:37
  356.1 6.3 %collective-permute-start.16 = (bf16[3,3,32,1]{3,2,1,0:T(8,128)(2,1)S(1)}, bf16[3,3,32,1]{3,2,1,0:T(8,128)(2,1)S(1)}, u32[]{:S(2)}, u32[]{:S(2)}) collective-permute-start(bf16[3,3,32,1]{3,2,1,0:T(8,128)(2,1)S(1)} %get-tuple-element.22), channel_id=1, source_target_pairs={{2,0},{4,2},{6,4},{8,6},{10,8},{12,10},{14,12},{3,1},{5,3},{7,5},{... | collective-permute-start | bytes 1736 | tf_op jit(solution)/shard_map/ppermute | solution.py:38
  363.5 24.4 %collective-permute-start.20 = (bf16[3,3,1,256]{3,2,1,0:T(2,128)(2,1)S(1)}, bf16[3,3,1,256]{3,2,1,0:T(2,128)(2,1)S(1)}, u32[]{:S(2)}, u32[]{:S(2)}) collective-permute-start(bf16[3,3,1,256]{3,2,1,0:T(2,128)(2,1)S(1)} %get-tuple-element.11), channel_id=1, source_target_pairs={{0,16},{16,32},{32,48},{48,64},{64,80},{80,96},{96,112},{112,128},... | collective-permute-start | bytes 13832 | tf_op jit(solution)/shard_map/ppermute | solution.py:37
  365.4 22.4 %collective-permute-start.21 = (bf16[3,3,1,256]{3,2,1,0:T(2,128)(2,1)S(1)}, bf16[3,3,1,256]{3,2,1,0:T(2,128)(2,1)S(1)}, u32[]{:S(2)}, u32[]{:S(2)}) collective-permute-start(bf16[3,3,1,256]{3,2,1,0:T(2,128)(2,1)S(1)} %get-tuple-element.12), channel_id=1, source_target_pairs={{16,0},{32,16},{48,32},{64,48},{80,64},{96,80},{112,96},{128,112},... | collective-permute-start | bytes 13832 | tf_op jit(solution)/shard_map/ppermute | solution.py:38
  371.8 16.1 %collective-permute-start.18 = (bf16[3,1,32,256]{3,2,1,0:T(8,128)(2,1)S(1)}, bf16[3,1,32,256]{3,2,1,0:T(8,128)(2,1)S(1)}, u32[]{:S(2)}, u32[]{:S(2)}) collective-permute-start(bf16[3,1,32,256]{3,2,1,0:T(8,128)(2,1)S(1)} %get-tuple-element.13), channel_id=1, source_target_pairs={{0,1},{2,3},{4,5},{6,7},{8,9},{10,11},{12,13},{14,15},{16,17},{18,... | collective-permute-start | bytes 147464 | tf_op jit(solution)/shard_map/ppermute | solution.py:37
  373.1 14.8 %collective-permute-start.23 = (bf16[3,1,32,256]{3,2,1,0:T(8,128)(2,1)S(1)}, bf16[3,1,32,256]{3,2,1,0:T(8,128)(2,1)S(1)}, u32[]{:S(2)}, u32[]{:S(2)}) collective-permute-start(bf16[3,1,32,256]{3,2,1,0:T(8,128)(2,1)S(1)} %get-tuple-element.14), channel_id=1, source_target_pairs={{1,0},{3,2},{5,4},{7,6},{9,8},{11,10},{13,12},{15,14},{17,16},{19,... | collective-permute-start | bytes 147464 | tf_op jit(solution)/shard_map/ppermute | solution.py:38
  377.2 4.4 %collective-permute-start.19 = (bf16[3,3,32,1]{3,2,1,0:T(8,128)(2,1)S(1)}, bf16[3,3,32,1]{3,2,1,0:T(8,128)(2,1)S(1)}, u32[]{:S(2)}, u32[]{:S(2)}) collective-permute-start(bf16[3,3,32,1]{3,2,1,0:T(8,128)(2,1)S(1)} %get-tuple-element.15), channel_id=1, source_target_pairs={{0,2},{2,4},{4,6},{6,8},{8,10},{10,12},{12,14},{1,3},{3,5},{5,7},{... | collective-permute-start | bytes 1736 | tf_op jit(solution)/shard_map/ppermute | solution.py:37
  381.6 6.3 %collective-permute-start.22 = (bf16[3,3,32,1]{3,2,1,0:T(8,128)(2,1)S(1)}, bf16[3,3,32,1]{3,2,1,0:T(8,128)(2,1)S(1)}, u32[]{:S(2)}, u32[]{:S(2)}) collective-permute-start(bf16[3,3,32,1]{3,2,1,0:T(8,128)(2,1)S(1)} %get-tuple-element.16), channel_id=1, source_target_pairs={{2,0},{4,2},{6,4},{8,6},{10,8},{12,10},{14,12},{3,1},{5,3},{7,5},{... | collective-permute-start | bytes 1736 | tf_op jit(solution)/shard_map/ppermute | solution.py:38
Sparse Core Ops, SparseCore 0:
  10.5 140.0 all-gather.2
  152.7 55.8 all-gather.4
where the time goes:
time: 398 us; the launch traced here: 396 us
  waiting for transfers between devices  151 us (38%)
  blocking collectives  101 us (25%)
  starting transfers between devices  80.7 us (20%)
  local copies, waits for them, and re-layouts  34.4 us (9%)
  between operations  14 us (4%)
  matrix products  9.51 us (2%)
  other arithmetic  5.67 us (1%)
    all_gather x1, waiting for transfers between devices, on_device(): lax.all_gather(column_taper, ROW, axis=0, tiled=True)  129 us
    ppermute x12, starting transfers between devices, padded_2(): lax.ppermute(first, axis, [(b, a) for a, b in up])  54.3 us
    all_to_all x1, blocking collectives, on_device(): lax.all_to_all(first_pass, ROW, split_axis=2, concat_axis=1, tiled=True)  34.5 us
    all_to_all x1, blocking collectives, summed_on_arrival(): lax.all_to_all(parts, axis, split_axis=0, concat_axis=0, tiled=True)  26.8 us
    ppermute x12, starting transfers between devices, padded_2(): lax.ppermute(last, axis, up)  26.4 us
    all_to_all x1, blocking collectives, on_device(): lax.all_to_all(tapered.astype(jnp.bfloat16), ROW, split_axis=1, concat_ax...  26.1 us
    unnamed x13, local copies, waits for them, and re-layouts  17.6 us
    ppermute x12, waiting for transfers between devices, padded_2(): lax.ppermute(first, axis, [(b, a) for a, b in up])  16.5 us
  transfers between devices with their start and end apart: 26, of which 8 were waited for; matrix products, arithmetic and copies ran while one was open for 6% of the time, Pallas kernels for 0%

commit v1 on v0

v1 whole, which is shorter than its diff:
```python
import jax
import jax.numpy as jnp
from jax import lax
from jax.experimental import pallas as pl
from jax.experimental.pallas import tpu as pltpu
from jax.sharding import PartitionSpec as P

STEPS = 4
BF = jnp.bfloat16
F32 = jnp.float32


def room(mebibytes):
    return pltpu.CompilerParams(vmem_limit_bytes=mebibytes * 1024 * 1024)


def in_hbm(x):
    return pltpu.with_memory_space_constraint(x, pltpu.HBM)


def shaped(shape, dtype):
    return jax.ShapeDtypeStruct(shape, dtype)


def slices_kernel(_, column_ref, row_ref, out_ref):
    tall = column_ref.shape[0]
    half = row_ref.shape[0] // 2
    wide = row_ref.shape[1]
    peers = out_ref.shape[0]
    out_ref[:, :tall, :] = jnp.broadcast_to(column_ref[...][None], (peers, *column_ref.shape))
    upper, lower = (row_ref[:half, :], row_ref[half:, :])
    out_ref[:, tall:, :wide] = jnp.broadcast_to(upper[None], (peers, half, wide))
    out_ref[:, tall:, wide:] = jnp.broadcast_to(lower[None], (peers, half, wide))


def taper_slices(at, column_taper, row_taper, peers, parts):
    tall, wide = (column_taper.shape[0], column_taper.shape[1] // parts)
    rows, narrow = (row_taper.shape[0], row_taper.shape[1] // parts)
    return pl.pallas_call(
        slices_kernel,
        out_shape=shaped((peers, tall + rows // 2, wide), BF),
        grid_spec=pltpu.PrefetchScalarGridSpec(
            num_scalar_prefetch=1,
            grid=(1,),
            in_specs=[
                pl.BlockSpec((tall, wide), lambda i, at: (0, at[0])),
                pl.BlockSpec((rows, narrow), lambda i, at: (0, at[0])),
            ],
            out_specs=pl.BlockSpec((peers, tall + rows // 2, wide), lambda i, at: (0, 0, 0)),
        ),
        compiler_params=room(6),
        name="taper_slices",
    )(at, column_taper, row_taper)


def row_part_kernel(tall, slices_ref, out_ref):
    half = slices_ref.shape[1] - tall
    wide = out_ref.shape[2]
    out_ref[:, :half, :] = slices_ref[:, tall:, :wide]
    out_ref[:, half:, :] = slices_ref[:, tall:, wide:]


def row_part(slices, tall, settled):
    peers, height, wide = slices.shape
    return pl.pallas_call(
        lambda a, *rest: row_part_kernel(tall, a, rest[-1]),
        out_shape=shaped((peers, 2 * (height - tall), wide // 2), BF),
        in_specs=[pl.BlockSpec(memory_space=pltpu.VMEM)]
        + [pl.BlockSpec(memory_space=pl.ANY)] * len(settled),
        compiler_params=room(4),
        name="row_part",
    )(slices, *settled)


def columns_kernel(tall, fields_ref, slices_ref, out_ref):
    units, levels, rows, wide = out_ref.shape
    taper = slices_ref[:, :tall, :].reshape(-1, slices_ref.shape[2])
    product = jnp.dot(fields_ref[...], taper, preferred_element_type=F32).astype(BF)
    for member in range(units // 2):
        for side in range(2):
            part = product[
                member * levels * rows : (member + 1) * levels * rows,
                side * wide : (side + 1) * wide,
            ]
            out_ref[member * 2 + side] = part.reshape(levels, rows, wide)


def columns_pass(fields, slices, tall, levels, rows, parts):
    count, depth = fields.shape
    peers, height, wide = slices.shape
    units = 2 * count // (levels * rows)
    return pl.pallas_call(
        lambda a, b, c: columns_kernel(tall, a, b, c),
        out_shape=shaped((units, levels, rows, wide // 2), BF),
        grid=(parts,),
        in_specs=[
            pl.BlockSpec((count // parts, depth), lambda i: (i, 0)),
            pl.BlockSpec((peers, height, wide), lambda i: (0, 0, 0)),
        ],
        out_specs=pl.BlockSpec((units // parts, levels, rows, wide // 2), lambda i: (i, 0, 0, 0)),
        compiler_params=room(14),
        name="columns_pass",
    )(in_hbm(fields), slices)


def rows_kernel(taper_ref, fields_ref, *refs):
    out_ref, whole_ref = refs[-2:]
    peers, levels, rows, wide = fields_ref.shape

    @pl.when(pl.program_id(0) == 0)
    def _():
        for level in range(levels):
            whole_ref[:, level * wide : (level + 1) * wide] = fields_ref[:, level].reshape(
                peers * rows, wide
            )

    taper = jnp.concatenate([taper_ref[i] for i in range(taper_ref.shape[0])], axis=1)
    product = jnp.dot(taper, whole_ref[...], preferred_element_type=F32).astype(BF)
    for level in range(levels):
        out_ref[:, level] = product[:, level * wide : (level + 1) * wide].reshape(-1, rows, wide)


def rows_pass(taper, fields, blocks, settled):
    peers, levels, rows, wide = fields.shape
    parts, height, narrow = taper.shape
    return pl.pallas_call(
        rows_kernel,
        out_shape=shaped((peers, levels, rows, wide), BF),
        grid=(blocks,),
        in_specs=[
            pl.BlockSpec((parts, height // blocks, narrow), lambda i: (0, i, 0)),
            pl.BlockSpec((peers, levels, rows, wide), lambda i: (0, 0, 0, 0)),
        ]
        + [pl.BlockSpec(memory_space=pl.ANY)] * len(settled),
        out_specs=pl.BlockSpec((peers // blocks, levels, rows, wide), lambda i: (i, 0, 0, 0)),
        scratch_shapes=[pltpu.VMEM((height, levels * wide), BF)],
        compiler_params=room(10),
        name="rows_pass",
    )(in_hbm(taper), fields, *settled)


def split_kernel(at_ref, fields_ref, *out_refs):
    wide = out_refs[0].shape[-1]
    for step, out_ref in enumerate(out_refs):
        start = pl.multiple_of((at_ref[0] ^ step) * wide, wide)
        out_ref[...] = fields_ref[:, :, :, :, pl.ds(start, wide)]


def split_columns(at, fields, parts):
    shape = (*fields.shape[:-1], fields.shape[-1] // parts)
    return pl.pallas_call(
        split_kernel,
        out_shape=[shaped(shape, BF)] * parts,
        in_specs=[
            pl.BlockSpec(memory_space=pltpu.SMEM),
            pl.BlockSpec(memory_space=pltpu.VMEM),
        ],
        out_specs=[pl.BlockSpec(memory_space=pltpu.VMEM)] * parts,
        compiler_params=room(8),
        name="split_columns",
    )(at, fields)


def weight_kernel(parts, at_ref, localized_ref, *refs):
    weights = refs[:parts]
    out_ref, whole_ref, first_ref, last_ref = refs[parts:]
    variables, members, levels = weights[0].shape[:3]
    wide = localized_ref.shape[-1]
    for level in range(levels):
        for side in range(2):
            lanes = slice(side * wide, (side + 1) * wide)
            sums = [None] * variables
            for step in range(parts):
                base = (at_ref[0] ^ step) * (2 * members)
                for member in range(members):
                    field = localized_ref[base + 2 * member + side, level].astype(F32)
                    for k in range(variables):
                        term = weights[step][k, member, level, :, lanes].astype(F32) * field
                        sums[k] = term if sums[k] is None else sums[k] + term
            for k in range(variables):
                out_ref[k, level, :, lanes] = sums[k]
                rounded = sums[k].astype(BF)
                whole_ref[k, level, :, lanes] = rounded
                (first_ref, last_ref)[side][k, level] = rounded


def weighted_sum(at, localized, weights):
    variables, _, levels, rows, wide = weights[0].shape
    shape = (variables, levels, rows, wide)
    edge = (variables, levels, rows, wide // 2)
    vmem = pl.BlockSpec(memory_space=pltpu.VMEM)
    return pl.pallas_call(
        lambda *refs: weight_kernel(len(weights), *refs),
        out_shape=[shaped(shape, F32), shaped(shape, BF), shaped(edge, BF), shaped(edge, BF)],
        in_specs=[pl.BlockSpec(memory_space=pltpu.SMEM)] + [vmem] * (1 + len(weights)),
        out_specs=[vmem] * 4,
        compiler_params=room(8),
        name="weighted_sum",
    )(at, localized, *weights)


def beside(from_left, from_right):
    lane = lax.broadcasted_iota(jnp.int32, from_left.shape, from_left.ndim - 1)
    wide = from_left.shape[-1]
    none = jnp.zeros_like(from_left)
    kept = jnp.where(lane >= wide - STEPS, from_left, none)
    return jnp.where(lane < STEPS, from_right, kept)


def above_below(from_next, from_previous):
    row = lax.broadcasted_iota(jnp.int32, from_next.shape, from_next.ndim - 2)
    return jnp.where(row < STEPS, from_next, from_previous)


def strips_kernel(own_ref, other_ref, *refs):
    (left, right, other_left, other_right), (top_ref, bottom_ref) = (refs[:4], refs[4:])
    variables, levels, rows, wide = own_ref.shape
    for rows_at, out_ref in ((slice(0, 8), top_ref), (slice(rows - 8, rows), bottom_ref)):
        for k in range(variables):
            for level in range(levels):
                for base, body, l_ref, r_ref in (
                    (0, own_ref, left, right),
                    (levels, other_ref, other_left, other_right),
                ):
                    out_ref[k, base + level, :, :wide] = body[k, level, rows_at]
                    sides = beside(
                        l_ref[k, level, rows_at].astype(F32), r_ref[k, level, rows_at].astype(F32)
                    )
                    out_ref[k, base + level, :, wide:] = sides.astype(BF)


def row_strips(own, other, *sides):
    variables, levels, rows, wide = own.shape
    shape = (variables, 2 * levels, 8, wide + sides[0].shape[-1])
    return pl.pallas_call(
        strips_kernel,
        out_shape=[shaped(shape, BF)] * 2,
        compiler_params=room(4),
        name="row_strips",
    )(own, other, *sides)


def advect_kernel(*refs):
    (
        flip_ref,
        own_ref,
        other_ref,
        left_ref,
        right_ref,
        other_left_ref,
        other_right_ref,
        next_ref,
        previous_ref,
        courant_ref,
        slope_ref,
        beside_ref,
        around_ref,
        opposite_ref,
        out_ref,
        first_ref,
        second_ref,
        terms_ref,
    ) = refs
    variables, levels, rows, wide = own_ref.shape
    deep, tall, full = first_ref.shape[1:]
    flip = flip_ref[0]
    sign = (1 - 2 * flip).astype(F32)
    directions = courant_ref.shape[0]

    def local(level):
        return jnp.where(flip == 1, levels - 1 - level, level)

    for level in range(deep):
        at = local(level % levels)
        mine = level < levels
        for k in range(variables):
            body, l_ref, r_ref = (
                (own_ref, left_ref, right_ref)
                if mine
                else (other_ref, other_left_ref, other_right_ref)
            )
            first_ref[k, level, :rows, :wide] = body[k, at].astype(F32)
            first_ref[k, level, :rows, wide:] = beside(
                l_ref[k, at].astype(F32), r_ref[k, at].astype(F32)
            )
            strip = at if mine else at + levels
            first_ref[k, level, rows:, :] = above_below(
                next_ref[k, strip].astype(F32), previous_ref[k, strip].astype(F32)
            )
        planes = []
        for a in range(directions + slope_ref.shape[0]):
            if mine:
                body = courant_ref[a, at] if a < directions else slope_ref[a - directions, at]
                upper = jnp.concatenate([body, beside_ref[a, at].astype(F32)], axis=1)
                plane = jnp.concatenate([upper, around_ref[a, at].astype(F32)], axis=0)
            else:
                plane = opposite_ref[a, at].astype(F32)
            planes.append(plane)
        planes[0] = planes[0] * sign
        kept = 1.0 - sum(jnp.abs(c) for c in planes[:directions])
        terms_ref[0, level] = kept
        for a in range(directions):
            terms_ref[1 + 2 * a, level] = jnp.maximum(planes[a], 0.0)
            terms_ref[2 + 2 * a, level] = -jnp.minimum(planes[a], 0.0)
        for a in range(directions, len(planes)):
            terms_ref[1 + directions + a, level] = planes[a]

    old_ref, new_ref = (first_ref, second_ref)
    for step in range(STEPS):
        reached = min(deep, levels + STEPS - 1 - step)
        last = step == STEPS - 1
        for level in range(reached):
            states = [old_ref[k, level] for k in range(variables)]
            for k in range(variables):
                state = states[k]
                total = terms_ref[0, level] * state
                if level > 0:
                    total = total + terms_ref[1, level] * old_ref[k, level - 1]
                if level + 1 < deep:
                    total = total + terms_ref[2, level] * old_ref[k, level + 1]
                total = total + terms_ref[3, level] * pltpu.roll(state, 1, 0)
                total = total + terms_ref[4, level] * pltpu.roll(state, tall - 1, 0)
                total = total + terms_ref[5, level] * pltpu.roll(state, 1, 1)
                total = total + terms_ref[6, level] * pltpu.roll(state, full - 1, 1)
                if k == 2:
                    total = total - (states[0] * terms_ref[7, level] + states[1] * terms_ref[8, level])
                if last:
                    out_ref[k, local(level)] = total[:rows, :wide]
                else:
                    new_ref[k, level] = total
        old_ref, new_ref = (new_ref, old_ref)


def advect(flip, *arrays):
    variables, levels, rows, wide = arrays[0].shape
    tall, full = (rows + 8, wide + arrays[2].shape[-1])
    vmem = pl.BlockSpec(memory_space=pltpu.VMEM)
    state = pltpu.VMEM((variables, 2 * levels, tall, full), F32)
    return pl.pallas_call(
        advect_kernel,
        out_shape=shaped((variables, levels, rows, wide), F32),
        in_specs=[pl.BlockSpec(memory_space=pltpu.SMEM)] + [vmem] * len(arrays),
        out_specs=vmem,
        scratch_shapes=[state, state, pltpu.VMEM((9, 2 * levels, tall, full), F32)],
        compiler_params=room(14),
        name="advect",
    )(flip, *arrays)


def chain(axis, step):
    size = lax.axis_size(axis)
    return [(i, i + step) for i in range(size) if 0 <= i + step < size]


def swap(axis):
    return [(0, 1), (1, 0)]


def neighbours(first, last, axis):
    from_left = lax.ppermute(last, axis, chain(axis, 1))
    from_right = lax.ppermute(first, axis, chain(axis, -1))
    return from_left, from_right


def across(first, last):
    size = lax.axis_size("mem")
    up = [(2 * i + k, 2 * (i + 1) + 1 - k) for i in range(size - 1) for k in range(2)]
    down = [(2 * (i + 1) + k, 2 * i + 1 - k) for i in range(size - 1) for k in range(2)]
    axes = ("mem", "lev")
    return lax.ppermute(last, axes, up), lax.ppermute(first, axes, down)


def background(courant_numbers, tracer_slope):
    whole = jnp.concatenate([courant_numbers, tracer_slope], axis=0).astype(BF)
    half = whole.shape[-1] // 2
    sides = beside(*neighbours(whole[..., :half], whole[..., half:], "mem"))
    wider = jnp.concatenate([whole, sides], axis=-1)
    from_previous, from_next = neighbours(wider[:, :, :8], wider[:, :, -8:], "row")
    around = above_below(from_next, from_previous)
    taller = jnp.concatenate([wider, around], axis=2)
    return sides, around, lax.ppermute(taller, "lev", swap("lev"))


def on_device(
    control_fields, perturbations, column_taper, row_taper, courant_numbers, tracer_slope
):
    members, levels, rows, columns = control_fields.shape
    parts, peers = (lax.axis_size("mem"), lax.axis_size("row"))
    tall = column_taper.shape[0]
    at = lax.axis_index("mem").astype(jnp.int32).reshape(1)
    flip = lax.axis_index("lev").astype(jnp.int32).reshape(1)

    every = lax.all_gather(
        control_fields.reshape(members * levels * rows, columns), "mem", axis=0, tiled=True
    )
    slices = lax.all_to_all(
        taper_slices(at, column_taper, row_taper, peers, parts), "row", 0, 0, tiled=True
    )
    sides, around, opposite = background(courant_numbers, tracer_slope)
    pieces = split_columns(at, perturbations, parts)
    weights = [pieces[0]]
    for step in range(1, parts):
        weights.append(lax.ppermute(pieces[step], "mem", [(i, i ^ step) for i in range(parts)]))
    first_pass = columns_pass(every, slices, tall, levels, rows, 4)
    row_whole = lax.all_gather(row_part(slices, tall, weights[1:]), "mem", axis=0, tiled=False)
    row_whole = row_whole.reshape(parts, row_taper.shape[1], -1)
    arrived = lax.all_to_all(first_pass, "row", 0, 0, tiled=True)
    tapered = rows_pass(row_whole, arrived, 4, [opposite])
    localized = lax.all_to_all(tapered, "row", 0, 0, tiled=True)
    own, rounded, first, last = weighted_sum(at, localized, weights)

    other = lax.ppermute(rounded, "lev", swap("lev"))
    left, right = neighbours(first, last, "mem")
    other_left, other_right = across(first, last)
    top, bottom = row_strips(rounded, other, left, right, other_left, other_right)
    from_previous, from_next = neighbours(top, bottom, "row")
    return advect(
        flip,
        own,
        other,
        left,
        right,
        other_left,
        other_right,
        from_next,
        from_previous,
        courant_numbers,
        tracer_slope,
        sides,
        around,
        opposite,
    )


def solution(mesh):
    grid = P(None, "lev", "row", "mem")
    placed = (
        P("mem", "lev", "row", None),
        P(None, "mem", "lev", "row", None),
        P("row", None),
        P("row", None),
        grid,
        grid,
    )
    return jax.shard_map(
        on_device, mesh=mesh, in_specs=placed, out_specs=grid, check_vma=False
    )
```

time: 398 us -> 226 us (0.57)
  the two profiles are of different devices: /device:TPU:73 before, /device:TPU:137 now
where the time goes in v1:
time: 226 us; the launch traced here: 225 us
  starting transfers between devices  95.3 us (42%)
  waiting for transfers between devices  64.6 us (29%)
  blocking collectives  29.6 us (13%)
  Pallas kernels  14.4 us (6%)
  between operations  13.7 us (6%)
  local copies, waits for them, and re-layouts  4.86 us (2%)
    ppermute x7, waiting for transfers between devices, on_device(): lax.ppermute(pieces[step], 'mem', [(i, i ^ step) for i in range(parts)])  31.4 us
    all_to_all x1, blocking collectives, on_device(): localized = lax.all_to_all(tapered, 'row', 0, 0, tiled=True)  29.6 us
    ppermute x7, starting transfers between devices, on_device(): lax.ppermute(pieces[step], 'mem', [(i, i ^ step) for i in range(parts)])  25.3 us
    ppermute x4, waiting for transfers between devices, neighbours(): from_left = lax.ppermute(last, axis, chain(axis, 1))  13.1 us
    all_to_all x1, starting transfers between devices, on_device(): lax.all_to_all(taper_slices(at, column_taper, row_taper, peers, parts), '...  13 us
    ppermute x2, starting transfers between devices, across(): return (lax.ppermute(last, axes, up), lax.ppermute(first, axes, down))  13 us
    ppermute x4, starting transfers between devices, neighbours(): from_left = lax.ppermute(last, axis, chain(axis, 1))  12.7 us
    ppermute x4, starting transfers between devices, neighbours(): from_right = lax.ppermute(first, axis, chain(axis, -1))  11.8 us
  transfers between devices with their start and end apart: 23, of which 12 were waited for; matrix products, arithmetic and copies ran while one was open for 1% of the time, Pallas kernels for 3%

profile of v1, /device:TPU:137, one launch (start us, length us, event | category | flops | bytes accessed | tf_op | source)
XLA Modules:
  0.0 224.7 jit_solution(4607494461382356207)
XLA Ops:
  10.2 13.0 %all-to-all-start = ((bf16[32,80,256]{2,1,0:T(8,128)(2,1)}), bf16[32,80,256]{2,1,0:T(8,128)(2,1)S(1)}, u32[]{:S(2)}, u32[]{:S(2)}) async-start(bf16[32,80,256]{2,1,0:T(8,128)(2,1)} %taper_slices.1), calls=%async_computation | async-start | bytes 2621440 | tf_op jit(solution)/shard_map/all_to_all | solution.py:396
  26.0 3.1 %collective-permute-start = (bf16[3,2,3,32,256]{4,3,2,1,0:T(8,128)(2,1)S(1)}, bf16[3,2,3,32,256]{4,3,2,1,0:T(8,128)(2,1)S(1)}, u32[]{:S(2)}, u32[]{:S(2)}) collective-permute-start(bf16[3,2,3,32,256]{4,3,2,1,0:T(8,128)(2,1)S(1)} %get-tuple-element.19), channel_id=1, source_target_pairs={{0,2},{2,0},{4,6},{6,4},{8,10},{10,8},{12,14},{14,12},{1,3},{3,1},... | collective-permute-start | bytes 884744 | tf_op jit(solution)/shard_map/ppermute | solution.py:403
  29.2 3.1 %collective-permute-start.1 = (bf16[3,2,3,32,256]{4,3,2,1,0:T(8,128)(2,1)S(1)}, bf16[3,2,3,32,256]{4,3,2,1,0:T(8,128)(2,1)S(1)}, u32[]{:S(2)}, u32[]{:S(2)}) collective-permute-start(bf16[3,2,3,32,256]{4,3,2,1,0:T(8,128)(2,1)S(1)} %get-tuple-element.20), channel_id=1, source_target_pairs={{0,4},{2,6},{4,0},{6,2},{8,12},{10,14},{12,8},{14,10},{1,5},{3,7},... | collective-permute-start | bytes 884744 | tf_op jit(solution)/shard_map/ppermute | solution.py:403
  32.3 2.3 %collective-permute-start.2 = (bf16[3,2,3,32,256]{4,3,2,1,0:T(8,128)(2,1)S(1)}, bf16[3,2,3,32,256]{4,3,2,1,0:T(8,128)(2,1)S(1)}, u32[]{:S(2)}, u32[]{:S(2)}) collective-permute-start(bf16[3,2,3,32,256]{4,3,2,1,0:T(8,128)(2,1)S(1)} %get-tuple-element.21), channel_id=1, source_target_pairs={{0,6},{2,4},{4,2},{6,0},{8,14},{10,12},{12,10},{14,8},{1,7},{3,5},... | collective-permute-start | bytes 884744 | tf_op jit(solution)/shard_map/ppermute | solution.py:403
  34.6 4.7 %collective-permute-start.3 = (bf16[3,2,3,32,256]{4,3,2,1,0:T(8,128)(2,1)S(1)}, bf16[3,2,3,32,256]{4,3,2,1,0:T(8,128)(2,1)S(1)}, u32[]{:S(2)}, u32[]{:S(2)}) collective-permute-start(bf16[3,2,3,32,256]{4,3,2,1,0:T(8,128)(2,1)S(1)} %get-tuple-element.22), channel_id=1, source_target_pairs={{0,8},{2,10},{4,12},{6,14},{8,0},{10,2},{12,4},{14,6},{1,9},{3,11}... | collective-permute-start | bytes 884744 | tf_op jit(solution)/shard_map/ppermute | solution.py:403
  39.3 2.5 %collective-permute-start.4 = (bf16[3,2,3,32,256]{4,3,2,1,0:T(8,128)(2,1)S(1)}, bf16[3,2,3,32,256]{4,3,2,1,0:T(8,128)(2,1)S(1)}, u32[]{:S(2)}, u32[]{:S(2)}) collective-permute-start(bf16[3,2,3,32,256]{4,3,2,1,0:T(8,128)(2,1)S(1)} %get-tuple-element.23), channel_id=1, source_target_pairs={{0,10},{2,8},{4,14},{6,12},{8,2},{10,0},{12,6},{14,4},{1,11},{3,9}... | collective-permute-start | bytes 884744 | tf_op jit(solution)/shard_map/ppermute | solution.py:403
  41.8 4.4 %collective-permute-start.5 = (bf16[3,2,3,32,256]{4,3,2,1,0:T(8,128)(2,1)S(1)}, bf16[3,2,3,32,256]{4,3,2,1,0:T(8,128)(2,1)S(1)}, u32[]{:S(2)}, u32[]{:S(2)}) collective-permute-start(bf16[3,2,3,32,256]{4,3,2,1,0:T(8,128)(2,1)S(1)} %get-tuple-element.24), channel_id=1, source_target_pairs={{0,12},{2,14},{4,8},{6,10},{8,4},{10,6},{12,0},{14,2},{1,13},{3,15... | collective-permute-start | bytes 884744 | tf_op jit(solution)/shard_map/ppermute | solution.py:403
  46.3 5.2 %collective-permute-start.6 = (bf16[3,2,3,32,256]{4,3,2,1,0:T(8,128)(2,1)S(1)}, bf16[3,2,3,32,256]{4,3,2,1,0:T(8,128)(2,1)S(1)}, u32[]{:S(2)}, u32[]{:S(2)}) collective-permute-start(bf16[3,2,3,32,256]{4,3,2,1,0:T(8,128)(2,1)S(1)} %get-tuple-element.25), channel_id=1, source_target_pairs={{0,14},{2,12},{4,10},{6,8},{8,6},{10,4},{12,2},{14,0},{1,15},{3,13... | collective-permute-start | bytes 884744 | tf_op jit(solution)/shard_map/ppermute | solution.py:403
  51.5 8.1 %collective-permute-done.2.rest_2_.refs_5_ = bf16[3,2,3,32,256]{4,3,2,1,0:T(8,128)(2,1)S(1)} collective-permute-done((bf16[3,2,3,32,256]{4,3,2,1,0:T(8,128)(2,1)S(1)}, bf16[3,2,3,32,256]{4,3,2,1,0:T(8,128)(2,1)S(1)}, u32[]{:S(2)}, u32[]{:S(2)}) %collective-permute-start.2) | collective-permute-done | bytes 294944 | tf_op jit(solution)/shard_map/ppermute | solution.py:403
  59.6 14.1 %collective-permute-done.3.rest_3_.refs_6_ = bf16[3,2,3,32,256]{4,3,2,1,0:T(8,128)(2,1)S(1)} collective-permute-done((bf16[3,2,3,32,256]{4,3,2,1,0:T(8,128)(2,1)S(1)}, bf16[3,2,3,32,256]{4,3,2,1,0:T(8,128)(2,1)S(1)}, u32[]{:S(2)}, u32[]{:S(2)}) %collective-permute-start.3) | collective-permute-done | bytes 294944 | tf_op jit(solution)/shard_map/ppermute | solution.py:403
  73.7 9.1 %collective-permute-done.4.rest_4_.refs_7_ = bf16[3,2,3,32,256]{4,3,2,1,0:T(8,128)(2,1)S(1)} collective-permute-done((bf16[3,2,3,32,256]{4,3,2,1,0:T(8,128)(2,1)S(1)}, bf16[3,2,3,32,256]{4,3,2,1,0:T(8,128)(2,1)S(1)}, u32[]{:S(2)}, u32[]{:S(2)}) %collective-permute-start.4) | collective-permute-done | bytes 294944 | tf_op jit(solution)/shard_map/ppermute | solution.py:403
  83.6 5.5 %columns_pass.1 = bf16[32,3,32,128]{3,2,1,0:T(8,128)(2,1)} custom-call(bf16[1536,2048]{1,0:T(8,128)(2,1)} %all-gather.4.cloned.1.call-done.a, bf16[32,80,256]{2,1,0:T(8,128)(2,1)S(1)} %all-to-all-done.a.b), custom_call_target="tpu_custom_call" | custom-call | tf_op jit(solution)/shard_map/columns_pass/pallas_call | solution.py:92
  89.1 11.2 %all-to-all-start.1 = ((bf16[32,3,32,128]{3,2,1,0:T(8,128)(2,1)}), bf16[32,3,32,128]{3,2,1,0:T(8,128)(2,1)S(1)}, u32[]{:S(2)}, u32[]{:S(2)}) async-start(bf16[32,3,32,128]{3,2,1,0:T(8,128)(2,1)} %columns_pass.1), calls=%async_computation.1 | async-start | bytes 1572864 | tf_op jit(solution)/shard_map/all_to_all | solution.py:407
  102.3 3.7 %collective-permute-start.8 = (bf16[5,3,32,128]{3,2,1,0:T(8,128)(2,1)S(1)}, bf16[5,3,32,128]{3,2,1,0:T(8,128)(2,1)S(1)}, u32[]{:S(2)}, u32[]{:S(2)}) collective-permute-start(bf16[5,3,32,128]{3,2,1,0:T(8,128)(2,1)S(1)} %get-tuple-element.35), channel_id=1, source_target_pairs={{0,2},{2,4},{4,6},{6,8},{8,10},{10,12},{12,14},{1,3},{3,5},{5,7},{... | collective-permute-start | bytes 368648 | tf_op jit(solution)/shard_map/ppermute | solution.py:360
  108.0 2.3 %collective-permute-done.8 = bf16[5,3,32,128]{3,2,1,0:T(8,128)(2,1)S(1)} collective-permute-done((bf16[5,3,32,128]{3,2,1,0:T(8,128)(2,1)S(1)}, bf16[5,3,32,128]{3,2,1,0:T(8,128)(2,1)S(1)}, u32[]{:S(2)}, u32[]{:S(2)}) %collective-permute-start.8) | collective-permute-done | bytes 122912 | tf_op jit(solution)/shard_map/ppermute | solution.py:360
  110.3 3.7 %collective-permute-done.7 = bf16[5,3,32,128]{3,2,1,0:T(8,128)(2,1)S(1)} collective-permute-done((bf16[5,3,32,128]{3,2,1,0:T(8,128)(2,1)S(1)}, bf16[5,3,32,128]{3,2,1,0:T(8,128)(2,1)S(1)}, u32[]{:S(2)}, u32[]{:S(2)}) %collective-permute-start.7) | collective-permute-done | bytes 122912 | tf_op jit(solution)/shard_map/ppermute | solution.py:361
  114.0 4.0 %collective-permute-start.10 = (bf16[5,3,8,384]{3,2,1,0:T(8,128)(2,1)S(1)}, bf16[5,3,8,384]{3,2,1,0:T(8,128)(2,1)S(1)}, u32[]{:S(2)}, u32[]{:S(2)}) collective-permute-start(bf16[5,3,8,384]{3,2,1,0:T(8,128)(2,1)S(1)} %get-tuple-element.33), channel_id=1, source_target_pairs={{0,16},{16,32},{32,48},{48,64},{64,80},{80,96},{96,112},{112,128},... | collective-permute-start | bytes 276488 | tf_op jit(solution)/shard_map/ppermute | solution.py:360
  118.0 4.3 %collective-permute-start.9 = (bf16[5,3,8,384]{3,2,1,0:T(8,128)(2,1)S(1)}, bf16[5,3,8,384]{3,2,1,0:T(8,128)(2,1)S(1)}, u32[]{:S(2)}, u32[]{:S(2)}) collective-permute-start(bf16[5,3,8,384]{3,2,1,0:T(8,128)(2,1)S(1)} %get-tuple-element.34), channel_id=1, source_target_pairs={{16,0},{32,16},{48,32},{64,48},{80,64},{96,80},{112,96},{128,112},... | collective-permute-start | bytes 276488 | tf_op jit(solution)/shard_map/ppermute | solution.py:361
  122.3 4.3 %collective-permute-done.10 = bf16[5,3,8,384]{3,2,1,0:T(8,128)(2,1)S(1)} collective-permute-done((bf16[5,3,8,384]{3,2,1,0:T(8,128)(2,1)S(1)}, bf16[5,3,8,384]{3,2,1,0:T(8,128)(2,1)S(1)}, u32[]{:S(2)}, u32[]{:S(2)}) %collective-permute-start.10) | collective-permute-done | bytes 92192 | tf_op jit(solution)/shard_map/ppermute | solution.py:360
  126.7 2.9 %collective-permute-start.11 = (bf16[5,3,40,384]{3,2,1,0:T(8,128)(2,1)S(1)}, bf16[5,3,40,384]{3,2,1,0:T(8,128)(2,1)S(1)}, u32[]{:S(2)}, u32[]{:S(2)}) collective-permute-start(bf16[5,3,40,384]{3,2,1,0:T(8,128)(2,1)S(1)} %pad_maximum_fusion), channel_id=1, source_target_pairs={{0,1},{1,0},{2,3},{3,2},{4,5},{5,4},{6,7},{7,6},{8,9},{9,8},{10,11... | collective-permute-start | bytes 1382408 | tf_op jit(solution)/shard_map/ppermute | solution.py:381
  129.7 10.7 %collective-permute-done.11.refs_0_.refs_13_ = bf16[5,3,40,384]{3,2,1,0:T(8,128)(2,1)S(1)} collective-permute-done((bf16[5,3,40,384]{3,2,1,0:T(8,128)(2,1)S(1)}, bf16[5,3,40,384]{3,2,1,0:T(8,128)(2,1)S(1)}, u32[]{:S(2)}, u32[]{:S(2)}) %collective-permute-start.11) | collective-permute-done | bytes 460832 | tf_op jit(solution)/shard_map/ppermute | solution.py:381
  140.4 3.7 %rows_pass.1 = bf16[32,3,32,128]{3,2,1,0:T(8,128)(2,1)S(1)} custom-call(bf16[8,1024,128]{2,1,0:T(8,128)(2,1)} %bitcast.4, bf16[32,3,32,128]{3,2,1,0:T(8,128)(2,1)S(1)} %all-to-all-done.1.fields_ref, bf16[5,3,40,384]{3,2,1,0:T(8,128)(2,1)S(1)} %collective-permute-done.11.refs_0_.refs_13_), custom_call_target="tpu_custom_call" | custom-call | tf_op jit(solution)/shard_map/rows_pass/pallas_call | solution.py:126
  144.1 29.6 %all_to_all.15.refs_1_ = bf16[32,3,32,128]{3,2,1,0:T(8,128)(2,1)S(1)} all-to-all(bf16[32,3,32,128]{3,2,1,0:T(8,128)(2,1)S(1)} %rows_pass.1), channel_id=1, replica_groups=mesh['row'=32,'mem'=8,'lev'=2] {'row'}, dimensions={0} | all-to-all | bytes 1572864 | tf_op jit(solution)/shard_map/all_to_all | solution.py:409
  174.2 5.3 %collective-permute-start.12 = (bf16[3,3,32,256]{3,2,1,0:T(8,128)(2,1)S(1)}, bf16[3,3,32,256]{3,2,1,0:T(8,128)(2,1)S(1)}, u32[]{:S(2)}, u32[]{:S(2)}) collective-permute-start(bf16[3,3,32,256]{3,2,1,0:T(8,128)(2,1)S(1)} %get-tuple-element.28.own_ref), channel_id=1, source_target_pairs={{0,1},{1,0},{2,3},{3,2},{4,5},{5,4},{6,7},{7,6},{8,9},{9,8},{10,11... | collective-permute-start | bytes 442376 | tf_op jit(solution)/shard_map/ppermute | solution.py:412
  179.5 9.5 %collective-permute-start.15 = (bf16[3,3,32,128]{3,2,1,0:T(8,128)(2,1)S(1)}, bf16[3,3,32,128]{3,2,1,0:T(8,128)(2,1)S(1)}, u32[]{:S(2)}, u32[]{:S(2)}) collective-permute-start(bf16[3,3,32,128]{3,2,1,0:T(8,128)(2,1)S(1)} %get-tuple-element.29), channel_id=1, source_target_pairs={{0,3},{1,2},{2,5},{3,4},{4,7},{5,6},{6,9},{7,8},{8,11},{9,10},{10,... | collective-permute-start | bytes 221192 | tf_op jit(solution)/shard_map/ppermute | solution.py:370
  189.0 2.5 %collective-permute-start.13 = (bf16[3,3,32,128]{3,2,1,0:T(8,128)(2,1)S(1)}, bf16[3,3,32,128]{3,2,1,0:T(8,128)(2,1)S(1)}, u32[]{:S(2)}, u32[]{:S(2)}) collective-permute-start(bf16[3,3,32,128]{3,2,1,0:T(8,128)(2,1)S(1)} %get-tuple-element.29), channel_id=1, source_target_pairs={{0,2},{2,4},{4,6},{6,8},{8,10},{10,12},{12,14},{1,3},{3,5},{5,7},{... | collective-permute-start | bytes 221192 | tf_op jit(solution)/shard_map/ppermute | solution.py:360
  191.5 3.5 %collective-permute-start.16 = (bf16[3,3,32,128]{3,2,1,0:T(8,128)(2,1)S(1)}, bf16[3,3,32,128]{3,2,1,0:T(8,128)(2,1)S(1)}, u32[]{:S(2)}, u32[]{:S(2)}) collective-permute-start(bf16[3,3,32,128]{3,2,1,0:T(8,128)(2,1)S(1)} %get-tuple-element.30), channel_id=1, source_target_pairs={{2,1},{3,0},{4,3},{5,2},{6,5},{7,4},{8,7},{9,6},{10,9},{11,8},{12,... | collective-permute-start | bytes 221192 | tf_op jit(solution)/shard_map/ppermute | solution.py:370
  198.1 2.6 %collective-permute-done.14.refs_1_.refs_4_ = bf16[3,3,32,128]{3,2,1,0:T(8,128)(2,1)S(1)} collective-permute-done((bf16[3,3,32,128]{3,2,1,0:T(8,128)(2,1)S(1)}, bf16[3,3,32,128]{3,2,1,0:T(8,128)(2,1)S(1)}, u32[]{:S(2)}, u32[]{:S(2)}) %collective-permute-start.14) | collective-permute-done | bytes 73760 | tf_op jit(solution)/shard_map/ppermute | solution.py:361
  200.7 3.7 %collective-permute-start.17 = (bf16[3,6,8,384]{3,2,1,0:T(8,128)(2,1)S(1)}, bf16[3,6,8,384]{3,2,1,0:T(8,128)(2,1)S(1)}, u32[]{:S(2)}, u32[]{:S(2)}) collective-permute-start(bf16[3,6,8,384]{3,2,1,0:T(8,128)(2,1)S(1)} %get-tuple-element.31), channel_id=1, source_target_pairs={{16,0},{32,16},{48,32},{64,48},{80,64},{96,80},{112,96},{128,112},... | collective-permute-start | bytes 331784 | tf_op jit(solution)/shard_map/ppermute | solution.py:361
  204.4 2.5 %collective-permute-start.18 = (bf16[3,6,8,384]{3,2,1,0:T(8,128)(2,1)S(1)}, bf16[3,6,8,384]{3,2,1,0:T(8,128)(2,1)S(1)}, u32[]{:S(2)}, u32[]{:S(2)}) collective-permute-start(bf16[3,6,8,384]{3,2,1,0:T(8,128)(2,1)S(1)} %get-tuple-element.32), channel_id=1, source_target_pairs={{0,16},{16,32},{32,48},{48,64},{64,80},{80,96},{96,112},{112,128},... | collective-permute-start | bytes 331784 | tf_op jit(solution)/shard_map/ppermute | solution.py:360
  208.1 6.6 %collective-permute-done.18.refs_8_ = bf16[3,6,8,384]{3,2,1,0:T(8,128)(2,1)S(1)} collective-permute-done((bf16[3,6,8,384]{3,2,1,0:T(8,128)(2,1)S(1)}, bf16[3,6,8,384]{3,2,1,0:T(8,128)(2,1)S(1)}, u32[]{:S(2)}, u32[]{:S(2)}) %collective-permute-start.18) | collective-permute-done | bytes 110624 | tf_op jit(solution)/shard_map/ppermute | solution.py:360
  214.7 3.2 %advect.1 = f32[3,3,32,256]{3,2,1,0:T(8,128)} custom-call(s32[1]{0:T(128)} %bitcast.refs_0_, f32[3,3,32,256]{3,2,1,0:T(8,128)S(1)} %get-tuple-element.27.refs_1_, bf16[3,3,32,256]{3,2,1,0:T(8,128)(2,1)S(1)} %collective-permute-done.12.other_ref.refs_2_, bf16[3,3,32,128]{3,2,1,0:T(8,128)(2,1)S(1)} %collective-permute-done.13.refs_0_.refs_3_, ...), custom_call_target="tpu_custom_call" | custom-call | tf_op jit(solution)/shard_map/advect/pallas_call | solution.py:339
  (50 shorter events, 16.3 us)
Async XLA Ops:
  6.5 77.1 %all-gather.4.cloned.1.call-start = ((), (), s32[]{:S(2)}) async-start(), calls=%async_computation.3 | async-start | bytes 7077888 | tf_op jit(solution)/shard_map/all_gather | solution.py:393
  7.3 1.0 copy-start.6
  8.2 0.8 copy-start.7
  10.2 72.6 %all-to-all-start = ((bf16[32,80,256]{2,1,0:T(8,128)(2,1)}), bf16[32,80,256]{2,1,0:T(8,128)(2,1)S(1)}, u32[]{:S(2)}, u32[]{:S(2)}) async-start(bf16[32,80,256]{2,1,0:T(8,128)(2,1)} %taper_slices.1), calls=%async_computation | async-start | bytes 2621440 | tf_op jit(solution)/shard_map/all_to_all | solution.py:396
  23.3 117.1 %all-gather.6.cloned.1.call-start = ((), (), s32[]{:S(2)}) async-start(), calls=%async_computation.4 | async-start | bytes 2359296 | tf_op jit(solution)/shard_map/all_gather | solution.py:405
  23.3 1.7 copy-start
  25.3 0.7 copy-start.4
  26.0 15.8 %collective-permute-start = (bf16[3,2,3,32,256]{4,3,2,1,0:T(8,128)(2,1)S(1)}, bf16[3,2,3,32,256]{4,3,2,1,0:T(8,128)(2,1)S(1)}, u32[]{:S(2)}, u32[]{:S(2)}) collective-permute-start(bf16[3,2,3,32,256]{4,3,2,1,0:T(8,128)(2,1)S(1)} %get-tuple-element.19), channel_id=1, source_target_pairs={{0,2},{2,0},{4,6},{6,4},{8,10},{10,8},{12,14},{14,12},{1,3},{3,1},... | collective-permute-start | bytes 884744 | tf_op jit(solution)/shard_map/ppermute | solution.py:403
  29.2 17.2 %collective-permute-start.1 = (bf16[3,2,3,32,256]{4,3,2,1,0:T(8,128)(2,1)S(1)}, bf16[3,2,3,32,256]{4,3,2,1,0:T(8,128)(2,1)S(1)}, u32[]{:S(2)}, u32[]{:S(2)}) collective-permute-start(bf16[3,2,3,32,256]{4,3,2,1,0:T(8,128)(2,1)S(1)} %get-tuple-element.20), channel_id=1, source_target_pairs={{0,4},{2,6},{4,0},{6,2},{8,12},{10,14},{12,8},{14,10},{1,5},{3,7},... | collective-permute-start | bytes 884744 | tf_op jit(solution)/shard_map/ppermute | solution.py:403
  32.3 27.3 %collective-permute-start.2 = (bf16[3,2,3,32,256]{4,3,2,1,0:T(8,128)(2,1)S(1)}, bf16[3,2,3,32,256]{4,3,2,1,0:T(8,128)(2,1)S(1)}, u32[]{:S(2)}, u32[]{:S(2)}) collective-permute-start(bf16[3,2,3,32,256]{4,3,2,1,0:T(8,128)(2,1)S(1)} %get-tuple-element.21), channel_id=1, source_target_pairs={{0,6},{2,4},{4,2},{6,0},{8,14},{10,12},{12,10},{14,8},{1,7},{3,5},... | collective-permute-start | bytes 884744 | tf_op jit(solution)/shard_map/ppermute | solution.py:403
  34.6 39.1 %collective-permute-start.3 = (bf16[3,2,3,32,256]{4,3,2,1,0:T(8,128)(2,1)S(1)}, bf16[3,2,3,32,256]{4,3,2,1,0:T(8,128)(2,1)S(1)}, u32[]{:S(2)}, u32[]{:S(2)}) collective-permute-start(bf16[3,2,3,32,256]{4,3,2,1,0:T(8,128)(2,1)S(1)} %get-tuple-element.22), channel_id=1, source_target_pairs={{0,8},{2,10},{4,12},{6,14},{8,0},{10,2},{12,4},{14,6},{1,9},{3,11}... | collective-permute-start | bytes 884744 | tf_op jit(solution)/shard_map/ppermute | solution.py:403
  39.3 43.5 %collective-permute-start.4 = (bf16[3,2,3,32,256]{4,3,2,1,0:T(8,128)(2,1)S(1)}, bf16[3,2,3,32,256]{4,3,2,1,0:T(8,128)(2,1)S(1)}, u32[]{:S(2)}, u32[]{:S(2)}) collective-permute-start(bf16[3,2,3,32,256]{4,3,2,1,0:T(8,128)(2,1)S(1)} %get-tuple-element.23), channel_id=1, source_target_pairs={{0,10},{2,8},{4,14},{6,12},{8,2},{10,0},{12,6},{14,4},{1,11},{3,9}... | collective-permute-start | bytes 884744 | tf_op jit(solution)/shard_map/ppermute | solution.py:403
  41.8 41.0 %collective-permute-start.5 = (bf16[3,2,3,32,256]{4,3,2,1,0:T(8,128)(2,1)S(1)}, bf16[3,2,3,32,256]{4,3,2,1,0:T(8,128)(2,1)S(1)}, u32[]{:S(2)}, u32[]{:S(2)}) collective-permute-start(bf16[3,2,3,32,256]{4,3,2,1,0:T(8,128)(2,1)S(1)} %get-tuple-element.24), channel_id=1, source_target_pairs={{0,12},{2,14},{4,8},{6,10},{8,4},{10,6},{12,0},{14,2},{1,13},{3,15... | collective-permute-start | bytes 884744 | tf_op jit(solution)/shard_map/ppermute | solution.py:403
  46.3 36.5 %collective-permute-start.6 = (bf16[3,2,3,32,256]{4,3,2,1,0:T(8,128)(2,1)S(1)}, bf16[3,2,3,32,256]{4,3,2,1,0:T(8,128)(2,1)S(1)}, u32[]{:S(2)}, u32[]{:S(2)}) collective-permute-start(bf16[3,2,3,32,256]{4,3,2,1,0:T(8,128)(2,1)S(1)} %get-tuple-element.25), channel_id=1, source_target_pairs={{0,14},{2,12},{4,10},{6,8},{8,6},{10,4},{12,2},{14,0},{1,15},{3,13... | collective-permute-start | bytes 884744 | tf_op jit(solution)/shard_map/ppermute | solution.py:403
  82.9 0.7 copy-start.2
  89.1 51.3 %all-to-all-start.1 = ((bf16[32,3,32,128]{3,2,1,0:T(8,128)(2,1)}), bf16[32,3,32,128]{3,2,1,0:T(8,128)(2,1)S(1)}, u32[]{:S(2)}, u32[]{:S(2)}) async-start(bf16[32,3,32,128]{3,2,1,0:T(8,128)(2,1)} %columns_pass.1), calls=%async_computation.1 | async-start | bytes 1572864 | tf_op jit(solution)/shard_map/all_to_all | solution.py:407
  102.3 8.0 %collective-permute-start.8 = (bf16[5,3,32,128]{3,2,1,0:T(8,128)(2,1)S(1)}, bf16[5,3,32,128]{3,2,1,0:T(8,128)(2,1)S(1)}, u32[]{:S(2)}, u32[]{:S(2)}) collective-permute-start(bf16[5,3,32,128]{3,2,1,0:T(8,128)(2,1)S(1)} %get-tuple-element.35), channel_id=1, source_target_pairs={{0,2},{2,4},{4,6},{6,8},{8,10},{10,12},{12,14},{1,3},{3,5},{5,7},{... | collective-permute-start | bytes 368648 | tf_op jit(solution)/shard_map/ppermute | solution.py:360
  106.0 7.9 %collective-permute-start.7 = (bf16[5,3,32,128]{3,2,1,0:T(8,128)(2,1)S(1)}, bf16[5,3,32,128]{3,2,1,0:T(8,128)(2,1)S(1)}, u32[]{:S(2)}, u32[]{:S(2)}) collective-permute-start(bf16[5,3,32,128]{3,2,1,0:T(8,128)(2,1)S(1)} %get-tuple-element.36), channel_id=1, source_target_pairs={{2,0},{4,2},{6,4},{8,6},{10,8},{12,10},{14,12},{3,1},{5,3},{7,5},{... | collective-permute-start | bytes 368648 | tf_op jit(solution)/shard_map/ppermute | solution.py:361
  114.0 12.6 %collective-permute-start.10 = (bf16[5,3,8,384]{3,2,1,0:T(8,128)(2,1)S(1)}, bf16[5,3,8,384]{3,2,1,0:T(8,128)(2,1)S(1)}, u32[]{:S(2)}, u32[]{:S(2)}) collective-permute-start(bf16[5,3,8,384]{3,2,1,0:T(8,128)(2,1)S(1)} %get-tuple-element.33), channel_id=1, source_target_pairs={{0,16},{16,32},{32,48},{48,64},{64,80},{80,96},{96,112},{112,128},... | collective-permute-start | bytes 276488 | tf_op jit(solution)/shard_map/ppermute | solution.py:360
  118.0 8.6 %collective-permute-start.9 = (bf16[5,3,8,384]{3,2,1,0:T(8,128)(2,1)S(1)}, bf16[5,3,8,384]{3,2,1,0:T(8,128)(2,1)S(1)}, u32[]{:S(2)}, u32[]{:S(2)}) collective-permute-start(bf16[5,3,8,384]{3,2,1,0:T(8,128)(2,1)S(1)} %get-tuple-element.34), channel_id=1, source_target_pairs={{16,0},{32,16},{48,32},{64,48},{80,64},{96,80},{112,96},{128,112},... | collective-permute-start | bytes 276488 | tf_op jit(solution)/shard_map/ppermute | solution.py:361
  126.7 13.6 %collective-permute-start.11 = (bf16[5,3,40,384]{3,2,1,0:T(8,128)(2,1)S(1)}, bf16[5,3,40,384]{3,2,1,0:T(8,128)(2,1)S(1)}, u32[]{:S(2)}, u32[]{:S(2)}) collective-permute-start(bf16[5,3,40,384]{3,2,1,0:T(8,128)(2,1)S(1)} %pad_maximum_fusion), channel_id=1, source_target_pairs={{0,1},{1,0},{2,3},{3,2},{4,5},{5,4},{6,7},{7,6},{8,9},{9,8},{10,11... | collective-permute-start | bytes 1382408 | tf_op jit(solution)/shard_map/ppermute | solution.py:381
  140.4 33.3 %copy-start.5 = (bf16[3,2,3,32,256]{4,3,2,1,0:T(8,128)(2,1)S(1)}, bf16[3,2,3,32,256]{4,3,2,1,0:T(8,128)(2,1)}, u32[]{:S(2)}) copy-start(bf16[3,2,3,32,256]{4,3,2,1,0:T(8,128)(2,1)} %copy-done.4) | copy-start | bytes 884740
  173.7 41.0 %copy-start.1 = (f32[3,3,32,256]{3,2,1,0:T(8,128)S(1)}, f32[3,3,32,256]{3,2,1,0:T(8,128)}, u32[]{:S(2)}) copy-start(f32[3,3,32,256]{3,2,1,0:T(8,128)} %refs_9_.1) | copy-start | bytes 884740
  173.7 41.0 %copy-start.3 = (f32[2,3,32,256]{3,2,1,0:T(8,128)S(1)}, f32[2,3,32,256]{3,2,1,0:T(8,128)}, u32[]{:S(2)}) copy-start(f32[2,3,32,256]{3,2,1,0:T(8,128)} %refs_10_.1) | copy-start | bytes 589828
  174.2 26.4 %collective-permute-start.12 = (bf16[3,3,32,256]{3,2,1,0:T(8,128)(2,1)S(1)}, bf16[3,3,32,256]{3,2,1,0:T(8,128)(2,1)S(1)}, u32[]{:S(2)}, u32[]{:S(2)}) collective-permute-start(bf16[3,3,32,256]{3,2,1,0:T(8,128)(2,1)S(1)} %get-tuple-element.28.own_ref), channel_id=1, source_target_pairs={{0,1},{1,0},{2,3},{3,2},{4,5},{5,4},{6,7},{7,6},{8,9},{9,8},{10,11... | collective-permute-start | bytes 442376 | tf_op jit(solution)/shard_map/ppermute | solution.py:412
  179.5 17.4 %collective-permute-start.15 = (bf16[3,3,32,128]{3,2,1,0:T(8,128)(2,1)S(1)}, bf16[3,3,32,128]{3,2,1,0:T(8,128)(2,1)S(1)}, u32[]{:S(2)}, u32[]{:S(2)}) collective-permute-start(bf16[3,3,32,128]{3,2,1,0:T(8,128)(2,1)S(1)} %get-tuple-element.29), channel_id=1, source_target_pairs={{0,3},{1,2},{2,5},{3,4},{4,7},{5,6},{6,9},{7,8},{8,11},{9,10},{10,... | collective-permute-start | bytes 221192 | tf_op jit(solution)/shard_map/ppermute | solution.py:370
  189.0 7.9 %collective-permute-start.13 = (bf16[3,3,32,128]{3,2,1,0:T(8,128)(2,1)S(1)}, bf16[3,3,32,128]{3,2,1,0:T(8,128)(2,1)S(1)}, u32[]{:S(2)}, u32[]{:S(2)}) collective-permute-start(bf16[3,3,32,128]{3,2,1,0:T(8,128)(2,1)S(1)} %get-tuple-element.29), channel_id=1, source_target_pairs={{0,2},{2,4},{4,6},{6,8},{8,10},{10,12},{12,14},{1,3},{3,5},{5,7},{... | collective-permute-start | bytes 221192 | tf_op jit(solution)/shard_map/ppermute | solution.py:360
  191.5 6.6 %collective-permute-start.16 = (bf16[3,3,32,128]{3,2,1,0:T(8,128)(2,1)S(1)}, bf16[3,3,32,128]{3,2,1,0:T(8,128)(2,1)S(1)}, u32[]{:S(2)}, u32[]{:S(2)}) collective-permute-start(bf16[3,3,32,128]{3,2,1,0:T(8,128)(2,1)S(1)} %get-tuple-element.30), channel_id=1, source_target_pairs={{2,1},{3,0},{4,3},{5,2},{6,5},{7,4},{8,7},{9,6},{10,9},{11,8},{12,... | collective-permute-start | bytes 221192 | tf_op jit(solution)/shard_map/ppermute | solution.py:370
  195.0 5.7 %collective-permute-start.14 = (bf16[3,3,32,128]{3,2,1,0:T(8,128)(2,1)S(1)}, bf16[3,3,32,128]{3,2,1,0:T(8,128)(2,1)S(1)}, u32[]{:S(2)}, u32[]{:S(2)}) collective-permute-start(bf16[3,3,32,128]{3,2,1,0:T(8,128)(2,1)S(1)} %get-tuple-element.30), channel_id=1, source_target_pairs={{2,0},{4,2},{6,4},{8,6},{10,8},{12,10},{14,12},{3,1},{5,3},{7,5},{... | collective-permute-start | bytes 221192 | tf_op jit(solution)/shard_map/ppermute | solution.py:361
  200.7 7.4 %collective-permute-start.17 = (bf16[3,6,8,384]{3,2,1,0:T(8,128)(2,1)S(1)}, bf16[3,6,8,384]{3,2,1,0:T(8,128)(2,1)S(1)}, u32[]{:S(2)}, u32[]{:S(2)}) collective-permute-start(bf16[3,6,8,384]{3,2,1,0:T(8,128)(2,1)S(1)} %get-tuple-element.31), channel_id=1, source_target_pairs={{16,0},{32,16},{48,32},{64,48},{80,64},{96,80},{112,96},{128,112},... | collective-permute-start | bytes 331784 | tf_op jit(solution)/shard_map/ppermute | solution.py:361
  204.4 10.3 %collective-permute-start.18 = (bf16[3,6,8,384]{3,2,1,0:T(8,128)(2,1)S(1)}, bf16[3,6,8,384]{3,2,1,0:T(8,128)(2,1)S(1)}, u32[]{:S(2)}, u32[]{:S(2)}) collective-permute-start(bf16[3,6,8,384]{3,2,1,0:T(8,128)(2,1)S(1)} %get-tuple-element.32), channel_id=1, source_target_pairs={{0,16},{16,32},{32,48},{48,64},{64,80},{80,96},{96,112},{112,128},... | collective-permute-start | bytes 331784 | tf_op jit(solution)/shard_map/ppermute | solution.py:360
Sparse Core Ops, SparseCore 0:
  9.5 71.8 all-gather.3
  83.7 32.1 all-gather.5

commit v2 on v1

--- a/solution.py
+++ b/solution.py
@@ -20,6 +20,19 @@
 
 def shaped(shape, dtype):
     return jax.ShapeDtypeStruct(shape, dtype)
+
+
+def after(arrays, settled):
+    count = len(arrays)
+    anywhere = pl.BlockSpec(memory_space=pl.ANY)
+    return pl.pallas_call(
+        lambda *refs: None,
+        out_shape=[shaped(x.shape, x.dtype) for x in arrays],
+        in_specs=[anywhere] * (count + len(settled)),
+        out_specs=[anywhere] * count,
+        input_output_aliases={i: i for i in range(count)},
+        name="after",
+    )(*arrays, *settled)
 
 
 def slices_kernel(_, column_ref, row_ref, out_ref):
@@ -50,7 +63,7 @@
         ),
         compiler_params=room(6),
         name="taper_slices",
-    )(at, column_taper, row_taper)
+    )(at, in_hbm(column_taper), in_hbm(row_taper))
 
 
 def row_part_kernel(tall, slices_ref, out_ref):
@@ -212,43 +225,50 @@
     return jnp.where(row < STEPS, from_next, from_previous)
 
 
-def strips_kernel(own_ref, other_ref, *refs):
-    (left, right, other_left, other_right), (top_ref, bottom_ref) = (refs[:4], refs[4:])
+def widen_kernel(body_ref, left_ref, right_ref, out_ref):
+    variables, levels, rows, wide = body_ref.shape
+    for k in range(variables):
+        for level in range(levels):
+            out_ref[k, level, :, :wide] = body_ref[k, level]
+            sides = beside(left_ref[k, level].astype(F32), right_ref[k, level].astype(F32))
+            out_ref[k, level, :, wide:] = sides.astype(BF)
+
+
+def widened(body, left, right):
+    shape = (*body.shape[:-1], body.shape[-1] + left.shape[-1])
+    return pl.pallas_call(
+        widen_kernel,
+        out_shape=shaped(shape, BF),
+        compiler_params=room(4),
+        name="widened",
+    )(body, left, right)
+
+
+def strips_kernel(own_ref, other_ref, top_ref, bottom_ref):
     variables, levels, rows, wide = own_ref.shape
     for rows_at, out_ref in ((slice(0, 8), top_ref), (slice(rows - 8, rows), bottom_ref)):
         for k in range(variables):
             for level in range(levels):
-                for base, body, l_ref, r_ref in (
-                    (0, own_ref, left, right),
-                    (levels, other_ref, other_left, other_right),
-                ):
-                    out_ref[k, base + level, :, :wide] = body[k, level, rows_at]
-                    sides = beside(
-                        l_ref[k, level, rows_at].astype(F32), r_ref[k, level, rows_at].astype(F32)
-                    )
-                    out_ref[k, base + level, :, wide:] = sides.astype(BF)
-
-
-def row_strips(own, other, *sides):
+                out_ref[k, level] = own_ref[k, level, rows_at]
+                out_ref[k, levels + level] = other_ref[k, level, rows_at]
+
+
+def row_strips(own, other):
     variables, levels, rows, wide = own.shape
-    shape = (variables, 2 * levels, 8, wide + sides[0].shape[-1])
     return pl.pallas_call(
         strips_kernel,
-        out_shape=[shaped(shape, BF)] * 2,
+        out_shape=[shaped((variables, 2 * levels, 8, wide), BF)] * 2,
         compiler_params=room(4),
         name="row_strips",
-    )(own, other, *sides)
+    )(own, other)
 
 
 def advect_kernel(*refs):
     (
         flip_ref,
         own_ref,
+        wider_ref,
         other_ref,
-        left_ref,
-        right_ref,
-        other_left_ref,
-        other_right_ref,
         next_ref,
         previous_ref,
         courant_ref,
@@ -274,15 +294,11 @@
         at = local(level % levels)
         mine = level < levels
         for k in range(variables):
-            body, l_ref, r_ref = (
-                (own_ref, left_ref, right_ref)
-                if mine
-                else (other_ref, other_left_ref, other_right_ref)
-            )
-            first_ref[k, level, :rows, :wide] = body[k, at].astype(F32)
-            first_ref[k, level, :rows, wide:] = beside(
-                l_ref[k, at].astype(F32), r_ref[k, at].astype(F32)
-            )
+            if mine:
+                first_ref[k, level, :rows, :wide] = own_ref[k, at]
+                first_ref[k, level, :rows, wide:] = wider_ref[k, at, :, wide:].astype(F32)
+            else:
+                first_ref[k, level, :rows, :] = other_ref[k, at].astype(F32)
             strip = at if mine else at + levels
             first_ref[k, level, rows:, :] = above_below(
                 next_ref[k, strip].astype(F32), previous_ref[k, strip].astype(F32)
@@ -333,7 +349,7 @@
 
 def advect(flip, *arrays):
     variables, levels, rows, wide = arrays[0].shape
-    tall, full = (rows + 8, wide + arrays[2].shape[-1])
+    tall, full = (rows + 8, arrays[2].shape[-1])
     vmem = pl.BlockSpec(memory_space=pltpu.VMEM)
     state = pltpu.VMEM((variables, 2 * levels, tall, full), F32)
     return pl.pallas_call(
@@ -362,14 +378,6 @@
     return from_left, from_right
 
 
-def across(first, last):
-    size = lax.axis_size("mem")
-    up = [(2 * i + k, 2 * (i + 1) + 1 - k) for i in range(size - 1) for k in range(2)]
-    down = [(2 * (i + 1) + k, 2 * i + 1 - k) for i in range(size - 1) for k in range(2)]
-    axes = ("mem", "lev")
-    return lax.ppermute(last, axes, up), lax.ppermute(first, axes, down)
-
-
 def background(courant_numbers, tracer_slope):
     whole = jnp.concatenate([courant_numbers, tracer_slope], axis=0).astype(BF)
     half = whole.shape[-1] // 2
@@ -377,8 +385,7 @@
     wider = jnp.concatenate([whole, sides], axis=-1)
     from_previous, from_next = neighbours(wider[:, :, :8], wider[:, :, -8:], "row")
     around = above_below(from_next, from_previous)
-    taller = jnp.concatenate([wider, around], axis=2)
-    return sides, around, lax.ppermute(taller, "lev", swap("lev"))
+    return sides, around, jnp.concatenate([wider, around], axis=2)
 
 
 def on_device(
@@ -396,32 +403,43 @@
     slices = lax.all_to_all(
         taper_slices(at, column_taper, row_taper, peers, parts), "row", 0, 0, tiled=True
     )
-    sides, around, opposite = background(courant_numbers, tracer_slope)
+    sides, around, taller = background(courant_numbers, tracer_slope)
     pieces = split_columns(at, perturbations, parts)
-    weights = [pieces[0]]
-    for step in range(1, parts):
-        weights.append(lax.ppermute(pieces[step], "mem", [(i, i ^ step) for i in range(parts)]))
-    first_pass = columns_pass(every, slices, tall, levels, rows, 4)
-    row_whole = lax.all_gather(row_part(slices, tall, weights[1:]), "mem", axis=0, tiled=False)
+    weights = dict(enumerate(pieces))
+
+    def exchange(steps):
+        for step in steps:
+            pairs = [(i, i ^ step) for i in range(parts)]
+            weights[step] = lax.ppermute(weights[step], "mem", pairs)
+        return [weights[step] for step in steps]
+
+    def hold(steps, settled):
+        for step, piece in zip(steps, after([weights[step] for step in steps], settled)):
+            weights[step] = piece
+
+    settled = [*exchange((1,)), taller]
+    first_pass = columns_pass(every, slices, tall, levels, rows, 2)
+    row_whole = lax.all_gather(row_part(slices, tall, settled), "mem", axis=0, tiled=False)
     row_whole = row_whole.reshape(parts, row_taper.shape[1], -1)
+    hold((2, 3, 6, 7), [first_pass])
     arrived = lax.all_to_all(first_pass, "row", 0, 0, tiled=True)
-    tapered = rows_pass(row_whole, arrived, 4, [opposite])
+    tapered = rows_pass(row_whole, arrived, 4, exchange((2, 3, 6, 7)))
+    hold((4, 5), [tapered])
+    (taller,) = after([taller], [tapered])
     localized = lax.all_to_all(tapered, "row", 0, 0, tiled=True)
+    exchange((4, 5))
+    opposite = lax.ppermute(taller, "lev", swap("lev"))
+    weights = [weights[step] for step in range(parts)]
     own, rounded, first, last = weighted_sum(at, localized, weights)
 
-    other = lax.ppermute(rounded, "lev", swap("lev"))
-    left, right = neighbours(first, last, "mem")
-    other_left, other_right = across(first, last)
-    top, bottom = row_strips(rounded, other, left, right, other_left, other_right)
-    from_previous, from_next = neighbours(top, bottom, "row")
+    wider = widened(rounded, *neighbours(first, last, "mem"))
+    other = lax.ppermute(wider, "lev", swap("lev"))
+    from_previous, from_next = neighbours(*row_strips(wider, other), "row")
     return advect(
         flip,
         own,
+        wider,
         other,
-        left,
-        right,
-        other_left,
-        other_right,
         from_next,
         from_previous,
         courant_numbers,

time: 226 us -> 197 us (0.87)
  the two profiles are of different devices: /device:TPU:137 before, /device:TPU:74 now
where the time goes in v2:
time: 197 us; the launch traced here: 196 us
  starting transfers between devices  93.7 us (48%)
  waiting for transfers between devices  65.1 us (33%)
  Pallas kernels  17 us (9%)
  between operations  13.8 us (7%)
  local copies, waits for them, and re-layouts  6.03 us (3%)
    ppermute x7, starting transfers between devices, exchange(): weights[step] = lax.ppermute(weights[step], 'mem', pairs)  19.3 us
    ppermute x4, waiting for transfers between devices, neighbours(): from_left = lax.ppermute(last, axis, chain(axis, 1))  17.7 us
    ppermute x4, starting transfers between devices, neighbours(): from_right = lax.ppermute(first, axis, chain(axis, -1))  15.9 us
    all_to_all x1, starting transfers between devices, on_device(): lax.all_to_all(taper_slices(at, column_taper, row_taper, peers, parts), '...  14.5 us
    all_gather x1, waiting for transfers between devices, on_device(): lax.all_gather(row_part(slices, tall, settled), 'mem', axis=0, tiled=False)  12.3 us
    all_to_all x1, starting transfers between devices, on_device(): localized = lax.all_to_all(tapered, 'row', 0, 0, tiled=True)  11.9 us
    all_to_all x1, starting transfers between devices, on_device(): arrived = lax.all_to_all(first_pass, 'row', 0, 0, tiled=True)  11.9 us
    ppermute x7, waiting for transfers between devices, exchange(): weights[step] = lax.ppermute(weights[step], 'mem', pairs)  11.5 us
  transfers between devices with their start and end apart: 22, of which 14 were waited for; matrix products, arithmetic and copies ran while one was open for 0% of the time, Pallas kernels for 5%

profile of v2, /device:TPU:74, one launch (start us, length us, event | category | flops | bytes accessed | tf_op | source)
XLA Modules:
  0.0 195.8 jit_solution(890901942956908355)
XLA Ops:
  7.3 2.0 %taper_slices.1 = bf16[32,80,256]{2,1,0:T(8,128)(2,1)} custom-call(s32[1]{0:T(128)} %bitcast.1._.at_ref.refs_0_, bf16[64,2048]{1,0:T(8,128)(2,1)} %column_ref.1, bf16[32,1024]{1,0:T(8,128)(2,1)} %row_ref.1), custom_call_target="tpu_custom_call" | custom-call | tf_op jit(solution)/shard_map/taper_slices/pallas_call | solution.py:52
  9.3 14.5 %all-to-all-start = ((bf16[32,80,256]{2,1,0:T(8,128)(2,1)}), bf16[32,80,256]{2,1,0:T(8,128)(2,1)S(1)}, u32[]{:S(2)}, u32[]{:S(2)}) async-start(bf16[32,80,256]{2,1,0:T(8,128)(2,1)} %taper_slices.1), calls=%async_computation | async-start | bytes 2621440 | tf_op jit(solution)/shard_map/all_to_all | solution.py:403
  23.9 1.9 collective-permute-start.2
  25.9 3.6 %collective-permute-start.1 = (bf16[5,3,32,128]{3,2,1,0:T(8,128)(2,1)S(1)}, bf16[5,3,32,128]{3,2,1,0:T(8,128)(2,1)S(1)}, u32[]{:S(2)}, u32[]{:S(2)}) collective-permute-start(bf16[5,3,32,128]{3,2,1,0:T(8,128)(2,1)S(1)} %get-tuple-element.48), channel_id=1, source_target_pairs={{2,0},{4,2},{6,4},{8,6},{10,8},{12,10},{14,12},{3,1},{5,3},{7,5},{... | collective-permute-start | bytes 368648 | tf_op jit(solution)/shard_map/ppermute | solution.py:377
  33.9 2.0 %collective-permute-start = (bf16[3,2,3,32,256]{4,3,2,1,0:T(8,128)(2,1)S(1)}, bf16[3,2,3,32,256]{4,3,2,1,0:T(8,128)(2,1)S(1)}, u32[]{:S(2)}, u32[]{:S(2)}) collective-permute-start(bf16[3,2,3,32,256]{4,3,2,1,0:T(8,128)(2,1)S(1)} %get-tuple-element.25), channel_id=1, source_target_pairs={{0,2},{2,0},{4,6},{6,4},{8,10},{10,8},{12,14},{14,12},{1,3},{3,1},... | collective-permute-start | bytes 884744 | tf_op jit(solution)/shard_map/ppermute | solution.py:413
  36.0 4.3 %collective-permute-start.4 = (bf16[5,3,8,384]{3,2,1,0:T(8,128)(2,1)S(1)}, bf16[5,3,8,384]{3,2,1,0:T(8,128)(2,1)S(1)}, u32[]{:S(2)}, u32[]{:S(2)}) collective-permute-start(bf16[5,3,8,384]{3,2,1,0:T(8,128)(2,1)S(1)} %get-tuple-element.45), channel_id=1, source_target_pairs={{0,16},{16,32},{32,48},{48,64},{64,80},{80,96},{96,112},{112,128},... | collective-permute-start | bytes 276488 | tf_op jit(solution)/shard_map/ppermute | solution.py:376
  40.3 4.6 %collective-permute-start.3 = (bf16[5,3,8,384]{3,2,1,0:T(8,128)(2,1)S(1)}, bf16[5,3,8,384]{3,2,1,0:T(8,128)(2,1)S(1)}, u32[]{:S(2)}, u32[]{:S(2)}) collective-permute-start(bf16[5,3,8,384]{3,2,1,0:T(8,128)(2,1)S(1)} %get-tuple-element.46), channel_id=1, source_target_pairs={{16,0},{32,16},{48,32},{64,48},{80,64},{96,80},{112,96},{128,112},... | collective-permute-start | bytes 276488 | tf_op jit(solution)/shard_map/ppermute | solution.py:377
  44.9 9.7 %collective-permute-done.4 = bf16[5,3,8,384]{3,2,1,0:T(8,128)(2,1)S(1)} collective-permute-done((bf16[5,3,8,384]{3,2,1,0:T(8,128)(2,1)S(1)}, bf16[5,3,8,384]{3,2,1,0:T(8,128)(2,1)S(1)}, u32[]{:S(2)}, u32[]{:S(2)}) %collective-permute-start.4) | collective-permute-done | bytes 92192 | tf_op jit(solution)/shard_map/ppermute | solution.py:376
  57.4 2.6 %all-gather.4.cloned.1.call-done.a = bf16[1536,2048]{1,0:T(8,128)(2,1)} async-done(((bf16[192,2048]{1,0:T(8,128)(2,1)}), bf16[1536,2048]{1,0:T(8,128)(2,1)}) %all-gather.4.cloned.1.call-update) | async-done | bytes 6291472 | tf_op jit(solution)/shard_map/all_gather | solution.py:400
  60.0 4.6 %columns_pass.1.refs_4_ = bf16[32,3,32,128]{3,2,1,0:T(8,128)(2,1)} custom-call(bf16[1536,2048]{1,0:T(8,128)(2,1)} %all-gather.4.cloned.1.call-done.a, bf16[32,80,256]{2,1,0:T(8,128)(2,1)S(1)} %all-to-all-done.a.b), custom_call_target="tpu_custom_call" | custom-call | tf_op jit(solution)/shard_map/columns_pass/pallas_call | solution.py:105
  64.6 11.9 %all-to-all-start.1 = ((bf16[32,3,32,128]{3,2,1,0:T(8,128)(2,1)}), bf16[32,3,32,128]{3,2,1,0:T(8,128)(2,1)S(1)}, u32[]{:S(2)}, u32[]{:S(2)}) async-start(bf16[32,3,32,128]{3,2,1,0:T(8,128)(2,1)} %columns_pass.1.refs_4_), calls=%async_computation.1 | async-start | bytes 1572864 | tf_op jit(solution)/shard_map/all_to_all | solution.py:425
  76.5 2.5 %collective-permute-start.5 = (bf16[3,2,3,32,256]{4,3,2,1,0:T(8,128)(2,1)}, bf16[3,2,3,32,256]{4,3,2,1,0:T(8,128)(2,1)S(1)}, u32[]{:S(2)}, u32[]{:S(2)}) collective-permute-start(bf16[3,2,3,32,256]{4,3,2,1,0:T(8,128)(2,1)} %get-tuple-element.30), channel_id=1, source_target_pairs={{0,4},{2,6},{4,0},{6,2},{8,12},{10,14},{12,8},{14,10},{1,5},{3,7},... | collective-permute-start | bytes 884744 | tf_op jit(solution)/shard_map/ppermute | solution.py:413
  79.0 2.4 %collective-permute-start.6 = (bf16[3,2,3,32,256]{4,3,2,1,0:T(8,128)(2,1)}, bf16[3,2,3,32,256]{4,3,2,1,0:T(8,128)(2,1)S(1)}, u32[]{:S(2)}, u32[]{:S(2)}) collective-permute-start(bf16[3,2,3,32,256]{4,3,2,1,0:T(8,128)(2,1)} %get-tuple-element.31), channel_id=1, source_target_pairs={{0,6},{2,4},{4,2},{6,0},{8,14},{10,12},{12,10},{14,8},{1,7},{3,5},... | collective-permute-start | bytes 884744 | tf_op jit(solution)/shard_map/ppermute | solution.py:413
  81.4 3.1 %collective-permute-start.7 = (bf16[3,2,3,32,256]{4,3,2,1,0:T(8,128)(2,1)}, bf16[3,2,3,32,256]{4,3,2,1,0:T(8,128)(2,1)S(1)}, u32[]{:S(2)}, u32[]{:S(2)}) collective-permute-start(bf16[3,2,3,32,256]{4,3,2,1,0:T(8,128)(2,1)} %get-tuple-element.32), channel_id=1, source_target_pairs={{0,12},{2,14},{4,8},{6,10},{8,4},{10,6},{12,0},{14,2},{1,13},{3,15... | collective-permute-start | bytes 884744 | tf_op jit(solution)/shard_map/ppermute | solution.py:413
  84.5 3.2 %collective-permute-start.8 = (bf16[3,2,3,32,256]{4,3,2,1,0:T(8,128)(2,1)}, bf16[3,2,3,32,256]{4,3,2,1,0:T(8,128)(2,1)S(1)}, u32[]{:S(2)}, u32[]{:S(2)}) collective-permute-start(bf16[3,2,3,32,256]{4,3,2,1,0:T(8,128)(2,1)} %get-tuple-element.33), channel_id=1, source_target_pairs={{0,14},{2,12},{4,10},{6,8},{8,6},{10,4},{12,2},{14,0},{1,15},{3,13... | collective-permute-start | bytes 884744 | tf_op jit(solution)/shard_map/ppermute | solution.py:413
  87.7 12.3 %all-gather.6.cloned.1.call-done = bf16[256,32,128]{2,1,0:T(8,128)(2,1)} async-done(((bf16[32,32,128]{2,1,0:T(8,128)(2,1)}), bf16[256,32,128]{2,1,0:T(8,128)(2,1)}) %all-gather.6.cloned.1.call-update) | async-done | bytes 2097168 | tf_op jit(solution)/shard_map/all_gather | solution.py:422
  101.3 3.7 %collective-permute-done.8.refs_3_.refs_9_ = bf16[3,2,3,32,256]{4,3,2,1,0:T(8,128)(2,1)S(1)} collective-permute-done((bf16[3,2,3,32,256]{4,3,2,1,0:T(8,128)(2,1)}, bf16[3,2,3,32,256]{4,3,2,1,0:T(8,128)(2,1)S(1)}, u32[]{:S(2)}, u32[]{:S(2)}) %collective-permute-start.8) | collective-permute-done | bytes 294944 | tf_op jit(solution)/shard_map/ppermute | solution.py:413
  105.0 4.5 %rows_pass.1.refs_2_.refs_1_ = bf16[32,3,32,128]{3,2,1,0:T(8,128)(2,1)} custom-call(bf16[8,1024,128]{2,1,0:T(8,128)(2,1)} %bitcast.4, bf16[32,3,32,128]{3,2,1,0:T(8,128)(2,1)S(1)} %all-to-all-done.1.fields_ref, bf16[3,2,3,32,256]{4,3,2,1,0:T(8,128)(2,1)S(1)} %collective-permute-done.5.refs_0_.refs_4_, ...), custom_call_target="tpu_custom_call" | custom-call | tf_op jit(solution)/shard_map/rows_pass/pallas_call | solution.py:139
  109.5 11.9 %all-to-all-start.2 = ((bf16[32,3,32,128]{3,2,1,0:T(8,128)(2,1)}), bf16[32,3,32,128]{3,2,1,0:T(8,128)(2,1)S(1)}, u32[]{:S(2)}, u32[]{:S(2)}) async-start(bf16[32,3,32,128]{3,2,1,0:T(8,128)(2,1)} %rows_pass.1.refs_2_.refs_1_), calls=%async_computation.2 | async-start | bytes 1572864 | tf_op jit(solution)/shard_map/all_to_all | solution.py:429
  121.5 3.7 %collective-permute-start.9 = (bf16[3,2,3,32,256]{4,3,2,1,0:T(8,128)(2,1)}, bf16[3,2,3,32,256]{4,3,2,1,0:T(8,128)(2,1)}, u32[]{:S(2)}, u32[]{:S(2)}) collective-permute-start(bf16[3,2,3,32,256]{4,3,2,1,0:T(8,128)(2,1)} %get-tuple-element.37), channel_id=1, source_target_pairs={{0,8},{2,10},{4,12},{6,14},{8,0},{10,2},{12,4},{14,6},{1,9},{3,11}... | collective-permute-start | bytes 884744 | tf_op jit(solution)/shard_map/ppermute | solution.py:413
  125.2 2.5 %collective-permute-start.10 = (bf16[3,2,3,32,256]{4,3,2,1,0:T(8,128)(2,1)}, bf16[3,2,3,32,256]{4,3,2,1,0:T(8,128)(2,1)}, u32[]{:S(2)}, u32[]{:S(2)}) collective-permute-start(bf16[3,2,3,32,256]{4,3,2,1,0:T(8,128)(2,1)} %get-tuple-element.38), channel_id=1, source_target_pairs={{0,10},{2,8},{4,14},{6,12},{8,2},{10,0},{12,6},{14,4},{1,11},{3,9}... | collective-permute-start | bytes 884744 | tf_op jit(solution)/shard_map/ppermute | solution.py:413
  127.7 4.2 %collective-permute-start.16 = (bf16[5,3,40,384]{3,2,1,0:T(8,128)(2,1)}, bf16[5,3,40,384]{3,2,1,0:T(8,128)(2,1)S(1)}, u32[]{:S(2)}, u32[]{:S(2)}) collective-permute-start(bf16[5,3,40,384]{3,2,1,0:T(8,128)(2,1)} %after.5), channel_id=1, source_target_pairs={{0,1},{1,0},{2,3},{3,2},{4,5},{5,4},{6,7},{7,6},{8,9},{9,8},{10,11... | collective-permute-start | bytes 1382408 | tf_op jit(solution)/shard_map/ppermute | solution.py:431
  131.9 3.2 %collective-permute-done.9.refs_6_ = bf16[3,2,3,32,256]{4,3,2,1,0:T(8,128)(2,1)} collective-permute-done((bf16[3,2,3,32,256]{4,3,2,1,0:T(8,128)(2,1)}, bf16[3,2,3,32,256]{4,3,2,1,0:T(8,128)(2,1)}, u32[]{:S(2)}, u32[]{:S(2)}) %collective-permute-start.9) | collective-permute-done | bytes 294944 | tf_op jit(solution)/shard_map/ppermute | solution.py:413
  135.1 3.3 %collective-permute-done.10.refs_7_ = bf16[3,2,3,32,256]{4,3,2,1,0:T(8,128)(2,1)} collective-permute-done((bf16[3,2,3,32,256]{4,3,2,1,0:T(8,128)(2,1)}, bf16[3,2,3,32,256]{4,3,2,1,0:T(8,128)(2,1)}, u32[]{:S(2)}, u32[]{:S(2)}) %collective-permute-start.10) | collective-permute-done | bytes 294944 | tf_op jit(solution)/shard_map/ppermute | solution.py:413
  138.4 9.3 %all-to-all-done.2.refs_1_ = bf16[32,3,32,128]{3,2,1,0:T(8,128)(2,1)S(1)} async-done(((bf16[32,3,32,128]{3,2,1,0:T(8,128)(2,1)}), bf16[32,3,32,128]{3,2,1,0:T(8,128)(2,1)S(1)}, u32[]{:S(2)}, u32[]{:S(2)}) %all-to-all-start.2) | async-done | bytes 786464 | tf_op jit(solution)/shard_map/all_to_all | solution.py:429
  152.3 3.6 %collective-permute-start.12 = (bf16[3,3,32,128]{3,2,1,0:T(8,128)(2,1)S(1)}, bf16[3,3,32,128]{3,2,1,0:T(8,128)(2,1)S(1)}, u32[]{:S(2)}, u32[]{:S(2)}) collective-permute-start(bf16[3,3,32,128]{3,2,1,0:T(8,128)(2,1)S(1)} %get-tuple-element.42), channel_id=1, source_target_pairs={{2,0},{4,2},{6,4},{8,6},{10,8},{12,10},{14,12},{3,1},{5,3},{7,5},{... | collective-permute-start | bytes 221192 | tf_op jit(solution)/shard_map/ppermute | solution.py:377
  157.9 5.0 %collective-permute-start.13 = (bf16[3,3,32,384]{3,2,1,0:T(8,128)(2,1)S(1)}, bf16[3,3,32,384]{3,2,1,0:T(8,128)(2,1)S(1)}, u32[]{:S(2)}, u32[]{:S(2)}) collective-permute-start(bf16[3,3,32,384]{3,2,1,0:T(8,128)(2,1)S(1)} %widened.1.own_ref.refs_2_), channel_id=1, source_target_pairs={{0,1},{1,0},{2,3},{3,2},{4,5},{5,4},{6,7},{7,6},{8,9},{9,8},{10,11... | collective-permute-start | bytes 663560 | tf_op jit(solution)/shard_map/ppermute | solution.py:436
  162.9 5.8 %collective-permute-done.13.other_ref.refs_3_ = bf16[3,3,32,384]{3,2,1,0:T(8,128)(2,1)S(1)} collective-permute-done((bf16[3,3,32,384]{3,2,1,0:T(8,128)(2,1)S(1)}, bf16[3,3,32,384]{3,2,1,0:T(8,128)(2,1)S(1)}, u32[]{:S(2)}, u32[]{:S(2)}) %collective-permute-start.13) | collective-permute-done | bytes 221216 | tf_op jit(solution)/shard_map/ppermute | solution.py:436
  168.8 4.1 %collective-permute-start.14 = (bf16[3,6,8,384]{3,2,1,0:T(8,128)(2,1)S(1)}, bf16[3,6,8,384]{3,2,1,0:T(8,128)(2,1)S(1)}, u32[]{:S(2)}, u32[]{:S(2)}) collective-permute-start(bf16[3,6,8,384]{3,2,1,0:T(8,128)(2,1)S(1)} %get-tuple-element.43), channel_id=1, source_target_pairs={{16,0},{32,16},{48,32},{64,48},{80,64},{96,80},{112,96},{128,112},... | collective-permute-start | bytes 331784 | tf_op jit(solution)/shard_map/ppermute | solution.py:377
  172.9 2.7 %collective-permute-start.15 = (bf16[3,6,8,384]{3,2,1,0:T(8,128)(2,1)S(1)}, bf16[3,6,8,384]{3,2,1,0:T(8,128)(2,1)S(1)}, u32[]{:S(2)}, u32[]{:S(2)}) collective-permute-start(bf16[3,6,8,384]{3,2,1,0:T(8,128)(2,1)S(1)} %get-tuple-element.44), channel_id=1, source_target_pairs={{0,16},{16,32},{32,48},{48,64},{64,80},{80,96},{96,112},{112,128},... | collective-permute-start | bytes 331784 | tf_op jit(solution)/shard_map/ppermute | solution.py:376
  176.9 7.9 %collective-permute-done.15.refs_5_ = bf16[3,6,8,384]{3,2,1,0:T(8,128)(2,1)S(1)} collective-permute-done((bf16[3,6,8,384]{3,2,1,0:T(8,128)(2,1)S(1)}, bf16[3,6,8,384]{3,2,1,0:T(8,128)(2,1)S(1)}, u32[]{:S(2)}, u32[]{:S(2)}) %collective-permute-start.15) | collective-permute-done | bytes 110624 | tf_op jit(solution)/shard_map/ppermute | solution.py:376
  185.8 3.1 %advect.1 = f32[3,3,32,256]{3,2,1,0:T(8,128)} custom-call(s32[1]{0:T(128)} %bitcast.refs_0_, f32[3,3,32,256]{3,2,1,0:T(8,128)S(1)} %copy-done.13, bf16[3,3,32,384]{3,2,1,0:T(8,128)(2,1)S(1)} %widened.1.own_ref.refs_2_, bf16[3,3,32,384]{3,2,1,0:T(8,128)(2,1)S(1)} %collective-permute-done.13.other_ref.refs_3_, ...), custom_call_target="tpu_custom_call" | custom-call | tf_op jit(solution)/shard_map/advect/pallas_call | solution.py:355
  (63 shorter events, 18.2 us)
Async XLA Ops:
  6.5 53.5 %all-gather.4.cloned.1.call-start = ((), (), s32[]{:S(2)}) async-start(), calls=%async_computation.3 | async-start | bytes 7077888 | tf_op jit(solution)/shard_map/all_gather | solution.py:400
  7.3 16.6 %copy-start.3 = (f32[2,3,32,256]{3,2,1,0:T(8,128)S(1)}, f32[2,3,32,256]{3,2,1,0:T(8,128)}, u32[]{:S(2)}) copy-start(f32[2,3,32,256]{3,2,1,0:T(8,128)} %refs_7_.1) | copy-start | bytes 589828
  7.3 16.6 %copy-start.2 = (f32[3,3,32,256]{3,2,1,0:T(8,128)S(1)}, f32[3,3,32,256]{3,2,1,0:T(8,128)}, u32[]{:S(2)}) copy-start(f32[3,3,32,256]{3,2,1,0:T(8,128)} %refs_6_.1) | copy-start | bytes 884740
  9.3 47.4 %all-to-all-start = ((bf16[32,80,256]{2,1,0:T(8,128)(2,1)}), bf16[32,80,256]{2,1,0:T(8,128)(2,1)S(1)}, u32[]{:S(2)}, u32[]{:S(2)}) async-start(bf16[32,80,256]{2,1,0:T(8,128)(2,1)} %taper_slices.1), calls=%async_computation | async-start | bytes 2621440 | tf_op jit(solution)/shard_map/all_to_all | solution.py:403
  23.8 76.3 %all-gather.6.cloned.1.call-start = ((), (), s32[]{:S(2)}) async-start(), calls=%async_computation.4 | async-start | bytes 2359296 | tf_op jit(solution)/shard_map/all_gather | solution.py:422
  23.9 12.0 %collective-permute-start.2 = (bf16[5,3,32,128]{3,2,1,0:T(8,128)(2,1)S(1)}, bf16[5,3,32,128]{3,2,1,0:T(8,128)(2,1)S(1)}, u32[]{:S(2)}, u32[]{:S(2)}) collective-permute-start(bf16[5,3,32,128]{3,2,1,0:T(8,128)(2,1)S(1)} %get-tuple-element.47), channel_id=1, source_target_pairs={{0,2},{2,4},{4,6},{6,8},{8,10},{10,12},{12,14},{1,3},{3,5},{5,7},{... | collective-permute-start | bytes 368648 | tf_op jit(solution)/shard_map/ppermute | solution.py:376
  25.9 10.1 %collective-permute-start.1 = (bf16[5,3,32,128]{3,2,1,0:T(8,128)(2,1)S(1)}, bf16[5,3,32,128]{3,2,1,0:T(8,128)(2,1)S(1)}, u32[]{:S(2)}, u32[]{:S(2)}) collective-permute-start(bf16[5,3,32,128]{3,2,1,0:T(8,128)(2,1)S(1)} %get-tuple-element.48), channel_id=1, source_target_pairs={{2,0},{4,2},{6,4},{8,6},{10,8},{12,10},{14,12},{3,1},{5,3},{7,5},{... | collective-permute-start | bytes 368648 | tf_op jit(solution)/shard_map/ppermute | solution.py:377
  29.5 1.9 copy-start.1
  33.9 20.6 %copy-start.6 = (bf16[3,2,3,32,256]{4,3,2,1,0:T(8,128)(2,1)}, bf16[3,2,3,32,256]{4,3,2,1,0:T(8,128)(2,1)S(1)}, u32[]{:S(2)}) copy-start(bf16[3,2,3,32,256]{4,3,2,1,0:T(8,128)(2,1)S(1)} %get-tuple-element.35.refs_0_) | copy-start | bytes 884740
  33.9 20.6 %copy-start.7 = (bf16[3,2,3,32,256]{4,3,2,1,0:T(8,128)(2,1)}, bf16[3,2,3,32,256]{4,3,2,1,0:T(8,128)(2,1)S(1)}, u32[]{:S(2)}) copy-start(bf16[3,2,3,32,256]{4,3,2,1,0:T(8,128)(2,1)S(1)} %get-tuple-element.36.refs_1_) | copy-start | bytes 884740
  33.9 20.6 %copy-start.8 = (bf16[3,2,3,32,256]{4,3,2,1,0:T(8,128)(2,1)}, bf16[3,2,3,32,256]{4,3,2,1,0:T(8,128)(2,1)S(1)}, u32[]{:S(2)}) copy-start(bf16[3,2,3,32,256]{4,3,2,1,0:T(8,128)(2,1)S(1)} %get-tuple-element.26.refs_0_) | copy-start | bytes 884740
  33.9 20.8 %copy-start.11 = (bf16[3,2,3,32,256]{4,3,2,1,0:T(8,128)(2,1)}, bf16[3,2,3,32,256]{4,3,2,1,0:T(8,128)(2,1)S(1)}, u32[]{:S(2)}) copy-start(bf16[3,2,3,32,256]{4,3,2,1,0:T(8,128)(2,1)S(1)} %get-tuple-element.29.refs_3_) | copy-start | bytes 884740
  33.9 20.8 %collective-permute-start = (bf16[3,2,3,32,256]{4,3,2,1,0:T(8,128)(2,1)S(1)}, bf16[3,2,3,32,256]{4,3,2,1,0:T(8,128)(2,1)S(1)}, u32[]{:S(2)}, u32[]{:S(2)}) collective-permute-start(bf16[3,2,3,32,256]{4,3,2,1,0:T(8,128)(2,1)S(1)} %get-tuple-element.25), channel_id=1, source_target_pairs={{0,2},{2,0},{4,6},{6,4},{8,10},{10,8},{12,14},{14,12},{1,3},{3,1},... | collective-permute-start | bytes 884744 | tf_op jit(solution)/shard_map/ppermute | solution.py:413
  36.0 18.5 %collective-permute-start.4 = (bf16[5,3,8,384]{3,2,1,0:T(8,128)(2,1)S(1)}, bf16[5,3,8,384]{3,2,1,0:T(8,128)(2,1)S(1)}, u32[]{:S(2)}, u32[]{:S(2)}) collective-permute-start(bf16[5,3,8,384]{3,2,1,0:T(8,128)(2,1)S(1)} %get-tuple-element.45), channel_id=1, source_target_pairs={{0,16},{16,32},{32,48},{48,64},{64,80},{80,96},{96,112},{112,128},... | collective-permute-start | bytes 276488 | tf_op jit(solution)/shard_map/ppermute | solution.py:376
  40.3 14.3 %collective-permute-start.3 = (bf16[5,3,8,384]{3,2,1,0:T(8,128)(2,1)S(1)}, bf16[5,3,8,384]{3,2,1,0:T(8,128)(2,1)S(1)}, u32[]{:S(2)}, u32[]{:S(2)}) collective-permute-start(bf16[5,3,8,384]{3,2,1,0:T(8,128)(2,1)S(1)} %get-tuple-element.46), channel_id=1, source_target_pairs={{16,0},{32,16},{48,32},{64,48},{80,64},{96,80},{112,96},{128,112},... | collective-permute-start | bytes 276488 | tf_op jit(solution)/shard_map/ppermute | solution.py:377
  54.7 9.9 %copy-start = (bf16[5,3,40,384]{3,2,1,0:T(8,128)(2,1)}, bf16[5,3,40,384]{3,2,1,0:T(8,128)(2,1)S(1)}, u32[]{:S(2)}) copy-start(bf16[5,3,40,384]{3,2,1,0:T(8,128)(2,1)S(1)} %pad_maximum_fusion.rest_1_.refs_0_) | copy-start | bytes 1382404
  64.6 40.4 %all-to-all-start.1 = ((bf16[32,3,32,128]{3,2,1,0:T(8,128)(2,1)}), bf16[32,3,32,128]{3,2,1,0:T(8,128)(2,1)S(1)}, u32[]{:S(2)}, u32[]{:S(2)}) async-start(bf16[32,3,32,128]{3,2,1,0:T(8,128)(2,1)} %columns_pass.1.refs_4_), calls=%async_computation.1 | async-start | bytes 1572864 | tf_op jit(solution)/shard_map/all_to_all | solution.py:425
  76.5 23.5 %collective-permute-start.5 = (bf16[3,2,3,32,256]{4,3,2,1,0:T(8,128)(2,1)}, bf16[3,2,3,32,256]{4,3,2,1,0:T(8,128)(2,1)S(1)}, u32[]{:S(2)}, u32[]{:S(2)}) collective-permute-start(bf16[3,2,3,32,256]{4,3,2,1,0:T(8,128)(2,1)} %get-tuple-element.30), channel_id=1, source_target_pairs={{0,4},{2,6},{4,0},{6,2},{8,12},{10,14},{12,8},{14,10},{1,5},{3,7},... | collective-permute-start | bytes 884744 | tf_op jit(solution)/shard_map/ppermute | solution.py:413
  79.0 22.3 %collective-permute-start.6 = (bf16[3,2,3,32,256]{4,3,2,1,0:T(8,128)(2,1)}, bf16[3,2,3,32,256]{4,3,2,1,0:T(8,128)(2,1)S(1)}, u32[]{:S(2)}, u32[]{:S(2)}) collective-permute-start(bf16[3,2,3,32,256]{4,3,2,1,0:T(8,128)(2,1)} %get-tuple-element.31), channel_id=1, source_target_pairs={{0,6},{2,4},{4,2},{6,0},{8,14},{10,12},{12,10},{14,8},{1,7},{3,5},... | collective-permute-start | bytes 884744 | tf_op jit(solution)/shard_map/ppermute | solution.py:413
  81.4 19.9 %collective-permute-start.7 = (bf16[3,2,3,32,256]{4,3,2,1,0:T(8,128)(2,1)}, bf16[3,2,3,32,256]{4,3,2,1,0:T(8,128)(2,1)S(1)}, u32[]{:S(2)}, u32[]{:S(2)}) collective-permute-start(bf16[3,2,3,32,256]{4,3,2,1,0:T(8,128)(2,1)} %get-tuple-element.32), channel_id=1, source_target_pairs={{0,12},{2,14},{4,8},{6,10},{8,4},{10,6},{12,0},{14,2},{1,13},{3,15... | collective-permute-start | bytes 884744 | tf_op jit(solution)/shard_map/ppermute | solution.py:413
  84.5 20.5 %collective-permute-start.8 = (bf16[3,2,3,32,256]{4,3,2,1,0:T(8,128)(2,1)}, bf16[3,2,3,32,256]{4,3,2,1,0:T(8,128)(2,1)S(1)}, u32[]{:S(2)}, u32[]{:S(2)}) collective-permute-start(bf16[3,2,3,32,256]{4,3,2,1,0:T(8,128)(2,1)} %get-tuple-element.33), channel_id=1, source_target_pairs={{0,14},{2,12},{4,10},{6,8},{8,6},{10,4},{12,2},{14,0},{1,15},{3,13... | collective-permute-start | bytes 884744 | tf_op jit(solution)/shard_map/ppermute | solution.py:413
  109.5 38.3 %all-to-all-start.2 = ((bf16[32,3,32,128]{3,2,1,0:T(8,128)(2,1)}), bf16[32,3,32,128]{3,2,1,0:T(8,128)(2,1)S(1)}, u32[]{:S(2)}, u32[]{:S(2)}) async-start(bf16[32,3,32,128]{3,2,1,0:T(8,128)(2,1)} %rows_pass.1.refs_2_.refs_1_), calls=%async_computation.2 | async-start | bytes 1572864 | tf_op jit(solution)/shard_map/all_to_all | solution.py:429
  121.5 13.7 %collective-permute-start.9 = (bf16[3,2,3,32,256]{4,3,2,1,0:T(8,128)(2,1)}, bf16[3,2,3,32,256]{4,3,2,1,0:T(8,128)(2,1)}, u32[]{:S(2)}, u32[]{:S(2)}) collective-permute-start(bf16[3,2,3,32,256]{4,3,2,1,0:T(8,128)(2,1)} %get-tuple-element.37), channel_id=1, source_target_pairs={{0,8},{2,10},{4,12},{6,14},{8,0},{10,2},{12,4},{14,6},{1,9},{3,11}... | collective-permute-start | bytes 884744 | tf_op jit(solution)/shard_map/ppermute | solution.py:413
  125.2 13.2 %collective-permute-start.10 = (bf16[3,2,3,32,256]{4,3,2,1,0:T(8,128)(2,1)}, bf16[3,2,3,32,256]{4,3,2,1,0:T(8,128)(2,1)}, u32[]{:S(2)}, u32[]{:S(2)}) collective-permute-start(bf16[3,2,3,32,256]{4,3,2,1,0:T(8,128)(2,1)} %get-tuple-element.38), channel_id=1, source_target_pairs={{0,10},{2,8},{4,14},{6,12},{8,2},{10,0},{12,6},{14,4},{1,11},{3,9}... | collective-permute-start | bytes 884744 | tf_op jit(solution)/shard_map/ppermute | solution.py:413
  127.7 47.9 %collective-permute-start.16 = (bf16[5,3,40,384]{3,2,1,0:T(8,128)(2,1)}, bf16[5,3,40,384]{3,2,1,0:T(8,128)(2,1)S(1)}, u32[]{:S(2)}, u32[]{:S(2)}) collective-permute-start(bf16[5,3,40,384]{3,2,1,0:T(8,128)(2,1)} %after.5), channel_id=1, source_target_pairs={{0,1},{1,0},{2,3},{3,2},{4,5},{5,4},{6,7},{7,6},{8,9},{9,8},{10,11... | collective-permute-start | bytes 1382408 | tf_op jit(solution)/shard_map/ppermute | solution.py:431
  147.8 1.0 copy-start.5
  150.3 18.4 %copy-start.12 = (f32[3,3,32,256]{3,2,1,0:T(8,128)}, f32[3,3,32,256]{3,2,1,0:T(8,128)S(1)}, u32[]{:S(2)}) copy-start(f32[3,3,32,256]{3,2,1,0:T(8,128)S(1)} %get-tuple-element.39.refs_1_) | copy-start | bytes 884740
  150.3 5.7 %collective-permute-start.11 = (bf16[3,3,32,128]{3,2,1,0:T(8,128)(2,1)S(1)}, bf16[3,3,32,128]{3,2,1,0:T(8,128)(2,1)S(1)}, u32[]{:S(2)}, u32[]{:S(2)}) collective-permute-start(bf16[3,3,32,128]{3,2,1,0:T(8,128)(2,1)S(1)} %get-tuple-element.41), channel_id=1, source_target_pairs={{0,2},{2,4},{4,6},{6,8},{8,10},{10,12},{12,14},{1,3},{3,5},{5,7},{... | collective-permute-start | bytes 221192 | tf_op jit(solution)/shard_map/ppermute | solution.py:376
  152.3 5.6 %collective-permute-start.12 = (bf16[3,3,32,128]{3,2,1,0:T(8,128)(2,1)S(1)}, bf16[3,3,32,128]{3,2,1,0:T(8,128)(2,1)S(1)}, u32[]{:S(2)}, u32[]{:S(2)}) collective-permute-start(bf16[3,3,32,128]{3,2,1,0:T(8,128)(2,1)S(1)} %get-tuple-element.42), channel_id=1, source_target_pairs={{2,0},{4,2},{6,4},{8,6},{10,8},{12,10},{14,12},{3,1},{5,3},{7,5},{... | collective-permute-start | bytes 221192 | tf_op jit(solution)/shard_map/ppermute | solution.py:377
  157.9 10.8 %collective-permute-start.13 = (bf16[3,3,32,384]{3,2,1,0:T(8,128)(2,1)S(1)}, bf16[3,3,32,384]{3,2,1,0:T(8,128)(2,1)S(1)}, u32[]{:S(2)}, u32[]{:S(2)}) collective-permute-start(bf16[3,3,32,384]{3,2,1,0:T(8,128)(2,1)S(1)} %widened.1.own_ref.refs_2_), channel_id=1, source_target_pairs={{0,1},{1,0},{2,3},{3,2},{4,5},{5,4},{6,7},{7,6},{8,9},{9,8},{10,11... | collective-permute-start | bytes 663560 | tf_op jit(solution)/shard_map/ppermute | solution.py:436
  168.8 8.1 %collective-permute-start.14 = (bf16[3,6,8,384]{3,2,1,0:T(8,128)(2,1)S(1)}, bf16[3,6,8,384]{3,2,1,0:T(8,128)(2,1)S(1)}, u32[]{:S(2)}, u32[]{:S(2)}) collective-permute-start(bf16[3,6,8,384]{3,2,1,0:T(8,128)(2,1)S(1)} %get-tuple-element.43), channel_id=1, source_target_pairs={{16,0},{32,16},{48,32},{64,48},{80,64},{96,80},{112,96},{128,112},... | collective-permute-start | bytes 331784 | tf_op jit(solution)/shard_map/ppermute | solution.py:377
  172.9 12.0 %collective-permute-start.15 = (bf16[3,6,8,384]{3,2,1,0:T(8,128)(2,1)S(1)}, bf16[3,6,8,384]{3,2,1,0:T(8,128)(2,1)S(1)}, u32[]{:S(2)}, u32[]{:S(2)}) collective-permute-start(bf16[3,6,8,384]{3,2,1,0:T(8,128)(2,1)S(1)} %get-tuple-element.44), channel_id=1, source_target_pairs={{0,16},{16,32},{32,48},{48,64},{64,80},{80,96},{96,112},{112,128},... | collective-permute-start | bytes 331784 | tf_op jit(solution)/shard_map/ppermute | solution.py:376
  (4 other events, 3.1 us)
Sparse Core Ops, SparseCore 0:
  9.5 50.4 all-gather.3
  62.1 37.8 all-gather.5

commit v3 on v2

--- a/solution.py
+++ b/solution.py
@@ -116,40 +116,49 @@
     )(in_hbm(fields), slices)
 
 
+def join_kernel(parts_ref, out_ref):
+    for i in range(parts_ref.shape[0]):
+        wide = parts_ref.shape[2]
+        out_ref[:, i * wide : (i + 1) * wide] = parts_ref[i]
+
+
+def joined(taper, blocks):
+    parts, height, narrow = taper.shape
+    return pl.pallas_call(
+        join_kernel,
+        out_shape=shaped((height, parts * narrow), BF),
+        grid=(blocks,),
+        in_specs=[pl.BlockSpec((parts, height // blocks, narrow), lambda i: (0, i, 0))],
+        out_specs=pl.BlockSpec((height // blocks, parts * narrow), lambda i: (i, 0)),
+        compiler_params=room(6),
+        name="joined",
+    )(in_hbm(taper))
+
+
 def rows_kernel(taper_ref, fields_ref, *refs):
     out_ref, whole_ref = refs[-2:]
     peers, levels, rows, wide = fields_ref.shape
-
-    @pl.when(pl.program_id(0) == 0)
-    def _():
-        for level in range(levels):
-            whole_ref[:, level * wide : (level + 1) * wide] = fields_ref[:, level].reshape(
-                peers * rows, wide
-            )
-
-    taper = jnp.concatenate([taper_ref[i] for i in range(taper_ref.shape[0])], axis=1)
-    product = jnp.dot(taper, whole_ref[...], preferred_element_type=F32).astype(BF)
+    for level in range(levels):
+        whole_ref[:, level * wide : (level + 1) * wide] = fields_ref[:, level].reshape(
+            peers * rows, wide
+        )
+    product = jnp.dot(taper_ref[...], whole_ref[...], preferred_element_type=F32).astype(BF)
     for level in range(levels):
         out_ref[:, level] = product[:, level * wide : (level + 1) * wide].reshape(-1, rows, wide)
 
 
-def rows_pass(taper, fields, blocks, settled):
+def rows_pass(taper, fields, settled):
     peers, levels, rows, wide = fields.shape
-    parts, height, narrow = taper.shape
+    vmem = pl.BlockSpec(memory_space=pltpu.VMEM)
     return pl.pallas_call(
         rows_kernel,
         out_shape=shaped((peers, levels, rows, wide), BF),
-        grid=(blocks,),
-        in_specs=[
-            pl.BlockSpec((parts, height // blocks, narrow), lambda i: (0, i, 0)),
-            pl.BlockSpec((peers, levels, rows, wide), lambda i: (0, 0, 0, 0)),
-        ]
-        + [pl.BlockSpec(memory_space=pl.ANY)] * len(settled),
-        out_specs=pl.BlockSpec((peers // blocks, levels, rows, wide), lambda i: (i, 0, 0, 0)),
-        scratch_shapes=[pltpu.VMEM((height, levels * wide), BF)],
-        compiler_params=room(10),
+        in_specs=[vmem, vmem] + [pl.BlockSpec(memory_space=pl.ANY)] * len(settled),
+        out_specs=vmem,
+        scratch_shapes=[pltpu.VMEM((peers * rows, levels * wide), BF)],
+        compiler_params=room(12),
         name="rows_pass",
-    )(in_hbm(taper), fields, *settled)
+    )(taper, fields, *settled)
 
 
 def split_kernel(at_ref, fields_ref, *out_refs):
@@ -225,42 +234,45 @@
     return jnp.where(row < STEPS, from_next, from_previous)
 
 
-def widen_kernel(body_ref, left_ref, right_ref, out_ref):
+def widen_kernel(body_ref, left_ref, right_ref, out_ref, top_ref, bottom_ref):
     variables, levels, rows, wide = body_ref.shape
     for k in range(variables):
         for level in range(levels):
             out_ref[k, level, :, :wide] = body_ref[k, level]
             sides = beside(left_ref[k, level].astype(F32), right_ref[k, level].astype(F32))
             out_ref[k, level, :, wide:] = sides.astype(BF)
+            top_ref[k, level] = out_ref[k, level, :8]
+            bottom_ref[k, level] = out_ref[k, level, rows - 8 :]
 
 
 def widened(body, left, right):
-    shape = (*body.shape[:-1], body.shape[-1] + left.shape[-1])
+    variables, levels, rows, wide = body.shape
+    full = wide + left.shape[-1]
+    strip = shaped((variables, levels, 8, full), BF)
     return pl.pallas_call(
         widen_kernel,
-        out_shape=shaped(shape, BF),
+        out_shape=[shaped((variables, levels, rows, full), BF), strip, strip],
         compiler_params=room(4),
         name="widened",
     )(body, left, right)
 
 
-def strips_kernel(own_ref, other_ref, top_ref, bottom_ref):
-    variables, levels, rows, wide = own_ref.shape
-    for rows_at, out_ref in ((slice(0, 8), top_ref), (slice(rows - 8, rows), bottom_ref)):
-        for k in range(variables):
-            for level in range(levels):
-                out_ref[k, level] = own_ref[k, level, rows_at]
-                out_ref[k, levels + level] = other_ref[k, level, rows_at]
-
-
-def row_strips(own, other):
-    variables, levels, rows, wide = own.shape
-    return pl.pallas_call(
-        strips_kernel,
-        out_shape=[shaped((variables, 2 * levels, 8, wide), BF)] * 2,
+def ring_kernel(next_ref, previous_ref, out_ref):
+    for k in range(out_ref.shape[0]):
+        for level in range(out_ref.shape[1]):
+            rows = above_below(
+                next_ref[k, level].astype(F32), previous_ref[k, level].astype(F32)
+            )
+            out_ref[k, level] = rows.astype(BF)
+
+
+def ring(from_next, from_previous):
+    return pl.pallas_call(
+        ring_kernel,
+        out_shape=shaped(from_next.shape, BF),
         compiler_params=room(4),
-        name="row_strips",
-    )(own, other)
+        name="ring",
+    )(from_next, from_previous)
 
 
 def advect_kernel(*refs):
@@ -269,8 +281,8 @@
         own_ref,
         wider_ref,
         other_ref,
-        next_ref,
-        previous_ref,
+        ring_ref,
+        other_ring_ref,
         courant_ref,
         slope_ref,
         beside_ref,
@@ -280,7 +292,11 @@
         first_ref,
         second_ref,
         terms_ref,
+        held_ref,
+        arrival,
     ) = refs
+    fetch = pltpu.make_async_copy(own_ref, held_ref, arrival)
+    fetch.start()
     variables, levels, rows, wide = own_ref.shape
     deep, tall, full = first_ref.shape[1:]
     flip = flip_ref[0]
@@ -295,14 +311,11 @@
         mine = level < levels
         for k in range(variables):
             if mine:
-                first_ref[k, level, :rows, :wide] = own_ref[k, at]
                 first_ref[k, level, :rows, wide:] = wider_ref[k, at, :, wide:].astype(F32)
             else:
                 first_ref[k, level, :rows, :] = other_ref[k, at].astype(F32)
-            strip = at if mine else at + levels
-            first_ref[k, level, rows:, :] = above_below(
-                next_ref[k, strip].astype(F32), previous_ref[k, strip].astype(F32)
-            )
+            strip_ref = ring_ref if mine else other_ring_ref
+            first_ref[k, level, rows:, :] = strip_ref[k, at].astype(F32)
         planes = []
         for a in range(directions + slope_ref.shape[0]):
             if mine:
@@ -320,6 +333,11 @@
             terms_ref[2 + 2 * a, level] = -jnp.minimum(planes[a], 0.0)
         for a in range(directions, len(planes)):
             terms_ref[1 + directions + a, level] = planes[a]
+
+    fetch.wait()
+    for level in range(levels):
+        for k in range(variables):
+            first_ref[k, level, :rows, :wide] = held_ref[k, local(level)]
 
     old_ref, new_ref = (first_ref, second_ref)
     for step in range(STEPS):
@@ -355,9 +373,16 @@
     return pl.pallas_call(
         advect_kernel,
         out_shape=shaped((variables, levels, rows, wide), F32),
-        in_specs=[pl.BlockSpec(memory_space=pltpu.SMEM)] + [vmem] * len(arrays),
+        in_specs=[pl.BlockSpec(memory_space=pltpu.SMEM), pl.BlockSpec(memory_space=pl.ANY)]
+        + [vmem] * (len(arrays) - 1),
         out_specs=vmem,
-        scratch_shapes=[state, state, pltpu.VMEM((9, 2 * levels, tall, full), F32)],
+        scratch_shapes=[
+            state,
+            state,
+            pltpu.VMEM((9, 2 * levels, tall, full), F32),
+            pltpu.VMEM((variables, levels, rows, wide), F32),
+            pltpu.SemaphoreType.DMA(()),
+        ],
         compiler_params=room(14),
         name="advect",
     )(flip, *arrays)
@@ -418,30 +443,31 @@
             weights[step] = piece
 
     settled = [*exchange((1,)), taller]
+    (taller,) = after([taller], [slices])
+    opposite = lax.ppermute(taller, "lev", swap("lev"))
     first_pass = columns_pass(every, slices, tall, levels, rows, 2)
     row_whole = lax.all_gather(row_part(slices, tall, settled), "mem", axis=0, tiled=False)
     row_whole = row_whole.reshape(parts, row_taper.shape[1], -1)
     hold((2, 3, 6, 7), [first_pass])
     arrived = lax.all_to_all(first_pass, "row", 0, 0, tiled=True)
-    tapered = rows_pass(row_whole, arrived, 4, exchange((2, 3, 6, 7)))
+    tapered = rows_pass(joined(row_whole, 4), arrived, [*exchange((2, 3, 6, 7)), opposite])
     hold((4, 5), [tapered])
-    (taller,) = after([taller], [tapered])
     localized = lax.all_to_all(tapered, "row", 0, 0, tiled=True)
     exchange((4, 5))
-    opposite = lax.ppermute(taller, "lev", swap("lev"))
     weights = [weights[step] for step in range(parts)]
     own, rounded, first, last = weighted_sum(at, localized, weights)
 
-    wider = widened(rounded, *neighbours(first, last, "mem"))
+    wider, top, bottom = widened(rounded, *neighbours(first, last, "mem"))
     other = lax.ppermute(wider, "lev", swap("lev"))
-    from_previous, from_next = neighbours(*row_strips(wider, other), "row")
+    from_previous, from_next = neighbours(top, bottom, "row")
+    rows_around = ring(from_next, from_previous)
     return advect(
         flip,
         own,
         wider,
         other,
-        from_next,
-        from_previous,
+        rows_around,
+        lax.ppermute(rows_around, "lev", swap("lev")),
         courant_numbers,
         tracer_slope,
         sides,

time: 197 us -> 191 us (0.970)
  the two profiles are of different devices: /device:TPU:74 before, /device:TPU:66 now
where the time goes in v3:
time: 191 us; the launch traced here: 190 us
  starting transfers between devices  89.3 us (47%)
  waiting for transfers between devices  65.1 us (34%)
  Pallas kernels  17.6 us (9%)
  between operations  13.9 us (7%)
  local copies, waits for them, and re-layouts  3.89 us (2%)
    ppermute x4, waiting for transfers between devices, neighbours(): from_left = lax.ppermute(last, axis, chain(axis, 1))  22.6 us
    ppermute x7, starting transfers between devices, exchange(): weights[step] = lax.ppermute(weights[step], 'mem', pairs)  20.3 us
    ppermute x4, starting transfers between devices, neighbours(): from_right = lax.ppermute(first, axis, chain(axis, -1))  16 us
    all_to_all x1, starting transfers between devices, on_device(): lax.all_to_all(taper_slices(at, column_taper, row_taper, peers, parts), '...  15.4 us
    ppermute x7, waiting for transfers between devices, exchange(): weights[step] = lax.ppermute(weights[step], 'mem', pairs)  11.1 us
    all_to_all x1, starting transfers between devices, on_device(): localized = lax.all_to_all(tapered, 'row', 0, 0, tiled=True)  10.9 us
    ppermute x4, starting transfers between devices, neighbours(): from_left = lax.ppermute(last, axis, chain(axis, 1))  10.7 us
    all_to_all x1, starting transfers between devices, on_device(): arrived = lax.all_to_all(first_pass, 'row', 0, 0, tiled=True)  8.43 us
  transfers between devices with their start and end apart: 23, of which 12 were waited for; matrix products, arithmetic and copies ran while one was open for 0% of the time, Pallas kernels for 5%

profile of v3, /device:TPU:66, one launch (start us, length us, event | category | flops | bytes accessed | tf_op | source)
XLA Modules:
  0.0 190.0 jit_solution(8086838635088327388)
XLA Ops:
  7.3 2.0 %taper_slices.1 = bf16[32,80,256]{2,1,0:T(8,128)(2,1)} custom-call(s32[1]{0:T(128)} %bitcast.1._.at_ref.refs_0_, bf16[64,2048]{1,0:T(8,128)(2,1)} %column_ref.1, bf16[32,1024]{1,0:T(8,128)(2,1)} %row_ref.1), custom_call_target="tpu_custom_call" | custom-call | tf_op jit(solution)/shard_map/taper_slices/pallas_call | solution.py:52
  9.3 15.4 %all-to-all-start = ((bf16[32,80,256]{2,1,0:T(8,128)(2,1)}), bf16[32,80,256]{2,1,0:T(8,128)(2,1)S(1)}, u32[]{:S(2)}, u32[]{:S(2)}) async-start(bf16[32,80,256]{2,1,0:T(8,128)(2,1)} %taper_slices.1), calls=%async_computation | async-start | bytes 2621440 | tf_op jit(solution)/shard_map/all_to_all | solution.py:428
  24.9 1.9 %collective-permute-start.2 = (bf16[5,3,32,128]{3,2,1,0:T(8,128)(2,1)S(1)}, bf16[5,3,32,128]{3,2,1,0:T(8,128)(2,1)S(1)}, u32[]{:S(2)}, u32[]{:S(2)}) collective-permute-start(bf16[5,3,32,128]{3,2,1,0:T(8,128)(2,1)S(1)} %get-tuple-element.49), channel_id=1, source_target_pairs={{0,2},{2,4},{4,6},{6,8},{8,10},{10,12},{12,14},{1,3},{3,5},{5,7},{... | collective-permute-start | bytes 368648 | tf_op jit(solution)/shard_map/ppermute | solution.py:401
  26.8 3.6 %collective-permute-start.1 = (bf16[5,3,32,128]{3,2,1,0:T(8,128)(2,1)S(1)}, bf16[5,3,32,128]{3,2,1,0:T(8,128)(2,1)S(1)}, u32[]{:S(2)}, u32[]{:S(2)}) collective-permute-start(bf16[5,3,32,128]{3,2,1,0:T(8,128)(2,1)S(1)} %get-tuple-element.50), channel_id=1, source_target_pairs={{2,0},{4,2},{6,4},{8,6},{10,8},{12,10},{14,12},{3,1},{5,3},{7,5},{... | collective-permute-start | bytes 368648 | tf_op jit(solution)/shard_map/ppermute | solution.py:402
  34.6 1.9 %collective-permute-start = (bf16[3,2,3,32,256]{4,3,2,1,0:T(8,128)(2,1)S(1)}, bf16[3,2,3,32,256]{4,3,2,1,0:T(8,128)(2,1)S(1)}, u32[]{:S(2)}, u32[]{:S(2)}) collective-permute-start(bf16[3,2,3,32,256]{4,3,2,1,0:T(8,128)(2,1)S(1)} %get-tuple-element.26), channel_id=1, source_target_pairs={{0,2},{2,0},{4,6},{6,4},{8,10},{10,8},{12,14},{14,12},{1,3},{3,1},... | collective-permute-start | bytes 884744 | tf_op jit(solution)/shard_map/ppermute | solution.py:438
  36.6 4.3 %collective-permute-start.4 = (bf16[5,3,8,384]{3,2,1,0:T(8,128)(2,1)S(1)}, bf16[5,3,8,384]{3,2,1,0:T(8,128)(2,1)S(1)}, u32[]{:S(2)}, u32[]{:S(2)}) collective-permute-start(bf16[5,3,8,384]{3,2,1,0:T(8,128)(2,1)S(1)} %get-tuple-element.47), channel_id=1, source_target_pairs={{0,16},{16,32},{32,48},{48,64},{64,80},{80,96},{96,112},{112,128},... | collective-permute-start | bytes 276488 | tf_op jit(solution)/shard_map/ppermute | solution.py:401
  40.9 4.6 %collective-permute-start.3 = (bf16[5,3,8,384]{3,2,1,0:T(8,128)(2,1)S(1)}, bf16[5,3,8,384]{3,2,1,0:T(8,128)(2,1)S(1)}, u32[]{:S(2)}, u32[]{:S(2)}) collective-permute-start(bf16[5,3,8,384]{3,2,1,0:T(8,128)(2,1)S(1)} %get-tuple-element.48), channel_id=1, source_target_pairs={{16,0},{32,16},{48,32},{64,48},{80,64},{96,80},{112,96},{128,112},... | collective-permute-start | bytes 276488 | tf_op jit(solution)/shard_map/ppermute | solution.py:402
  45.5 15.7 %collective-permute-done.4 = bf16[5,3,8,384]{3,2,1,0:T(8,128)(2,1)S(1)} collective-permute-done((bf16[5,3,8,384]{3,2,1,0:T(8,128)(2,1)S(1)}, bf16[5,3,8,384]{3,2,1,0:T(8,128)(2,1)S(1)}, u32[]{:S(2)}, u32[]{:S(2)}) %collective-permute-start.4) | collective-permute-done | bytes 92192 | tf_op jit(solution)/shard_map/ppermute | solution.py:401
  61.4 5.8 %all-to-all-done.a.b.refs_1_ = bf16[32,80,256]{2,1,0:T(8,128)(2,1)S(1)} async-done(((bf16[32,80,256]{2,1,0:T(8,128)(2,1)}), bf16[32,80,256]{2,1,0:T(8,128)(2,1)S(1)}, u32[]{:S(2)}, u32[]{:S(2)}) %all-to-all-start) | async-done | bytes 1310752 | tf_op jit(solution)/shard_map/all_to_all | solution.py:428
  68.1 4.6 %columns_pass.1.refs_4_ = bf16[32,3,32,128]{3,2,1,0:T(8,128)(2,1)} custom-call(bf16[1536,2048]{1,0:T(8,128)(2,1)} %all-gather.4.cloned.1.call-done.a, bf16[32,80,256]{2,1,0:T(8,128)(2,1)S(1)} %all-to-all-done.a.b.refs_1_), custom_call_target="tpu_custom_call" | custom-call | tf_op jit(solution)/shard_map/columns_pass/pallas_call | solution.py:105
  72.7 8.4 %all-to-all-start.1 = ((bf16[32,3,32,128]{3,2,1,0:T(8,128)(2,1)}), bf16[32,3,32,128]{3,2,1,0:T(8,128)(2,1)S(1)}, u32[]{:S(2)}, u32[]{:S(2)}) async-start(bf16[32,3,32,128]{3,2,1,0:T(8,128)(2,1)} %columns_pass.1.refs_4_), calls=%async_computation.1 | async-start | bytes 1572864 | tf_op jit(solution)/shard_map/all_to_all | solution.py:452
  83.1 3.4 %collective-permute-start.5 = (bf16[3,2,3,32,256]{4,3,2,1,0:T(8,128)(2,1)}, bf16[3,2,3,32,256]{4,3,2,1,0:T(8,128)(2,1)}, u32[]{:S(2)}, u32[]{:S(2)}) collective-permute-start(bf16[3,2,3,32,256]{4,3,2,1,0:T(8,128)(2,1)} %get-tuple-element.31), channel_id=1, source_target_pairs={{0,4},{2,6},{4,0},{6,2},{8,12},{10,14},{12,8},{14,10},{1,5},{3,7},... | collective-permute-start | bytes 884744 | tf_op jit(solution)/shard_map/ppermute | solution.py:438
  86.5 1.9 %collective-permute-start.6 = (bf16[3,2,3,32,256]{4,3,2,1,0:T(8,128)(2,1)}, bf16[3,2,3,32,256]{4,3,2,1,0:T(8,128)(2,1)}, u32[]{:S(2)}, u32[]{:S(2)}) collective-permute-start(bf16[3,2,3,32,256]{4,3,2,1,0:T(8,128)(2,1)} %get-tuple-element.32), channel_id=1, source_target_pairs={{0,6},{2,4},{4,2},{6,0},{8,14},{10,12},{12,10},{14,8},{1,7},{3,5},... | collective-permute-start | bytes 884744 | tf_op jit(solution)/shard_map/ppermute | solution.py:438
  88.4 3.1 %collective-permute-start.7 = (bf16[3,2,3,32,256]{4,3,2,1,0:T(8,128)(2,1)}, bf16[3,2,3,32,256]{4,3,2,1,0:T(8,128)(2,1)}, u32[]{:S(2)}, u32[]{:S(2)}) collective-permute-start(bf16[3,2,3,32,256]{4,3,2,1,0:T(8,128)(2,1)} %get-tuple-element.33), channel_id=1, source_target_pairs={{0,12},{2,14},{4,8},{6,10},{8,4},{10,6},{12,0},{14,2},{1,13},{3,15... | collective-permute-start | bytes 884744 | tf_op jit(solution)/shard_map/ppermute | solution.py:438
  91.6 2.7 %collective-permute-start.8 = (bf16[3,2,3,32,256]{4,3,2,1,0:T(8,128)(2,1)}, bf16[3,2,3,32,256]{4,3,2,1,0:T(8,128)(2,1)}, u32[]{:S(2)}, u32[]{:S(2)}) collective-permute-start(bf16[3,2,3,32,256]{4,3,2,1,0:T(8,128)(2,1)} %get-tuple-element.34), channel_id=1, source_target_pairs={{0,14},{2,12},{4,10},{6,8},{8,6},{10,4},{12,2},{14,0},{1,15},{3,13... | collective-permute-start | bytes 884744 | tf_op jit(solution)/shard_map/ppermute | solution.py:438
  94.3 4.5 %all-gather.6.cloned.1.call-done = bf16[256,32,128]{2,1,0:T(8,128)(2,1)} async-done(((bf16[32,32,128]{2,1,0:T(8,128)(2,1)}), bf16[256,32,128]{2,1,0:T(8,128)(2,1)}) %all-gather.6.cloned.1.call-update) | async-done | bytes 2097168 | tf_op jit(solution)/shard_map/all_gather | solution.py:449
  98.8 2.6 %joined.1.taper_ref = bf16[1024,1024]{1,0:T(8,128)(2,1)S(1)} custom-call(bf16[8,1024,128]{2,1,0:T(8,128)(2,1)} %bitcast.4), custom_call_target="tpu_custom_call" | custom-call | tf_op jit(solution)/shard_map/joined/pallas_call | solution.py:127
  101.4 6.6 %collective-permute-done.9.refs_4_.refs_10_ = bf16[5,3,40,384]{3,2,1,0:T(8,128)(2,1)S(1)} collective-permute-done((bf16[5,3,40,384]{3,2,1,0:T(8,128)(2,1)}, bf16[5,3,40,384]{3,2,1,0:T(8,128)(2,1)S(1)}, u32[]{:S(2)}, u32[]{:S(2)}) %collective-permute-start.9) | collective-permute-done | bytes 460832 | tf_op jit(solution)/shard_map/ppermute | solution.py:447
  108.0 2.2 %rows_pass.1.refs_2_ = bf16[32,3,32,128]{3,2,1,0:T(8,128)(2,1)} custom-call(bf16[1024,1024]{1,0:T(8,128)(2,1)S(1)} %joined.1.taper_ref, bf16[32,3,32,128]{3,2,1,0:T(8,128)(2,1)S(1)} %all-to-all-done.1.fields_ref, bf16[3,2,3,32,256]{4,3,2,1,0:T(8,128)(2,1)} %collective-permute-done.5.refs_0_.refs_4_, ...), custom_call_target="tpu_custom_call" | custom-call | tf_op jit(solution)/shard_map/rows_pass/pallas_call | solution.py:153
  110.2 10.9 %all-to-all-start.2 = ((bf16[32,3,32,128]{3,2,1,0:T(8,128)(2,1)}), bf16[32,3,32,128]{3,2,1,0:T(8,128)(2,1)S(1)}, u32[]{:S(2)}, u32[]{:S(2)}) async-start(bf16[32,3,32,128]{3,2,1,0:T(8,128)(2,1)} %rows_pass.1.refs_2_), calls=%async_computation.2 | async-start | bytes 1572864 | tf_op jit(solution)/shard_map/all_to_all | solution.py:455
  121.1 5.4 %collective-permute-start.10 = (bf16[3,2,3,32,256]{4,3,2,1,0:T(8,128)(2,1)}, bf16[3,2,3,32,256]{4,3,2,1,0:T(8,128)(2,1)S(1)}, u32[]{:S(2)}, u32[]{:S(2)}) collective-permute-start(bf16[3,2,3,32,256]{4,3,2,1,0:T(8,128)(2,1)} %get-tuple-element.38), channel_id=1, source_target_pairs={{0,8},{2,10},{4,12},{6,14},{8,0},{10,2},{12,4},{14,6},{1,9},{3,11}... | collective-permute-start | bytes 884744 | tf_op jit(solution)/shard_map/ppermute | solution.py:438
  128.4 5.8 %collective-permute-done.10.refs_6_ = bf16[3,2,3,32,256]{4,3,2,1,0:T(8,128)(2,1)S(1)} collective-permute-done((bf16[3,2,3,32,256]{4,3,2,1,0:T(8,128)(2,1)}, bf16[3,2,3,32,256]{4,3,2,1,0:T(8,128)(2,1)S(1)}, u32[]{:S(2)}, u32[]{:S(2)}) %collective-permute-start.10) | collective-permute-done | bytes 294944 | tf_op jit(solution)/shard_map/ppermute | solution.py:438
  134.3 5.2 %collective-permute-done.11.refs_7_ = bf16[3,2,3,32,256]{4,3,2,1,0:T(8,128)(2,1)S(1)} collective-permute-done((bf16[3,2,3,32,256]{4,3,2,1,0:T(8,128)(2,1)}, bf16[3,2,3,32,256]{4,3,2,1,0:T(8,128)(2,1)S(1)}, u32[]{:S(2)}, u32[]{:S(2)}) %collective-permute-start.11) | collective-permute-done | bytes 294944 | tf_op jit(solution)/shard_map/ppermute | solution.py:438
  139.5 7.5 %all-to-all-done.2.refs_1_ = bf16[32,3,32,128]{3,2,1,0:T(8,128)(2,1)S(1)} async-done(((bf16[32,3,32,128]{3,2,1,0:T(8,128)(2,1)}), bf16[32,3,32,128]{3,2,1,0:T(8,128)(2,1)S(1)}, u32[]{:S(2)}, u32[]{:S(2)}) %all-to-all-start.2) | async-done | bytes 786464 | tf_op jit(solution)/shard_map/all_to_all | solution.py:455
  150.7 3.6 %collective-permute-start.13 = (bf16[3,3,32,128]{3,2,1,0:T(8,128)(2,1)S(1)}, bf16[3,3,32,128]{3,2,1,0:T(8,128)(2,1)S(1)}, u32[]{:S(2)}, u32[]{:S(2)}) collective-permute-start(bf16[3,3,32,128]{3,2,1,0:T(8,128)(2,1)S(1)} %get-tuple-element.43), channel_id=1, source_target_pairs={{2,0},{4,2},{6,4},{8,6},{10,8},{12,10},{14,12},{3,1},{5,3},{7,5},{... | collective-permute-start | bytes 221192 | tf_op jit(solution)/shard_map/ppermute | solution.py:402
  156.3 3.6 %collective-permute-start.14 = (bf16[3,3,32,384]{3,2,1,0:T(8,128)(2,1)S(1)}, bf16[3,3,32,384]{3,2,1,0:T(8,128)(2,1)S(1)}, u32[]{:S(2)}, u32[]{:S(2)}) collective-permute-start(bf16[3,3,32,384]{3,2,1,0:T(8,128)(2,1)S(1)} %get-tuple-element.44.refs_2_), channel_id=1, source_target_pairs={{0,1},{1,0},{2,3},{3,2},{4,5},{5,4},{6,7},{7,6},{8,9},{9,8},{10,11... | collective-permute-start | bytes 663560 | tf_op jit(solution)/shard_map/ppermute | solution.py:461
  160.0 4.2 %collective-permute-start.15 = (bf16[3,3,8,384]{3,2,1,0:T(8,128)(2,1)S(1)}, bf16[3,3,8,384]{3,2,1,0:T(8,128)(2,1)S(1)}, u32[]{:S(2)}, u32[]{:S(2)}) collective-permute-start(bf16[3,3,8,384]{3,2,1,0:T(8,128)(2,1)S(1)} %get-tuple-element.45), channel_id=1, source_target_pairs={{16,0},{32,16},{48,32},{64,48},{80,64},{96,80},{112,96},{128,112},... | collective-permute-start | bytes 165896 | tf_op jit(solution)/shard_map/ppermute | solution.py:402
  164.2 2.6 %collective-permute-start.16 = (bf16[3,3,8,384]{3,2,1,0:T(8,128)(2,1)S(1)}, bf16[3,3,8,384]{3,2,1,0:T(8,128)(2,1)S(1)}, u32[]{:S(2)}, u32[]{:S(2)}) collective-permute-start(bf16[3,3,8,384]{3,2,1,0:T(8,128)(2,1)S(1)} %get-tuple-element.46), channel_id=1, source_target_pairs={{0,16},{16,32},{32,48},{48,64},{64,80},{80,96},{96,112},{112,128},... | collective-permute-start | bytes 165896 | tf_op jit(solution)/shard_map/ppermute | solution.py:401
  167.0 6.9 %collective-permute-done.16.previous_ref = bf16[3,3,8,384]{3,2,1,0:T(8,128)(2,1)S(1)} collective-permute-done((bf16[3,3,8,384]{3,2,1,0:T(8,128)(2,1)S(1)}, bf16[3,3,8,384]{3,2,1,0:T(8,128)(2,1)S(1)}, u32[]{:S(2)}, u32[]{:S(2)}) %collective-permute-start.16) | collective-permute-done | bytes 55328 | tf_op jit(solution)/shard_map/ppermute | solution.py:401
  173.9 1.9 %collective-permute-start.17 = (bf16[3,3,8,384]{3,2,1,0:T(8,128)(2,1)S(1)}, bf16[3,3,8,384]{3,2,1,0:T(8,128)(2,1)S(1)}, u32[]{:S(2)}, u32[]{:S(2)}) collective-permute-start(bf16[3,3,8,384]{3,2,1,0:T(8,128)(2,1)S(1)} %ring.1.refs_4_), channel_id=1, source_target_pairs={{0,1},{1,0},{2,3},{3,2},{4,5},{5,4},{6,7},{7,6},{8,9},{9,8},{10,11... | collective-permute-start | bytes 165896 | tf_op jit(solution)/shard_map/ppermute | solution.py:470
  175.8 4.1 %collective-permute-done.17.refs_5_ = bf16[3,3,8,384]{3,2,1,0:T(8,128)(2,1)S(1)} collective-permute-done((bf16[3,3,8,384]{3,2,1,0:T(8,128)(2,1)S(1)}, bf16[3,3,8,384]{3,2,1,0:T(8,128)(2,1)S(1)}, u32[]{:S(2)}, u32[]{:S(2)}) %collective-permute-start.17) | collective-permute-done | bytes 55328 | tf_op jit(solution)/shard_map/ppermute | solution.py:470
  180.0 3.2 %advect.1 = f32[3,3,32,256]{3,2,1,0:T(8,128)} custom-call(s32[1]{0:T(128)} %bitcast.refs_0_, f32[3,3,32,256]{3,2,1,0:T(8,128)S(1)} %get-tuple-element.40.refs_1_, bf16[3,3,32,384]{3,2,1,0:T(8,128)(2,1)S(1)} %get-tuple-element.44.refs_2_, bf16[3,3,32,384]{3,2,1,0:T(8,128)(2,1)S(1)} %collective-permute-done.14.refs_3_, ...), custom_call_target="tpu_custom_call" | custom-call | tf_op jit(solution)/shard_map/advect/pallas_call | solution.py:373
  (76 shorter events, 16.0 us)
Async XLA Ops:
  6.5 61.5 %all-gather.4.cloned.1.call-start = ((), (), s32[]{:S(2)}) async-start(), calls=%async_computation.3 | async-start | bytes 7077888 | tf_op jit(solution)/shard_map/all_gather | solution.py:425
  9.3 57.9 %all-to-all-start = ((bf16[32,80,256]{2,1,0:T(8,128)(2,1)}), bf16[32,80,256]{2,1,0:T(8,128)(2,1)S(1)}, u32[]{:S(2)}, u32[]{:S(2)}) async-start(bf16[32,80,256]{2,1,0:T(8,128)(2,1)} %taper_slices.1), calls=%async_computation | async-start | bytes 2621440 | tf_op jit(solution)/shard_map/all_to_all | solution.py:428
  24.7 74.1 %all-gather.6.cloned.1.call-start = ((), (), s32[]{:S(2)}) async-start(), calls=%async_computation.4 | async-start | bytes 2359296 | tf_op jit(solution)/shard_map/all_gather | solution.py:449
  24.9 11.7 %collective-permute-start.2 = (bf16[5,3,32,128]{3,2,1,0:T(8,128)(2,1)S(1)}, bf16[5,3,32,128]{3,2,1,0:T(8,128)(2,1)S(1)}, u32[]{:S(2)}, u32[]{:S(2)}) collective-permute-start(bf16[5,3,32,128]{3,2,1,0:T(8,128)(2,1)S(1)} %get-tuple-element.49), channel_id=1, source_target_pairs={{0,2},{2,4},{4,6},{6,8},{8,10},{10,12},{12,14},{1,3},{3,5},{5,7},{... | collective-permute-start | bytes 368648 | tf_op jit(solution)/shard_map/ppermute | solution.py:401
  26.8 9.8 %collective-permute-start.1 = (bf16[5,3,32,128]{3,2,1,0:T(8,128)(2,1)S(1)}, bf16[5,3,32,128]{3,2,1,0:T(8,128)(2,1)S(1)}, u32[]{:S(2)}, u32[]{:S(2)}) collective-permute-start(bf16[5,3,32,128]{3,2,1,0:T(8,128)(2,1)S(1)} %get-tuple-element.50), channel_id=1, source_target_pairs={{2,0},{4,2},{6,4},{8,6},{10,8},{12,10},{14,12},{3,1},{5,3},{7,5},{... | collective-permute-start | bytes 368648 | tf_op jit(solution)/shard_map/ppermute | solution.py:402
  34.6 26.6 %copy-start.13 = (bf16[3,2,3,32,256]{4,3,2,1,0:T(8,128)(2,1)}, bf16[3,2,3,32,256]{4,3,2,1,0:T(8,128)(2,1)S(1)}, u32[]{:S(2)}) copy-start(bf16[3,2,3,32,256]{4,3,2,1,0:T(8,128)(2,1)S(1)} %get-tuple-element.36.refs_0_) | copy-start | bytes 884740
  34.6 26.6 %copy-start.14 = (bf16[3,2,3,32,256]{4,3,2,1,0:T(8,128)(2,1)}, bf16[3,2,3,32,256]{4,3,2,1,0:T(8,128)(2,1)S(1)}, u32[]{:S(2)}) copy-start(bf16[3,2,3,32,256]{4,3,2,1,0:T(8,128)(2,1)S(1)} %get-tuple-element.37.refs_1_) | copy-start | bytes 884740
  34.6 26.6 %copy-start.15 = (bf16[3,2,3,32,256]{4,3,2,1,0:T(8,128)(2,1)}, bf16[3,2,3,32,256]{4,3,2,1,0:T(8,128)(2,1)S(1)}, u32[]{:S(2)}) copy-start(bf16[3,2,3,32,256]{4,3,2,1,0:T(8,128)(2,1)S(1)} %get-tuple-element.27.refs_0_) | copy-start | bytes 884740
  34.6 26.7 %copy-start.18 = (bf16[3,2,3,32,256]{4,3,2,1,0:T(8,128)(2,1)}, bf16[3,2,3,32,256]{4,3,2,1,0:T(8,128)(2,1)S(1)}, u32[]{:S(2)}) copy-start(bf16[3,2,3,32,256]{4,3,2,1,0:T(8,128)(2,1)S(1)} %get-tuple-element.30.refs_3_) | copy-start | bytes 884740
  34.6 26.7 %collective-permute-start = (bf16[3,2,3,32,256]{4,3,2,1,0:T(8,128)(2,1)S(1)}, bf16[3,2,3,32,256]{4,3,2,1,0:T(8,128)(2,1)S(1)}, u32[]{:S(2)}, u32[]{:S(2)}) collective-permute-start(bf16[3,2,3,32,256]{4,3,2,1,0:T(8,128)(2,1)S(1)} %get-tuple-element.26), channel_id=1, source_target_pairs={{0,2},{2,0},{4,6},{6,4},{8,10},{10,8},{12,14},{14,12},{1,3},{3,1},... | collective-permute-start | bytes 884744 | tf_op jit(solution)/shard_map/ppermute | solution.py:438
  36.6 24.5 %collective-permute-start.4 = (bf16[5,3,8,384]{3,2,1,0:T(8,128)(2,1)S(1)}, bf16[5,3,8,384]{3,2,1,0:T(8,128)(2,1)S(1)}, u32[]{:S(2)}, u32[]{:S(2)}) collective-permute-start(bf16[5,3,8,384]{3,2,1,0:T(8,128)(2,1)S(1)} %get-tuple-element.47), channel_id=1, source_target_pairs={{0,16},{16,32},{32,48},{48,64},{64,80},{80,96},{96,112},{112,128},... | collective-permute-start | bytes 276488 | tf_op jit(solution)/shard_map/ppermute | solution.py:401
  40.9 20.2 %collective-permute-start.3 = (bf16[5,3,8,384]{3,2,1,0:T(8,128)(2,1)S(1)}, bf16[5,3,8,384]{3,2,1,0:T(8,128)(2,1)S(1)}, u32[]{:S(2)}, u32[]{:S(2)}) collective-permute-start(bf16[5,3,8,384]{3,2,1,0:T(8,128)(2,1)S(1)} %get-tuple-element.48), channel_id=1, source_target_pairs={{16,0},{32,16},{48,32},{64,48},{80,64},{96,80},{112,96},{128,112},... | collective-permute-start | bytes 276488 | tf_op jit(solution)/shard_map/ppermute | solution.py:402
  72.7 35.2 %all-to-all-start.1 = ((bf16[32,3,32,128]{3,2,1,0:T(8,128)(2,1)}), bf16[32,3,32,128]{3,2,1,0:T(8,128)(2,1)S(1)}, u32[]{:S(2)}, u32[]{:S(2)}) async-start(bf16[32,3,32,128]{3,2,1,0:T(8,128)(2,1)} %columns_pass.1.refs_4_), calls=%async_computation.1 | async-start | bytes 1572864 | tf_op jit(solution)/shard_map/all_to_all | solution.py:452
  81.2 26.8 %collective-permute-start.9 = (bf16[5,3,40,384]{3,2,1,0:T(8,128)(2,1)}, bf16[5,3,40,384]{3,2,1,0:T(8,128)(2,1)S(1)}, u32[]{:S(2)}, u32[]{:S(2)}) collective-permute-start(bf16[5,3,40,384]{3,2,1,0:T(8,128)(2,1)} %after.4), channel_id=1, source_target_pairs={{0,1},{1,0},{2,3},{3,2},{4,5},{5,4},{6,7},{7,6},{8,9},{9,8},{10,11... | collective-permute-start | bytes 1382408 | tf_op jit(solution)/shard_map/ppermute | solution.py:447
  83.1 24.8 %collective-permute-start.5 = (bf16[3,2,3,32,256]{4,3,2,1,0:T(8,128)(2,1)}, bf16[3,2,3,32,256]{4,3,2,1,0:T(8,128)(2,1)}, u32[]{:S(2)}, u32[]{:S(2)}) collective-permute-start(bf16[3,2,3,32,256]{4,3,2,1,0:T(8,128)(2,1)} %get-tuple-element.31), channel_id=1, source_target_pairs={{0,4},{2,6},{4,0},{6,2},{8,12},{10,14},{12,8},{14,10},{1,5},{3,7},... | collective-permute-start | bytes 884744 | tf_op jit(solution)/shard_map/ppermute | solution.py:438
  86.5 21.4 %collective-permute-start.6 = (bf16[3,2,3,32,256]{4,3,2,1,0:T(8,128)(2,1)}, bf16[3,2,3,32,256]{4,3,2,1,0:T(8,128)(2,1)}, u32[]{:S(2)}, u32[]{:S(2)}) collective-permute-start(bf16[3,2,3,32,256]{4,3,2,1,0:T(8,128)(2,1)} %get-tuple-element.32), channel_id=1, source_target_pairs={{0,6},{2,4},{4,2},{6,0},{8,14},{10,12},{12,10},{14,8},{1,7},{3,5},... | collective-permute-start | bytes 884744 | tf_op jit(solution)/shard_map/ppermute | solution.py:438
  88.4 19.5 %collective-permute-start.7 = (bf16[3,2,3,32,256]{4,3,2,1,0:T(8,128)(2,1)}, bf16[3,2,3,32,256]{4,3,2,1,0:T(8,128)(2,1)}, u32[]{:S(2)}, u32[]{:S(2)}) collective-permute-start(bf16[3,2,3,32,256]{4,3,2,1,0:T(8,128)(2,1)} %get-tuple-element.33), channel_id=1, source_target_pairs={{0,12},{2,14},{4,8},{6,10},{8,4},{10,6},{12,0},{14,2},{1,13},{3,15... | collective-permute-start | bytes 884744 | tf_op jit(solution)/shard_map/ppermute | solution.py:438
  91.6 16.4 %collective-permute-start.8 = (bf16[3,2,3,32,256]{4,3,2,1,0:T(8,128)(2,1)}, bf16[3,2,3,32,256]{4,3,2,1,0:T(8,128)(2,1)}, u32[]{:S(2)}, u32[]{:S(2)}) collective-permute-start(bf16[3,2,3,32,256]{4,3,2,1,0:T(8,128)(2,1)} %get-tuple-element.34), channel_id=1, source_target_pairs={{0,14},{2,12},{4,10},{6,8},{8,6},{10,4},{12,2},{14,0},{1,15},{3,13... | collective-permute-start | bytes 884744 | tf_op jit(solution)/shard_map/ppermute | solution.py:438
  110.2 36.8 %copy-start.6 = (bf16[3,2,3,32,256]{4,3,2,1,0:T(8,128)(2,1)S(1)}, bf16[3,2,3,32,256]{4,3,2,1,0:T(8,128)(2,1)}, u32[]{:S(2)}) copy-start(bf16[3,2,3,32,256]{4,3,2,1,0:T(8,128)(2,1)} %copy-done.5) | copy-start | bytes 884740
  110.2 36.8 %copy-start.12 = (bf16[3,2,3,32,256]{4,3,2,1,0:T(8,128)(2,1)S(1)}, bf16[3,2,3,32,256]{4,3,2,1,0:T(8,128)(2,1)}, u32[]{:S(2)}) copy-start(bf16[3,2,3,32,256]{4,3,2,1,0:T(8,128)(2,1)} %copy-done.11) | copy-start | bytes 884740
  110.2 36.8 %all-to-all-start.2 = ((bf16[32,3,32,128]{3,2,1,0:T(8,128)(2,1)}), bf16[32,3,32,128]{3,2,1,0:T(8,128)(2,1)S(1)}, u32[]{:S(2)}, u32[]{:S(2)}) async-start(bf16[32,3,32,128]{3,2,1,0:T(8,128)(2,1)} %rows_pass.1.refs_2_), calls=%async_computation.2 | async-start | bytes 1572864 | tf_op jit(solution)/shard_map/all_to_all | solution.py:455
  121.1 58.8 %copy-start.4 = (f32[3,3,32,256]{3,2,1,0:T(8,128)S(1)}, f32[3,3,32,256]{3,2,1,0:T(8,128)}, u32[]{:S(2)}) copy-start(f32[3,3,32,256]{3,2,1,0:T(8,128)} %refs_6_.1) | copy-start | bytes 884740
  121.1 58.8 %copy-start.8 = (bf16[5,3,8,384]{3,2,1,0:T(8,128)(2,1)S(1)}, bf16[5,3,8,384]{3,2,1,0:T(8,128)(2,1)}, u32[]{:S(2)}) copy-start(bf16[5,3,8,384]{3,2,1,0:T(8,128)(2,1)} %copy-done.7) | copy-start | bytes 276484
  121.1 58.8 %copy-start.10 = (f32[2,3,32,256]{3,2,1,0:T(8,128)S(1)}, f32[2,3,32,256]{3,2,1,0:T(8,128)}, u32[]{:S(2)}) copy-start(f32[2,3,32,256]{3,2,1,0:T(8,128)} %refs_7_.1) | copy-start | bytes 589828
  121.1 13.1 %collective-permute-start.10 = (bf16[3,2,3,32,256]{4,3,2,1,0:T(8,128)(2,1)}, bf16[3,2,3,32,256]{4,3,2,1,0:T(8,128)(2,1)S(1)}, u32[]{:S(2)}, u32[]{:S(2)}) collective-permute-start(bf16[3,2,3,32,256]{4,3,2,1,0:T(8,128)(2,1)} %get-tuple-element.38), channel_id=1, source_target_pairs={{0,8},{2,10},{4,12},{6,14},{8,0},{10,2},{12,4},{14,6},{1,9},{3,11}... | collective-permute-start | bytes 884744 | tf_op jit(solution)/shard_map/ppermute | solution.py:438
  126.5 13.0 %collective-permute-start.11 = (bf16[3,2,3,32,256]{4,3,2,1,0:T(8,128)(2,1)}, bf16[3,2,3,32,256]{4,3,2,1,0:T(8,128)(2,1)S(1)}, u32[]{:S(2)}, u32[]{:S(2)}) collective-permute-start(bf16[3,2,3,32,256]{4,3,2,1,0:T(8,128)(2,1)} %get-tuple-element.39), channel_id=1, source_target_pairs={{0,10},{2,8},{4,14},{6,12},{8,2},{10,0},{12,6},{14,4},{1,11},{3,9}... | collective-permute-start | bytes 884744 | tf_op jit(solution)/shard_map/ppermute | solution.py:438
  148.8 5.7 %collective-permute-start.12 = (bf16[3,3,32,128]{3,2,1,0:T(8,128)(2,1)S(1)}, bf16[3,3,32,128]{3,2,1,0:T(8,128)(2,1)S(1)}, u32[]{:S(2)}, u32[]{:S(2)}) collective-permute-start(bf16[3,3,32,128]{3,2,1,0:T(8,128)(2,1)S(1)} %get-tuple-element.42), channel_id=1, source_target_pairs={{0,2},{2,4},{4,6},{6,8},{8,10},{10,12},{12,14},{1,3},{3,5},{5,7},{... | collective-permute-start | bytes 221192 | tf_op jit(solution)/shard_map/ppermute | solution.py:401
  150.7 5.6 %collective-permute-start.13 = (bf16[3,3,32,128]{3,2,1,0:T(8,128)(2,1)S(1)}, bf16[3,3,32,128]{3,2,1,0:T(8,128)(2,1)S(1)}, u32[]{:S(2)}, u32[]{:S(2)}) collective-permute-start(bf16[3,3,32,128]{3,2,1,0:T(8,128)(2,1)S(1)} %get-tuple-element.43), channel_id=1, source_target_pairs={{2,0},{4,2},{6,4},{8,6},{10,8},{12,10},{14,12},{3,1},{5,3},{7,5},{... | collective-permute-start | bytes 221192 | tf_op jit(solution)/shard_map/ppermute | solution.py:402
  156.3 23.6 %collective-permute-start.14 = (bf16[3,3,32,384]{3,2,1,0:T(8,128)(2,1)S(1)}, bf16[3,3,32,384]{3,2,1,0:T(8,128)(2,1)S(1)}, u32[]{:S(2)}, u32[]{:S(2)}) collective-permute-start(bf16[3,3,32,384]{3,2,1,0:T(8,128)(2,1)S(1)} %get-tuple-element.44.refs_2_), channel_id=1, source_target_pairs={{0,1},{1,0},{2,3},{3,2},{4,5},{5,4},{6,7},{7,6},{8,9},{9,8},{10,11... | collective-permute-start | bytes 663560 | tf_op jit(solution)/shard_map/ppermute | solution.py:461
  160.0 7.1 %collective-permute-start.15 = (bf16[3,3,8,384]{3,2,1,0:T(8,128)(2,1)S(1)}, bf16[3,3,8,384]{3,2,1,0:T(8,128)(2,1)S(1)}, u32[]{:S(2)}, u32[]{:S(2)}) collective-permute-start(bf16[3,3,8,384]{3,2,1,0:T(8,128)(2,1)S(1)} %get-tuple-element.45), channel_id=1, source_target_pairs={{16,0},{32,16},{48,32},{64,48},{80,64},{96,80},{112,96},{128,112},... | collective-permute-start | bytes 165896 | tf_op jit(solution)/shard_map/ppermute | solution.py:402
  164.2 9.7 %collective-permute-start.16 = (bf16[3,3,8,384]{3,2,1,0:T(8,128)(2,1)S(1)}, bf16[3,3,8,384]{3,2,1,0:T(8,128)(2,1)S(1)}, u32[]{:S(2)}, u32[]{:S(2)}) collective-permute-start(bf16[3,3,8,384]{3,2,1,0:T(8,128)(2,1)S(1)} %get-tuple-element.46), channel_id=1, source_target_pairs={{0,16},{16,32},{32,48},{48,64},{64,80},{80,96},{96,112},{112,128},... | collective-permute-start | bytes 165896 | tf_op jit(solution)/shard_map/ppermute | solution.py:401
  173.9 6.0 %collective-permute-start.17 = (bf16[3,3,8,384]{3,2,1,0:T(8,128)(2,1)S(1)}, bf16[3,3,8,384]{3,2,1,0:T(8,128)(2,1)S(1)}, u32[]{:S(2)}, u32[]{:S(2)}) collective-permute-start(bf16[3,3,8,384]{3,2,1,0:T(8,128)(2,1)S(1)} %ring.1.refs_4_), channel_id=1, source_target_pairs={{0,1},{1,0},{2,3},{3,2},{4,5},{5,4},{6,7},{7,6},{8,9},{9,8},{10,11... | collective-permute-start | bytes 165896 | tf_op jit(solution)/shard_map/ppermute | solution.py:470
  (10 other events, 78.5 us)
Sparse Core Ops, SparseCore 0:
  9.5 50.5 all-gather.3
  68.2 30.5 all-gather.5

commit v4 on v3

--- a/solution.py
+++ b/solution.py
@@ -35,49 +35,48 @@
     )(*arrays, *settled)
 
 
-def slices_kernel(_, column_ref, row_ref, out_ref):
+def slices_kernel(which_ref, column_ref, row_ref, out_ref):
+    peers, height, wide = out_ref.shape
     tall = column_ref.shape[0]
-    half = row_ref.shape[0] // 2
-    wide = row_ref.shape[1]
-    peers = out_ref.shape[0]
+    narrow = row_ref.shape[1] // 2
     out_ref[:, :tall, :] = jnp.broadcast_to(column_ref[...][None], (peers, *column_ref.shape))
-    upper, lower = (row_ref[:half, :], row_ref[half:, :])
-    out_ref[:, tall:, :wide] = jnp.broadcast_to(upper[None], (peers, half, wide))
-    out_ref[:, tall:, wide:] = jnp.broadcast_to(lower[None], (peers, half, wide))
-
-
-def taper_slices(at, column_taper, row_taper, peers, parts):
+    mine = row_ref[...].astype(F32)
+    mine = jnp.where(which_ref[1] == 1, mine[:, narrow:], mine[:, :narrow]).astype(BF)
+    pieces = [mine[8 * i : 8 * i + 8] for i in range(wide // narrow)]
+    slab = jnp.concatenate(pieces, axis=1)
+    out_ref[:, tall:, :] = jnp.broadcast_to(slab[None], (peers, *slab.shape))
+
+
+def taper_slices(which, column_taper, row_taper, peers, parts):
     tall, wide = (column_taper.shape[0], column_taper.shape[1] // parts)
     rows, narrow = (row_taper.shape[0], row_taper.shape[1] // parts)
+    shape = (peers, tall + rows * narrow // 2 // wide, wide)
     return pl.pallas_call(
         slices_kernel,
-        out_shape=shaped((peers, tall + rows // 2, wide), BF),
+        out_shape=shaped(shape, BF),
         grid_spec=pltpu.PrefetchScalarGridSpec(
             num_scalar_prefetch=1,
             grid=(1,),
             in_specs=[
-                pl.BlockSpec((tall, wide), lambda i, at: (0, at[0])),
-                pl.BlockSpec((rows, narrow), lambda i, at: (0, at[0])),
+                pl.BlockSpec((tall, wide), lambda i, which: (0, which[0])),
+                pl.BlockSpec((rows, narrow), lambda i, which: (0, which[0])),
             ],
-            out_specs=pl.BlockSpec((peers, tall + rows // 2, wide), lambda i, at: (0, 0, 0)),
+            out_specs=pl.BlockSpec(shape, lambda i, which: (0, 0, 0)),
         ),
         compiler_params=room(6),
         name="taper_slices",
-    )(at, in_hbm(column_taper), in_hbm(row_taper))
-
-
-def row_part_kernel(tall, slices_ref, out_ref):
-    half = slices_ref.shape[1] - tall
-    wide = out_ref.shape[2]
-    out_ref[:, :half, :] = slices_ref[:, tall:, :wide]
-    out_ref[:, half:, :] = slices_ref[:, tall:, wide:]
+    )(which, in_hbm(column_taper), in_hbm(row_taper))
 
 
 def row_part(slices, tall, settled):
     peers, height, wide = slices.shape
-    return pl.pallas_call(
-        lambda a, *rest: row_part_kernel(tall, a, rest[-1]),
-        out_shape=shaped((peers, 2 * (height - tall), wide // 2), BF),
+
+    def kernel(slices_ref, *refs):
+        refs[-1][...] = slices_ref[:, tall:, :]
+
+    return pl.pallas_call(
+        kernel,
+        out_shape=shaped((peers, height - tall, wide), BF),
         in_specs=[pl.BlockSpec(memory_space=pltpu.VMEM)]
         + [pl.BlockSpec(memory_space=pl.ANY)] * len(settled),
         compiler_params=room(4),
@@ -85,10 +84,17 @@
     )(slices, *settled)
 
 
-def columns_kernel(tall, fields_ref, slices_ref, out_ref):
+def columns_kernel(tall, *refs):
+    slices_ref, out_ref = refs[-2:]
     units, levels, rows, wide = out_ref.shape
-    taper = slices_ref[:, :tall, :].reshape(-1, slices_ref.shape[2])
-    product = jnp.dot(fields_ref[...], taper, preferred_element_type=F32).astype(BF)
+    product = None
+    for i, fields_ref in enumerate(refs[:-2]):
+        depth = fields_ref.shape[1]
+        count = depth // tall
+        taper = slices_ref[i * count : (i + 1) * count, :tall, :].reshape(depth, 2 * wide)
+        part = jnp.dot(fields_ref[...], taper, preferred_element_type=F32)
+        product = part if product is None else product + part
+    product = product.astype(BF)
     for member in range(units // 2):
         for side in range(2):
             part = product[
@@ -98,41 +104,78 @@
             out_ref[member * 2 + side] = part.reshape(levels, rows, wide)
 
 
-def columns_pass(fields, slices, tall, levels, rows, parts):
+def columns_pass(fields, slices, tall, levels, rows, blocks, streams):
     count, depth = fields.shape
     peers, height, wide = slices.shape
     units = 2 * count // (levels * rows)
-    return pl.pallas_call(
-        lambda a, b, c: columns_kernel(tall, a, b, c),
+    fields = in_hbm(fields)
+
+    def stream(j):
+        return pl.BlockSpec((count // blocks, depth // streams), lambda i: (i, j))
+
+    return pl.pallas_call(
+        lambda *refs: columns_kernel(tall, *refs),
         out_shape=shaped((units, levels, rows, wide // 2), BF),
-        grid=(parts,),
-        in_specs=[
-            pl.BlockSpec((count // parts, depth), lambda i: (i, 0)),
-            pl.BlockSpec((peers, height, wide), lambda i: (0, 0, 0)),
-        ],
-        out_specs=pl.BlockSpec((units // parts, levels, rows, wide // 2), lambda i: (i, 0, 0, 0)),
+        grid=(blocks,),
+        in_specs=[stream(j) for j in range(streams)]
+        + [pl.BlockSpec((peers, height, wide), lambda i: (0, 0, 0))],
+        out_specs=pl.BlockSpec((units // blocks, levels, rows, wide // 2), lambda i: (i, 0, 0, 0)),
         compiler_params=room(14),
         name="columns_pass",
-    )(in_hbm(fields), slices)
-
-
-def join_kernel(parts_ref, out_ref):
-    for i in range(parts_ref.shape[0]):
-        wide = parts_ref.shape[2]
-        out_ref[:, i * wide : (i + 1) * wide] = parts_ref[i]
-
-
-def joined(taper, blocks):
-    parts, height, narrow = taper.shape
-    return pl.pallas_call(
+    )(*[fields] * streams, slices)
+
+
+def pair_kernel(own_ref, other_ref, _, out_ref):
+    out_ref[0] = own_ref[...]
+    out_ref[1] = other_ref[...]
+
+
+def paired(own, other, settled):
+    whole = pl.BlockSpec(own.shape, lambda i: (0, 0, 0))
+    return pl.pallas_call(
+        pair_kernel,
+        out_shape=shaped((2, *own.shape), own.dtype),
+        grid=(1,),
+        in_specs=[whole, whole, pl.BlockSpec(memory_space=pl.ANY)],
+        out_specs=pl.BlockSpec((2, *own.shape), lambda i: (0, 0, 0, 0)),
+        compiler_params=room(4),
+        name="paired",
+    )(own, other, settled)
+
+
+def join_kernel(flip_ref, parts_ref, out_ref):
+    parts, _, count, tall, wide = parts_ref.shape
+    pieces = out_ref.shape[1] // tall
+    narrow = wide // pieces
+    for part in range(parts):
+        for j in range(count):
+            pair = [parts_ref[part, k ^ flip_ref[0], j].astype(F32) for k in range(2)]
+            for i in range(pieces):
+                lanes = slice(i * narrow, (i + 1) * narrow)
+                both = jnp.concatenate([x[:, lanes] for x in pair], axis=1)
+                at = slice(part * 2 * narrow, (part + 1) * 2 * narrow)
+                out_ref[j, i * tall : (i + 1) * tall, at] = both.astype(BF)
+
+
+def joined(flip, taper, rows, blocks):
+    parts, _, peers, tall, wide = taper.shape
+    across = 2 * parts * tall * wide // rows
+    count = peers // blocks
+    whole = pl.pallas_call(
         join_kernel,
-        out_shape=shaped((height, parts * narrow), BF),
-        grid=(blocks,),
-        in_specs=[pl.BlockSpec((parts, height // blocks, narrow), lambda i: (0, i, 0))],
-        out_specs=pl.BlockSpec((height // blocks, parts * narrow), lambda i: (i, 0)),
+        out_shape=shaped((peers, rows, across), BF),
+        grid_spec=pltpu.PrefetchScalarGridSpec(
+            num_scalar_prefetch=1,
+            grid=(blocks,),
+            in_specs=[
+                pl.BlockSpec((parts, 2, count, tall, wide), lambda i, flip: (0, 0, i, 0, 0))
+            ],
+            out_specs=pl.BlockSpec((count, rows, across), lambda i, flip: (i, 0, 0)),
+        ),
         compiler_params=room(6),
         name="joined",
-    )(in_hbm(taper))
+    )(flip, in_hbm(taper))
+    return whole.reshape(peers * rows, across)
 
 
 def rows_kernel(taper_ref, fields_ref, *refs):
@@ -234,55 +277,59 @@
     return jnp.where(row < STEPS, from_next, from_previous)
 
 
-def widen_kernel(body_ref, left_ref, right_ref, out_ref, top_ref, bottom_ref):
+def edges_kernel(body_ref, left_ref, right_ref, sides_ref, top_ref, bottom_ref):
     variables, levels, rows, wide = body_ref.shape
     for k in range(variables):
         for level in range(levels):
-            out_ref[k, level, :, :wide] = body_ref[k, level]
             sides = beside(left_ref[k, level].astype(F32), right_ref[k, level].astype(F32))
-            out_ref[k, level, :, wide:] = sides.astype(BF)
-            top_ref[k, level] = out_ref[k, level, :8]
-            bottom_ref[k, level] = out_ref[k, level, rows - 8 :]
-
-
-def widened(body, left, right):
+            sides_ref[k, level] = sides.astype(BF)
+            for at, out_ref in ((slice(0, 8), top_ref), (slice(rows - 8, rows), bottom_ref)):
+                out_ref[k, level, :, :wide] = body_ref[k, level, at]
+                out_ref[k, level, :, wide:] = sides_ref[k, level, at]
+
+
+def edges(body, left, right):
     variables, levels, rows, wide = body.shape
-    full = wide + left.shape[-1]
-    strip = shaped((variables, levels, 8, full), BF)
-    return pl.pallas_call(
-        widen_kernel,
-        out_shape=[shaped((variables, levels, rows, full), BF), strip, strip],
+    strip = shaped((variables, levels, 8, wide + left.shape[-1]), BF)
+    return pl.pallas_call(
+        edges_kernel,
+        out_shape=[shaped(left.shape, BF), strip, strip],
         compiler_params=room(4),
-        name="widened",
+        name="edges",
     )(body, left, right)
 
 
-def ring_kernel(next_ref, previous_ref, out_ref):
-    for k in range(out_ref.shape[0]):
-        for level in range(out_ref.shape[1]):
-            rows = above_below(
+def frame_kernel(sides_ref, next_ref, previous_ref, out_ref):
+    variables, levels, rows, wide = sides_ref.shape
+    for k in range(variables):
+        for level in range(levels):
+            out_ref[k, level, :rows] = sides_ref[k, level]
+            around = above_below(
                 next_ref[k, level].astype(F32), previous_ref[k, level].astype(F32)
-            )
-            out_ref[k, level] = rows.astype(BF)
-
-
-def ring(from_next, from_previous):
-    return pl.pallas_call(
-        ring_kernel,
-        out_shape=shaped(from_next.shape, BF),
+            ).astype(BF)
+            for i in range(around.shape[1] // wide):
+                at = rows + 8 * i
+                out_ref[k, level, at : at + 8] = around[:, i * wide : (i + 1) * wide]
+
+
+def frame(sides, from_next, from_previous):
+    variables, levels, rows, wide = sides.shape
+    tall = rows + 8 * (from_next.shape[-1] // wide)
+    return pl.pallas_call(
+        frame_kernel,
+        out_shape=shaped((variables, levels, tall, wide), BF),
         compiler_params=room(4),
-        name="ring",
-    )(from_next, from_previous)
+        name="frame",
+    )(sides, from_next, from_previous)
 
 
 def advect_kernel(*refs):
     (
         flip_ref,
         own_ref,
-        wider_ref,
         other_ref,
-        ring_ref,
-        other_ring_ref,
+        frame_ref,
+        other_frame_ref,
         courant_ref,
         slope_ref,
         beside_ref,
@@ -310,12 +357,14 @@
         at = local(level % levels)
         mine = level < levels
         for k in range(variables):
-            if mine:
-                first_ref[k, level, :rows, wide:] = wider_ref[k, at, :, wide:].astype(F32)
-            else:
-                first_ref[k, level, :rows, :] = other_ref[k, at].astype(F32)
-            strip_ref = ring_ref if mine else other_ring_ref
-            first_ref[k, level, rows:, :] = strip_ref[k, at].astype(F32)
+            around_of = frame_ref if mine else other_frame_ref
+            if not mine:
+                first_ref[k, level, :rows, :wide] = other_ref[k, at].astype(F32)
+            first_ref[k, level, :rows, wide:] = around_of[k, at, :rows].astype(F32)
+            for i in range(full // (full - wide)):
+                lanes = slice(i * (full - wide), (i + 1) * (full - wide))
+                strip = around_of[k, at, rows + 8 * i : rows + 8 * (i + 1)]
+                first_ref[k, level, rows:, lanes] = strip.astype(F32)
         planes = []
         for a in range(directions + slope_ref.shape[0]):
             if mine:
@@ -367,7 +416,7 @@
 
 def advect(flip, *arrays):
     variables, levels, rows, wide = arrays[0].shape
-    tall, full = (rows + 8, arrays[2].shape[-1])
+    tall, full = (rows + 8, wide + arrays[2].shape[-1])
     vmem = pl.BlockSpec(memory_space=pltpu.VMEM)
     state = pltpu.VMEM((variables, 2 * levels, tall, full), F32)
     return pl.pallas_call(
@@ -426,7 +475,7 @@
         control_fields.reshape(members * levels * rows, columns), "mem", axis=0, tiled=True
     )
     slices = lax.all_to_all(
-        taper_slices(at, column_taper, row_taper, peers, parts), "row", 0, 0, tiled=True
+        taper_slices(jnp.concatenate([at, flip]), column_taper, row_taper, peers, parts), "row", 0, 0, tiled=True
     )
     sides, around, taller = background(courant_numbers, tracer_slope)
     pieces = split_columns(at, perturbations, parts)
@@ -445,29 +494,30 @@
     settled = [*exchange((1,)), taller]
     (taller,) = after([taller], [slices])
     opposite = lax.ppermute(taller, "lev", swap("lev"))
-    first_pass = columns_pass(every, slices, tall, levels, rows, 2)
-    row_whole = lax.all_gather(row_part(slices, tall, settled), "mem", axis=0, tiled=False)
-    row_whole = row_whole.reshape(parts, row_taper.shape[1], -1)
-    hold((2, 3, 6, 7), [first_pass])
+    first_pass = columns_pass(every, slices, tall, levels, rows, 2, 1)
+    half = row_part(slices, tall, settled)
+    both = paired(half, lax.ppermute(half, "lev", swap("lev")), first_pass)
+    (first_pass,) = after([first_pass], [both])
+    row_whole = lax.all_gather(both, "mem", axis=0, tiled=False)
+    hold((2, 3, 6), [first_pass])
     arrived = lax.all_to_all(first_pass, "row", 0, 0, tiled=True)
-    tapered = rows_pass(joined(row_whole, 4), arrived, [*exchange((2, 3, 6, 7)), opposite])
-    hold((4, 5), [tapered])
+    tapered = rows_pass(joined(flip, row_whole, row_taper.shape[0], 4), arrived, [*exchange((2, 3, 6)), opposite])
+    hold((4, 5, 7), [tapered])
     localized = lax.all_to_all(tapered, "row", 0, 0, tiled=True)
-    exchange((4, 5))
+    exchange((4, 5, 7))
     weights = [weights[step] for step in range(parts)]
     own, rounded, first, last = weighted_sum(at, localized, weights)
 
-    wider, top, bottom = widened(rounded, *neighbours(first, last, "mem"))
-    other = lax.ppermute(wider, "lev", swap("lev"))
+    other = lax.ppermute(rounded, "lev", swap("lev"))
+    outside, top, bottom = edges(rounded, *neighbours(first, last, "mem"))
     from_previous, from_next = neighbours(top, bottom, "row")
-    rows_around = ring(from_next, from_previous)
+    framed = frame(outside, from_next, from_previous)
     return advect(
         flip,
         own,
-        wider,
         other,
-        rows_around,
-        lax.ppermute(rows_around, "lev", swap("lev")),
+        framed,
+        lax.ppermute(framed, "lev", swap("lev")),
         courant_numbers,
         tracer_slope,
         sides,

time: 191 us -> 189 us (0.990)
  the two profiles are of different devices: /device:TPU:66 before, /device:TPU:68 now
where the time goes in v4:
time: 189 us; the launch traced here: 188 us
  starting transfers between devices  92.6 us (49%)
  waiting for transfers between devices  57.2 us (30%)
  Pallas kernels  17.5 us (9%)
  between operations  13.9 us (7%)
  local copies, waits for them, and re-layouts  4.64 us (2%)
  other arithmetic  2.22 us (1%)
    ppermute x7, starting transfers between devices, exchange(): weights[step] = lax.ppermute(weights[step], 'mem', pairs)  18.7 us
    ppermute x4, waiting for transfers between devices, neighbours(): from_left = lax.ppermute(last, axis, chain(axis, 1))  17.7 us
    ppermute x4, starting transfers between devices, neighbours(): from_right = lax.ppermute(first, axis, chain(axis, -1))  16.9 us
    all_to_all x1, starting transfers between devices, on_device(): lax.all_to_all(taper_slices(jnp.concatenate([at, flip]), column_taper, ro...  15.5 us
    ppermute x7, waiting for transfers between devices, exchange(): weights[step] = lax.ppermute(weights[step], 'mem', pairs)  14.7 us
    all_gather x1, waiting for transfers between devices, on_device(): row_whole = lax.all_gather(both, 'mem', axis=0, tiled=False)  13.3 us
    all_to_all x1, starting transfers between devices, on_device(): localized = lax.all_to_all(tapered, 'row', 0, 0, tiled=True)  12.2 us
    ppermute x4, starting transfers between devices, neighbours(): from_left = lax.ppermute(last, axis, chain(axis, 1))  10 us
  transfers between devices with their start and end apart: 24, of which 13 were waited for; matrix products, arithmetic and copies ran while one was open for 1% of the time, Pallas kernels for 5%

profile of v4, /device:TPU:68, one launch (start us, length us, event | category | flops | bytes accessed | tf_op | source)
XLA Modules:
  0.0 188.2 jit_solution(12696750324384159673)
XLA Ops:
  7.3 2.5 %taper_slices.1 = bf16[32,72,256]{2,1,0:T(8,128)(2,1)} custom-call(s32[2]{0:T(128)S(1)} %pad_add_fusion.which_ref, bf16[64,2048]{1,0:T(8,128)(2,1)} %column_ref.1, bf16[32,1024]{1,0:T(8,128)(2,1)} %row_ref.1), custom_call_target="tpu_custom_call" | custom-call | tf_op jit(solution)/shard_map/taper_slices/pallas_call | solution.py:54
  9.8 15.5 %all-to-all-start = ((bf16[32,72,256]{2,1,0:T(8,128)(2,1)}), bf16[32,72,256]{2,1,0:T(8,128)(2,1)S(1)}, u32[]{:S(2)}, u32[]{:S(2)}) async-start(bf16[32,72,256]{2,1,0:T(8,128)(2,1)} %taper_slices.1), calls=%async_computation | async-start | bytes 2359296 | tf_op jit(solution)/shard_map/all_to_all | solution.py:477
  27.4 1.9 %collective-permute-start.2 = (bf16[5,3,32,128]{3,2,1,0:T(8,128)(2,1)S(1)}, bf16[5,3,32,128]{3,2,1,0:T(8,128)(2,1)S(1)}, u32[]{:S(2)}, u32[]{:S(2)}) collective-permute-start(bf16[5,3,32,128]{3,2,1,0:T(8,128)(2,1)S(1)} %get-tuple-element.49), channel_id=1, source_target_pairs={{0,2},{2,4},{4,6},{6,8},{8,10},{10,12},{12,14},{1,3},{3,5},{5,7},{... | collective-permute-start | bytes 368648 | tf_op jit(solution)/shard_map/ppermute | solution.py:450
  29.3 3.6 %collective-permute-start.1 = (bf16[5,3,32,128]{3,2,1,0:T(8,128)(2,1)S(1)}, bf16[5,3,32,128]{3,2,1,0:T(8,128)(2,1)S(1)}, u32[]{:S(2)}, u32[]{:S(2)}) collective-permute-start(bf16[5,3,32,128]{3,2,1,0:T(8,128)(2,1)S(1)} %get-tuple-element.50), channel_id=1, source_target_pairs={{2,0},{4,2},{6,4},{8,6},{10,8},{12,10},{14,12},{3,1},{5,3},{7,5},{... | collective-permute-start | bytes 368648 | tf_op jit(solution)/shard_map/ppermute | solution.py:451
  38.2 4.3 %collective-permute-start.4 = (bf16[5,3,8,384]{3,2,1,0:T(8,128)(2,1)S(1)}, bf16[5,3,8,384]{3,2,1,0:T(8,128)(2,1)S(1)}, u32[]{:S(2)}, u32[]{:S(2)}) collective-permute-start(bf16[5,3,8,384]{3,2,1,0:T(8,128)(2,1)S(1)} %get-tuple-element.47), channel_id=1, source_target_pairs={{0,16},{16,32},{32,48},{48,64},{64,80},{80,96},{96,112},{112,128},... | collective-permute-start | bytes 276488 | tf_op jit(solution)/shard_map/ppermute | solution.py:450
  42.5 4.6 %collective-permute-start.3 = (bf16[5,3,8,384]{3,2,1,0:T(8,128)(2,1)S(1)}, bf16[5,3,8,384]{3,2,1,0:T(8,128)(2,1)S(1)}, u32[]{:S(2)}, u32[]{:S(2)}) collective-permute-start(bf16[5,3,8,384]{3,2,1,0:T(8,128)(2,1)S(1)} %get-tuple-element.48), channel_id=1, source_target_pairs={{16,0},{32,16},{48,32},{64,48},{80,64},{96,80},{112,96},{128,112},... | collective-permute-start | bytes 276488 | tf_op jit(solution)/shard_map/ppermute | solution.py:451
  47.1 12.3 %collective-permute-done.4 = bf16[5,3,8,384]{3,2,1,0:T(8,128)(2,1)S(1)} collective-permute-done((bf16[5,3,8,384]{3,2,1,0:T(8,128)(2,1)S(1)}, bf16[5,3,8,384]{3,2,1,0:T(8,128)(2,1)S(1)}, u32[]{:S(2)}, u32[]{:S(2)}) %collective-permute-start.4) | collective-permute-done | bytes 92192 | tf_op jit(solution)/shard_map/ppermute | solution.py:450
  59.6 2.9 %all-to-all-done.slices_ref.refs_1_ = bf16[32,72,256]{2,1,0:T(8,128)(2,1)S(1)} async-done(((bf16[32,72,256]{2,1,0:T(8,128)(2,1)}), bf16[32,72,256]{2,1,0:T(8,128)(2,1)S(1)}, u32[]{:S(2)}, u32[]{:S(2)}) %all-to-all-start) | async-done | bytes 1179680 | tf_op jit(solution)/shard_map/all_to_all | solution.py:477
  62.6 1.9 %collective-permute-start.5 = (bf16[32,8,256]{2,1,0:T(8,128)(2,1)S(1)}, bf16[32,8,256]{2,1,0:T(8,128)(2,1)S(1)}, u32[]{:S(2)}, u32[]{:S(2)}) collective-permute-start(bf16[32,8,256]{2,1,0:T(8,128)(2,1)S(1)} %row_part.1.own_ref), channel_id=1, source_target_pairs={{0,1},{1,0},{2,3},{3,2},{4,5},{5,4},{6,7},{7,6},{8,9},{9,8},{10,11... | collective-permute-start | bytes 393224 | tf_op jit(solution)/shard_map/ppermute | solution.py:499
  64.5 3.9 %columns_pass.1._.refs_0_ = bf16[32,3,32,128]{3,2,1,0:T(8,128)(2,1)S(1)} custom-call(bf16[1536,2048]{1,0:T(8,128)(2,1)} %all-gather.4.cloned.1.call-done.refs_0_, bf16[32,72,256]{2,1,0:T(8,128)(2,1)S(1)} %all-to-all-done.slices_ref.refs_1_), custom_call_target="tpu_custom_call" | custom-call | tf_op jit(solution)/shard_map/columns_pass/pallas_call | solution.py:116
  70.2 7.8 %all-to-all-start.1 = ((bf16[32,3,32,128]{3,2,1,0:T(8,128)(2,1)}), bf16[32,3,32,128]{3,2,1,0:T(8,128)(2,1)S(1)}, u32[]{:S(2)}, u32[]{:S(2)}) async-start(bf16[32,3,32,128]{3,2,1,0:T(8,128)(2,1)} %after.4.refs_3_), calls=%async_computation.1 | async-start | bytes 1572864 | tf_op jit(solution)/shard_map/all_to_all | solution.py:503
  78.1 3.2 %collective-permute-start.9 = (bf16[5,3,40,384]{3,2,1,0:T(8,128)(2,1)}, bf16[5,3,40,384]{3,2,1,0:T(8,128)(2,1)S(1)}, u32[]{:S(2)}, u32[]{:S(2)}) collective-permute-start(bf16[5,3,40,384]{3,2,1,0:T(8,128)(2,1)} %after.6), channel_id=1, source_target_pairs={{0,1},{1,0},{2,3},{3,2},{4,5},{5,4},{6,7},{7,6},{8,9},{9,8},{10,11... | collective-permute-start | bytes 1382408 | tf_op jit(solution)/shard_map/ppermute | solution.py:496
  81.2 3.0 %collective-permute-start.6 = (bf16[3,2,3,32,256]{4,3,2,1,0:T(8,128)(2,1)}, bf16[3,2,3,32,256]{4,3,2,1,0:T(8,128)(2,1)}, u32[]{:S(2)}, u32[]{:S(2)}) collective-permute-start(bf16[3,2,3,32,256]{4,3,2,1,0:T(8,128)(2,1)} %get-tuple-element.30), channel_id=1, source_target_pairs={{0,4},{2,6},{4,0},{6,2},{8,12},{10,14},{12,8},{14,10},{1,5},{3,7},... | collective-permute-start | bytes 884744 | tf_op jit(solution)/shard_map/ppermute | solution.py:487
  84.3 1.9 %collective-permute-start.7 = (bf16[3,2,3,32,256]{4,3,2,1,0:T(8,128)(2,1)}, bf16[3,2,3,32,256]{4,3,2,1,0:T(8,128)(2,1)}, u32[]{:S(2)}, u32[]{:S(2)}) collective-permute-start(bf16[3,2,3,32,256]{4,3,2,1,0:T(8,128)(2,1)} %get-tuple-element.31), channel_id=1, source_target_pairs={{0,6},{2,4},{4,2},{6,0},{8,14},{10,12},{12,10},{14,8},{1,7},{3,5},... | collective-permute-start | bytes 884744 | tf_op jit(solution)/shard_map/ppermute | solution.py:487
  86.2 1.9 %collective-permute-start.8 = (bf16[3,2,3,32,256]{4,3,2,1,0:T(8,128)(2,1)}, bf16[3,2,3,32,256]{4,3,2,1,0:T(8,128)(2,1)}, u32[]{:S(2)}, u32[]{:S(2)}) collective-permute-start(bf16[3,2,3,32,256]{4,3,2,1,0:T(8,128)(2,1)} %get-tuple-element.32), channel_id=1, source_target_pairs={{0,12},{2,14},{4,8},{6,10},{8,4},{10,6},{12,0},{14,2},{1,13},{3,15... | collective-permute-start | bytes 884744 | tf_op jit(solution)/shard_map/ppermute | solution.py:487
  88.1 13.3 %all-gather.6.cloned.1.call-done = bf16[16,32,8,256]{3,2,1,0:T(8,128)(2,1)} async-done(((bf16[2,32,8,256]{3,2,1,0:T(8,128)(2,1)}), bf16[16,32,8,256]{3,2,1,0:T(8,128)(2,1)}) %all-gather.6.cloned.1.call-update) | async-done | bytes 2097168 | tf_op jit(solution)/shard_map/all_gather | solution.py:501
  101.5 2.9 %joined.1 = bf16[32,32,1024]{2,1,0:T(8,128)(2,1)S(1)} custom-call(s32[1]{0:T(128)} %bitcast.flip_ref.refs_0_, bf16[8,2,32,8,256]{4,3,2,1,0:T(8,128)(2,1)} %bitcast.6), custom_call_target="tpu_custom_call" | custom-call | tf_op jit(solution)/shard_map/joined/pallas_call | solution.py:164
  105.5 2.2 %rows_pass.1.refs_3_ = bf16[32,3,32,128]{3,2,1,0:T(8,128)(2,1)} custom-call(bf16[1024,1024]{1,0:T(8,128)(2,1)S(1)} %bitcast.5, bf16[32,3,32,128]{3,2,1,0:T(8,128)(2,1)S(1)} %all-to-all-done.1.fields_ref, bf16[3,2,3,32,256]{4,3,2,1,0:T(8,128)(2,1)} %collective-permute-done.6.refs_0_.refs_4_, ...), custom_call_target="tpu_custom_call" | custom-call | tf_op jit(solution)/shard_map/rows_pass/pallas_call | solution.py:196
  107.7 12.2 %all-to-all-start.2 = ((bf16[32,3,32,128]{3,2,1,0:T(8,128)(2,1)}), bf16[32,3,32,128]{3,2,1,0:T(8,128)(2,1)S(1)}, u32[]{:S(2)}, u32[]{:S(2)}) async-start(bf16[32,3,32,128]{3,2,1,0:T(8,128)(2,1)} %rows_pass.1.refs_3_), calls=%async_computation.2 | async-start | bytes 1572864 | tf_op jit(solution)/shard_map/all_to_all | solution.py:506
  120.0 2.9 %collective-permute-start.10 = (bf16[3,2,3,32,256]{4,3,2,1,0:T(8,128)(2,1)}, bf16[3,2,3,32,256]{4,3,2,1,0:T(8,128)(2,1)S(1)}, u32[]{:S(2)}, u32[]{:S(2)}) collective-permute-start(bf16[3,2,3,32,256]{4,3,2,1,0:T(8,128)(2,1)} %get-tuple-element.37), channel_id=1, source_target_pairs={{0,8},{2,10},{4,12},{6,14},{8,0},{10,2},{12,4},{14,6},{1,9},{3,11}... | collective-permute-start | bytes 884744 | tf_op jit(solution)/shard_map/ppermute | solution.py:487
  122.9 3.4 %collective-permute-start.11 = (bf16[3,2,3,32,256]{4,3,2,1,0:T(8,128)(2,1)}, bf16[3,2,3,32,256]{4,3,2,1,0:T(8,128)(2,1)S(1)}, u32[]{:S(2)}, u32[]{:S(2)}) collective-permute-start(bf16[3,2,3,32,256]{4,3,2,1,0:T(8,128)(2,1)} %get-tuple-element.38), channel_id=1, source_target_pairs={{0,10},{2,8},{4,14},{6,12},{8,2},{10,0},{12,6},{14,4},{1,11},{3,9}... | collective-permute-start | bytes 884744 | tf_op jit(solution)/shard_map/ppermute | solution.py:487
  126.3 3.7 %collective-permute-start.12 = (bf16[3,2,3,32,256]{4,3,2,1,0:T(8,128)(2,1)}, bf16[3,2,3,32,256]{4,3,2,1,0:T(8,128)(2,1)S(1)}, u32[]{:S(2)}, u32[]{:S(2)}) collective-permute-start(bf16[3,2,3,32,256]{4,3,2,1,0:T(8,128)(2,1)} %get-tuple-element.39), channel_id=1, source_target_pairs={{0,14},{2,12},{4,10},{6,8},{8,6},{10,4},{12,2},{14,0},{1,15},{3,13... | collective-permute-start | bytes 884744 | tf_op jit(solution)/shard_map/ppermute | solution.py:487
  130.0 3.8 %collective-permute-done.10.refs_6_ = bf16[3,2,3,32,256]{4,3,2,1,0:T(8,128)(2,1)S(1)} collective-permute-done((bf16[3,2,3,32,256]{4,3,2,1,0:T(8,128)(2,1)}, bf16[3,2,3,32,256]{4,3,2,1,0:T(8,128)(2,1)S(1)}, u32[]{:S(2)}, u32[]{:S(2)}) %collective-permute-start.10) | collective-permute-done | bytes 294944 | tf_op jit(solution)/shard_map/ppermute | solution.py:487
  133.8 3.2 %collective-permute-done.11.refs_7_ = bf16[3,2,3,32,256]{4,3,2,1,0:T(8,128)(2,1)S(1)} collective-permute-done((bf16[3,2,3,32,256]{4,3,2,1,0:T(8,128)(2,1)}, bf16[3,2,3,32,256]{4,3,2,1,0:T(8,128)(2,1)S(1)}, u32[]{:S(2)}, u32[]{:S(2)}) %collective-permute-start.11) | collective-permute-done | bytes 294944 | tf_op jit(solution)/shard_map/ppermute | solution.py:487
  137.0 7.7 %collective-permute-done.12.refs_9_ = bf16[3,2,3,32,256]{4,3,2,1,0:T(8,128)(2,1)S(1)} collective-permute-done((bf16[3,2,3,32,256]{4,3,2,1,0:T(8,128)(2,1)}, bf16[3,2,3,32,256]{4,3,2,1,0:T(8,128)(2,1)S(1)}, u32[]{:S(2)}, u32[]{:S(2)}) %collective-permute-start.12) | collective-permute-done | bytes 294944 | tf_op jit(solution)/shard_map/ppermute | solution.py:487
  150.4 3.6 %collective-permute-start.15 = (bf16[3,3,32,128]{3,2,1,0:T(8,128)(2,1)S(1)}, bf16[3,3,32,128]{3,2,1,0:T(8,128)(2,1)S(1)}, u32[]{:S(2)}, u32[]{:S(2)}) collective-permute-start(bf16[3,3,32,128]{3,2,1,0:T(8,128)(2,1)S(1)} %get-tuple-element.43), channel_id=1, source_target_pairs={{2,0},{4,2},{6,4},{8,6},{10,8},{12,10},{14,12},{3,1},{5,3},{7,5},{... | collective-permute-start | bytes 221192 | tf_op jit(solution)/shard_map/ppermute | solution.py:451
  156.1 5.1 %collective-permute-start.16 = (bf16[3,3,8,384]{3,2,1,0:T(8,128)(2,1)S(1)}, bf16[3,3,8,384]{3,2,1,0:T(8,128)(2,1)S(1)}, u32[]{:S(2)}, u32[]{:S(2)}) collective-permute-start(bf16[3,3,8,384]{3,2,1,0:T(8,128)(2,1)S(1)} %get-tuple-element.45), channel_id=1, source_target_pairs={{16,0},{32,16},{48,32},{64,48},{80,64},{96,80},{112,96},{128,112},... | collective-permute-start | bytes 165896 | tf_op jit(solution)/shard_map/ppermute | solution.py:451
  163.1 2.7 %collective-permute-start.13 = (bf16[3,3,32,256]{3,2,1,0:T(8,128)(2,1)S(1)}, bf16[3,3,32,256]{3,2,1,0:T(8,128)(2,1)S(1)}, u32[]{:S(2)}, u32[]{:S(2)}) collective-permute-start(bf16[3,3,32,256]{3,2,1,0:T(8,128)(2,1)S(1)} %get-tuple-element.41.body_ref), channel_id=1, source_target_pairs={{0,1},{1,0},{2,3},{3,2},{4,5},{5,4},{6,7},{7,6},{8,9},{9,8},{10,11... | collective-permute-start | bytes 442376 | tf_op jit(solution)/shard_map/ppermute | solution.py:511
  165.7 5.2 %collective-permute-done.17.previous_ref = bf16[3,3,8,384]{3,2,1,0:T(8,128)(2,1)S(1)} collective-permute-done((bf16[3,3,8,384]{3,2,1,0:T(8,128)(2,1)S(1)}, bf16[3,3,8,384]{3,2,1,0:T(8,128)(2,1)S(1)}, u32[]{:S(2)}, u32[]{:S(2)}) %collective-permute-start.17) | collective-permute-done | bytes 55328 | tf_op jit(solution)/shard_map/ppermute | solution.py:450
  171.0 3.6 %collective-permute-start.18 = (bf16[3,3,56,128]{3,2,1,0:T(8,128)(2,1)S(1)}, bf16[3,3,56,128]{3,2,1,0:T(8,128)(2,1)S(1)}, u32[]{:S(2)}, u32[]{:S(2)}) collective-permute-start(bf16[3,3,56,128]{3,2,1,0:T(8,128)(2,1)S(1)} %frame.1.refs_3_), channel_id=1, source_target_pairs={{0,1},{1,0},{2,3},{3,2},{4,5},{5,4},{6,7},{7,6},{8,9},{9,8},{10,11... | collective-permute-start | bytes 387080 | tf_op jit(solution)/shard_map/ppermute | solution.py:520
  174.6 3.5 %collective-permute-done.18.refs_4_ = bf16[3,3,56,128]{3,2,1,0:T(8,128)(2,1)S(1)} collective-permute-done((bf16[3,3,56,128]{3,2,1,0:T(8,128)(2,1)S(1)}, bf16[3,3,56,128]{3,2,1,0:T(8,128)(2,1)S(1)}, u32[]{:S(2)}, u32[]{:S(2)}) %collective-permute-start.18) | collective-permute-done | bytes 129056 | tf_op jit(solution)/shard_map/ppermute | solution.py:520
  178.1 3.2 %advect.1 = f32[3,3,32,256]{3,2,1,0:T(8,128)} custom-call(s32[1]{0:T(128)} %bitcast.flip_ref.refs_0_, f32[3,3,32,256]{3,2,1,0:T(8,128)S(1)} %get-tuple-element.40.refs_1_, bf16[3,3,32,256]{3,2,1,0:T(8,128)(2,1)S(1)} %collective-permute-done.13.refs_2_, bf16[3,3,56,128]{3,2,1,0:T(8,128)(2,1)S(1)} %frame.1.refs_3_, ...), custom_call_target="tpu_custom_call" | custom-call | tf_op jit(solution)/shard_map/advect/pallas_call | solution.py:422
  (83 shorter events, 20.7 us)
Async XLA Ops:
  6.5 58.0 %all-gather.4.cloned.1.call-start = ((), (), s32[]{:S(2)}) async-start(), calls=%async_computation.3 | async-start | bytes 7077888 | tf_op jit(solution)/shard_map/all_gather | solution.py:474
  9.8 52.7 %all-to-all-start = ((bf16[32,72,256]{2,1,0:T(8,128)(2,1)}), bf16[32,72,256]{2,1,0:T(8,128)(2,1)S(1)}, u32[]{:S(2)}, u32[]{:S(2)}) async-start(bf16[32,72,256]{2,1,0:T(8,128)(2,1)} %taper_slices.1), calls=%async_computation | async-start | bytes 2359296 | tf_op jit(solution)/shard_map/all_to_all | solution.py:477
  25.3 76.1 %all-gather.6.cloned.1.call-start = ((), (), s32[]{:S(2)}) async-start(), calls=%async_computation.4 | async-start | bytes 2359296 | tf_op jit(solution)/shard_map/all_gather | solution.py:501
  27.4 10.8 %collective-permute-start.2 = (bf16[5,3,32,128]{3,2,1,0:T(8,128)(2,1)S(1)}, bf16[5,3,32,128]{3,2,1,0:T(8,128)(2,1)S(1)}, u32[]{:S(2)}, u32[]{:S(2)}) collective-permute-start(bf16[5,3,32,128]{3,2,1,0:T(8,128)(2,1)S(1)} %get-tuple-element.49), channel_id=1, source_target_pairs={{0,2},{2,4},{4,6},{6,8},{8,10},{10,12},{12,14},{1,3},{3,5},{5,7},{... | collective-permute-start | bytes 368648 | tf_op jit(solution)/shard_map/ppermute | solution.py:450
  29.3 8.9 %collective-permute-start.1 = (bf16[5,3,32,128]{3,2,1,0:T(8,128)(2,1)S(1)}, bf16[5,3,32,128]{3,2,1,0:T(8,128)(2,1)S(1)}, u32[]{:S(2)}, u32[]{:S(2)}) collective-permute-start(bf16[5,3,32,128]{3,2,1,0:T(8,128)(2,1)S(1)} %get-tuple-element.50), channel_id=1, source_target_pairs={{2,0},{4,2},{6,4},{8,6},{10,8},{12,10},{14,12},{3,1},{5,3},{7,5},{... | collective-permute-start | bytes 368648 | tf_op jit(solution)/shard_map/ppermute | solution.py:451
  36.2 23.2 %copy-start.10 = (bf16[3,2,3,32,256]{4,3,2,1,0:T(8,128)(2,1)}, bf16[3,2,3,32,256]{4,3,2,1,0:T(8,128)(2,1)S(1)}, u32[]{:S(2)}) copy-start(bf16[3,2,3,32,256]{4,3,2,1,0:T(8,128)(2,1)S(1)} %get-tuple-element.34.refs_0_) | copy-start | bytes 884740
  36.2 23.2 %copy-start.11 = (bf16[3,2,3,32,256]{4,3,2,1,0:T(8,128)(2,1)}, bf16[3,2,3,32,256]{4,3,2,1,0:T(8,128)(2,1)S(1)}, u32[]{:S(2)}) copy-start(bf16[3,2,3,32,256]{4,3,2,1,0:T(8,128)(2,1)S(1)} %get-tuple-element.35.refs_1_) | copy-start | bytes 884740
  36.2 23.4 %copy-start.12 = (bf16[3,2,3,32,256]{4,3,2,1,0:T(8,128)(2,1)}, bf16[3,2,3,32,256]{4,3,2,1,0:T(8,128)(2,1)S(1)}, u32[]{:S(2)}) copy-start(bf16[3,2,3,32,256]{4,3,2,1,0:T(8,128)(2,1)S(1)} %get-tuple-element.36.refs_2_) | copy-start | bytes 884740
  36.2 23.4 %collective-permute-start = (bf16[3,2,3,32,256]{4,3,2,1,0:T(8,128)(2,1)S(1)}, bf16[3,2,3,32,256]{4,3,2,1,0:T(8,128)(2,1)S(1)}, u32[]{:S(2)}, u32[]{:S(2)}) collective-permute-start(bf16[3,2,3,32,256]{4,3,2,1,0:T(8,128)(2,1)S(1)} %get-tuple-element.26), channel_id=1, source_target_pairs={{0,2},{2,0},{4,6},{6,4},{8,10},{10,8},{12,14},{14,12},{1,3},{3,1},... | collective-permute-start | bytes 884744 | tf_op jit(solution)/shard_map/ppermute | solution.py:487
  38.2 21.2 %collective-permute-start.4 = (bf16[5,3,8,384]{3,2,1,0:T(8,128)(2,1)S(1)}, bf16[5,3,8,384]{3,2,1,0:T(8,128)(2,1)S(1)}, u32[]{:S(2)}, u32[]{:S(2)}) collective-permute-start(bf16[5,3,8,384]{3,2,1,0:T(8,128)(2,1)S(1)} %get-tuple-element.47), channel_id=1, source_target_pairs={{0,16},{16,32},{32,48},{48,64},{64,80},{80,96},{96,112},{112,128},... | collective-permute-start | bytes 276488 | tf_op jit(solution)/shard_map/ppermute | solution.py:450
  42.5 16.9 %collective-permute-start.3 = (bf16[5,3,8,384]{3,2,1,0:T(8,128)(2,1)S(1)}, bf16[5,3,8,384]{3,2,1,0:T(8,128)(2,1)S(1)}, u32[]{:S(2)}, u32[]{:S(2)}) collective-permute-start(bf16[5,3,8,384]{3,2,1,0:T(8,128)(2,1)S(1)} %get-tuple-element.48), channel_id=1, source_target_pairs={{16,0},{32,16},{48,32},{64,48},{80,64},{96,80},{112,96},{128,112},... | collective-permute-start | bytes 276488 | tf_op jit(solution)/shard_map/ppermute | solution.py:451
  62.6 6.9 %collective-permute-start.5 = (bf16[32,8,256]{2,1,0:T(8,128)(2,1)S(1)}, bf16[32,8,256]{2,1,0:T(8,128)(2,1)S(1)}, u32[]{:S(2)}, u32[]{:S(2)}) collective-permute-start(bf16[32,8,256]{2,1,0:T(8,128)(2,1)S(1)} %row_part.1.own_ref), channel_id=1, source_target_pairs={{0,1},{1,0},{2,3},{3,2},{4,5},{5,4},{6,7},{7,6},{8,9},{9,8},{10,11... | collective-permute-start | bytes 393224 | tf_op jit(solution)/shard_map/ppermute | solution.py:499
  70.2 35.3 %all-to-all-start.1 = ((bf16[32,3,32,128]{3,2,1,0:T(8,128)(2,1)}), bf16[32,3,32,128]{3,2,1,0:T(8,128)(2,1)S(1)}, u32[]{:S(2)}, u32[]{:S(2)}) async-start(bf16[32,3,32,128]{3,2,1,0:T(8,128)(2,1)} %after.4.refs_3_), calls=%async_computation.1 | async-start | bytes 1572864 | tf_op jit(solution)/shard_map/all_to_all | solution.py:503
  78.1 27.4 %collective-permute-start.9 = (bf16[5,3,40,384]{3,2,1,0:T(8,128)(2,1)}, bf16[5,3,40,384]{3,2,1,0:T(8,128)(2,1)S(1)}, u32[]{:S(2)}, u32[]{:S(2)}) collective-permute-start(bf16[5,3,40,384]{3,2,1,0:T(8,128)(2,1)} %after.6), channel_id=1, source_target_pairs={{0,1},{1,0},{2,3},{3,2},{4,5},{5,4},{6,7},{7,6},{8,9},{9,8},{10,11... | collective-permute-start | bytes 1382408 | tf_op jit(solution)/shard_map/ppermute | solution.py:496
  81.2 24.3 %collective-permute-start.6 = (bf16[3,2,3,32,256]{4,3,2,1,0:T(8,128)(2,1)}, bf16[3,2,3,32,256]{4,3,2,1,0:T(8,128)(2,1)}, u32[]{:S(2)}, u32[]{:S(2)}) collective-permute-start(bf16[3,2,3,32,256]{4,3,2,1,0:T(8,128)(2,1)} %get-tuple-element.30), channel_id=1, source_target_pairs={{0,4},{2,6},{4,0},{6,2},{8,12},{10,14},{12,8},{14,10},{1,5},{3,7},... | collective-permute-start | bytes 884744 | tf_op jit(solution)/shard_map/ppermute | solution.py:487
  84.3 21.2 %collective-permute-start.7 = (bf16[3,2,3,32,256]{4,3,2,1,0:T(8,128)(2,1)}, bf16[3,2,3,32,256]{4,3,2,1,0:T(8,128)(2,1)}, u32[]{:S(2)}, u32[]{:S(2)}) collective-permute-start(bf16[3,2,3,32,256]{4,3,2,1,0:T(8,128)(2,1)} %get-tuple-element.31), channel_id=1, source_target_pairs={{0,6},{2,4},{4,2},{6,0},{8,14},{10,12},{12,10},{14,8},{1,7},{3,5},... | collective-permute-start | bytes 884744 | tf_op jit(solution)/shard_map/ppermute | solution.py:487
  86.2 19.3 %collective-permute-start.8 = (bf16[3,2,3,32,256]{4,3,2,1,0:T(8,128)(2,1)}, bf16[3,2,3,32,256]{4,3,2,1,0:T(8,128)(2,1)}, u32[]{:S(2)}, u32[]{:S(2)}) collective-permute-start(bf16[3,2,3,32,256]{4,3,2,1,0:T(8,128)(2,1)} %get-tuple-element.32), channel_id=1, source_target_pairs={{0,12},{2,14},{4,8},{6,10},{8,4},{10,6},{12,0},{14,2},{1,13},{3,15... | collective-permute-start | bytes 884744 | tf_op jit(solution)/shard_map/ppermute | solution.py:487
  107.7 38.1 %copy-start.6 = (bf16[3,2,3,32,256]{4,3,2,1,0:T(8,128)(2,1)S(1)}, bf16[3,2,3,32,256]{4,3,2,1,0:T(8,128)(2,1)}, u32[]{:S(2)}) copy-start(bf16[3,2,3,32,256]{4,3,2,1,0:T(8,128)(2,1)} %copy-done.5) | copy-start | bytes 884740
  107.7 38.1 %copy-start.17 = (bf16[3,2,3,32,256]{4,3,2,1,0:T(8,128)(2,1)S(1)}, bf16[3,2,3,32,256]{4,3,2,1,0:T(8,128)(2,1)}, u32[]{:S(2)}) copy-start(bf16[3,2,3,32,256]{4,3,2,1,0:T(8,128)(2,1)} %copy-done.16) | copy-start | bytes 884740
  107.7 38.1 %all-to-all-start.2 = ((bf16[32,3,32,128]{3,2,1,0:T(8,128)(2,1)}), bf16[32,3,32,128]{3,2,1,0:T(8,128)(2,1)S(1)}, u32[]{:S(2)}, u32[]{:S(2)}) async-start(bf16[32,3,32,128]{3,2,1,0:T(8,128)(2,1)} %rows_pass.1.refs_3_), calls=%async_computation.2 | async-start | bytes 1572864 | tf_op jit(solution)/shard_map/all_to_all | solution.py:506
  120.0 58.2 %copy-start.4 = (f32[3,3,32,256]{3,2,1,0:T(8,128)S(1)}, f32[3,3,32,256]{3,2,1,0:T(8,128)}, u32[]{:S(2)}) copy-start(f32[3,3,32,256]{3,2,1,0:T(8,128)} %refs_5_.1) | copy-start | bytes 884740
  120.0 58.2 %copy-start.8 = (bf16[5,3,8,384]{3,2,1,0:T(8,128)(2,1)S(1)}, bf16[5,3,8,384]{3,2,1,0:T(8,128)(2,1)}, u32[]{:S(2)}) copy-start(bf16[5,3,8,384]{3,2,1,0:T(8,128)(2,1)} %copy-done.7) | copy-start | bytes 276484
  120.0 58.1 %copy-start.9 = (f32[2,3,32,256]{3,2,1,0:T(8,128)S(1)}, f32[2,3,32,256]{3,2,1,0:T(8,128)}, u32[]{:S(2)}) copy-start(f32[2,3,32,256]{3,2,1,0:T(8,128)} %refs_6_.1) | copy-start | bytes 589828
  120.0 13.8 %collective-permute-start.10 = (bf16[3,2,3,32,256]{4,3,2,1,0:T(8,128)(2,1)}, bf16[3,2,3,32,256]{4,3,2,1,0:T(8,128)(2,1)S(1)}, u32[]{:S(2)}, u32[]{:S(2)}) collective-permute-start(bf16[3,2,3,32,256]{4,3,2,1,0:T(8,128)(2,1)} %get-tuple-element.37), channel_id=1, source_target_pairs={{0,8},{2,10},{4,12},{6,14},{8,0},{10,2},{12,4},{14,6},{1,9},{3,11}... | collective-permute-start | bytes 884744 | tf_op jit(solution)/shard_map/ppermute | solution.py:487
  122.9 14.1 %collective-permute-start.11 = (bf16[3,2,3,32,256]{4,3,2,1,0:T(8,128)(2,1)}, bf16[3,2,3,32,256]{4,3,2,1,0:T(8,128)(2,1)S(1)}, u32[]{:S(2)}, u32[]{:S(2)}) collective-permute-start(bf16[3,2,3,32,256]{4,3,2,1,0:T(8,128)(2,1)} %get-tuple-element.38), channel_id=1, source_target_pairs={{0,10},{2,8},{4,14},{6,12},{8,2},{10,0},{12,6},{14,4},{1,11},{3,9}... | collective-permute-start | bytes 884744 | tf_op jit(solution)/shard_map/ppermute | solution.py:487
  126.3 18.4 %collective-permute-start.12 = (bf16[3,2,3,32,256]{4,3,2,1,0:T(8,128)(2,1)}, bf16[3,2,3,32,256]{4,3,2,1,0:T(8,128)(2,1)S(1)}, u32[]{:S(2)}, u32[]{:S(2)}) collective-permute-start(bf16[3,2,3,32,256]{4,3,2,1,0:T(8,128)(2,1)} %get-tuple-element.39), channel_id=1, source_target_pairs={{0,14},{2,12},{4,10},{6,8},{8,6},{10,4},{12,2},{14,0},{1,15},{3,13... | collective-permute-start | bytes 884744 | tf_op jit(solution)/shard_map/ppermute | solution.py:487
  148.5 5.7 %collective-permute-start.14 = (bf16[3,3,32,128]{3,2,1,0:T(8,128)(2,1)S(1)}, bf16[3,3,32,128]{3,2,1,0:T(8,128)(2,1)S(1)}, u32[]{:S(2)}, u32[]{:S(2)}) collective-permute-start(bf16[3,3,32,128]{3,2,1,0:T(8,128)(2,1)S(1)} %get-tuple-element.42), channel_id=1, source_target_pairs={{0,2},{2,4},{4,6},{6,8},{8,10},{10,12},{12,14},{1,3},{3,5},{5,7},{... | collective-permute-start | bytes 221192 | tf_op jit(solution)/shard_map/ppermute | solution.py:450
  150.4 5.6 %collective-permute-start.15 = (bf16[3,3,32,128]{3,2,1,0:T(8,128)(2,1)S(1)}, bf16[3,3,32,128]{3,2,1,0:T(8,128)(2,1)S(1)}, u32[]{:S(2)}, u32[]{:S(2)}) collective-permute-start(bf16[3,3,32,128]{3,2,1,0:T(8,128)(2,1)S(1)} %get-tuple-element.43), channel_id=1, source_target_pairs={{2,0},{4,2},{6,4},{8,6},{10,8},{12,10},{14,12},{3,1},{5,3},{7,5},{... | collective-permute-start | bytes 221192 | tf_op jit(solution)/shard_map/ppermute | solution.py:451
  156.1 9.7 %collective-permute-start.16 = (bf16[3,3,8,384]{3,2,1,0:T(8,128)(2,1)S(1)}, bf16[3,3,8,384]{3,2,1,0:T(8,128)(2,1)S(1)}, u32[]{:S(2)}, u32[]{:S(2)}) collective-permute-start(bf16[3,3,8,384]{3,2,1,0:T(8,128)(2,1)S(1)} %get-tuple-element.45), channel_id=1, source_target_pairs={{16,0},{32,16},{48,32},{64,48},{80,64},{96,80},{112,96},{128,112},... | collective-permute-start | bytes 165896 | tf_op jit(solution)/shard_map/ppermute | solution.py:451
  161.1 9.8 %collective-permute-start.17 = (bf16[3,3,8,384]{3,2,1,0:T(8,128)(2,1)S(1)}, bf16[3,3,8,384]{3,2,1,0:T(8,128)(2,1)S(1)}, u32[]{:S(2)}, u32[]{:S(2)}) collective-permute-start(bf16[3,3,8,384]{3,2,1,0:T(8,128)(2,1)S(1)} %get-tuple-element.46), channel_id=1, source_target_pairs={{0,16},{16,32},{32,48},{48,64},{64,80},{80,96},{96,112},{112,128},... | collective-permute-start | bytes 165896 | tf_op jit(solution)/shard_map/ppermute | solution.py:450
  163.1 11.5 %collective-permute-start.13 = (bf16[3,3,32,256]{3,2,1,0:T(8,128)(2,1)S(1)}, bf16[3,3,32,256]{3,2,1,0:T(8,128)(2,1)S(1)}, u32[]{:S(2)}, u32[]{:S(2)}) collective-permute-start(bf16[3,3,32,256]{3,2,1,0:T(8,128)(2,1)S(1)} %get-tuple-element.41.body_ref), channel_id=1, source_target_pairs={{0,1},{1,0},{2,3},{3,2},{4,5},{5,4},{6,7},{7,6},{8,9},{9,8},{10,11... | collective-permute-start | bytes 442376 | tf_op jit(solution)/shard_map/ppermute | solution.py:511
  171.0 7.1 %collective-permute-start.18 = (bf16[3,3,56,128]{3,2,1,0:T(8,128)(2,1)S(1)}, bf16[3,3,56,128]{3,2,1,0:T(8,128)(2,1)S(1)}, u32[]{:S(2)}, u32[]{:S(2)}) collective-permute-start(bf16[3,3,56,128]{3,2,1,0:T(8,128)(2,1)S(1)} %frame.1.refs_3_), channel_id=1, source_target_pairs={{0,1},{1,0},{2,3},{3,2},{4,5},{5,4},{6,7},{7,6},{8,9},{9,8},{10,11... | collective-permute-start | bytes 387080 | tf_op jit(solution)/shard_map/ppermute | solution.py:520
  (12 other events, 58.0 us)
Sparse Core Ops, SparseCore 0:
  9.5 50.2 all-gather.3
  70.3 31.1 all-gather.5

commit v5 on v4

--- a/solution.py
+++ b/solution.py
@@ -38,13 +38,13 @@
 def slices_kernel(which_ref, column_ref, row_ref, out_ref):
     peers, height, wide = out_ref.shape
     tall = column_ref.shape[0]
-    narrow = row_ref.shape[1] // 2
+    narrow = row_ref.shape[1]
     out_ref[:, :tall, :] = jnp.broadcast_to(column_ref[...][None], (peers, *column_ref.shape))
-    mine = row_ref[...].astype(F32)
-    mine = jnp.where(which_ref[1] == 1, mine[:, narrow:], mine[:, :narrow]).astype(BF)
-    pieces = [mine[8 * i : 8 * i + 8] for i in range(wide // narrow)]
-    slab = jnp.concatenate(pieces, axis=1)
-    out_ref[:, tall:, :] = jnp.broadcast_to(slab[None], (peers, *slab.shape))
+    for i in range(wide // narrow):
+        piece = row_ref[(height - tall) * i : (height - tall) * (i + 1)]
+        out_ref[:, tall:, i * narrow : (i + 1) * narrow] = jnp.broadcast_to(
+            piece[None], (peers, *piece.shape)
+        )
 
 
 def taper_slices(which, column_taper, row_taper, peers, parts):
@@ -59,7 +59,7 @@
             grid=(1,),
             in_specs=[
                 pl.BlockSpec((tall, wide), lambda i, which: (0, which[0])),
-                pl.BlockSpec((rows, narrow), lambda i, which: (0, which[0])),
+                pl.BlockSpec((rows // 2, narrow), lambda i, which: (which[1], which[0])),
             ],
             out_specs=pl.BlockSpec(shape, lambda i, which: (0, 0, 0)),
         ),
@@ -145,16 +145,15 @@
 
 def join_kernel(flip_ref, parts_ref, out_ref):
     parts, _, count, tall, wide = parts_ref.shape
-    pieces = out_ref.shape[1] // tall
-    narrow = wide // pieces
+    narrow = out_ref.shape[3] // parts
     for part in range(parts):
-        for j in range(count):
-            pair = [parts_ref[part, k ^ flip_ref[0], j].astype(F32) for k in range(2)]
-            for i in range(pieces):
-                lanes = slice(i * narrow, (i + 1) * narrow)
-                both = jnp.concatenate([x[:, lanes] for x in pair], axis=1)
-                at = slice(part * 2 * narrow, (part + 1) * 2 * narrow)
-                out_ref[j, i * tall : (i + 1) * tall, at] = both.astype(BF)
+        at = slice(part * narrow, (part + 1) * narrow)
+        for k in range(2):
+            for j in range(count):
+                for i in range(wide // narrow):
+                    out_ref[j, k ^ flip_ref[0], i * tall : (i + 1) * tall, at] = parts_ref[
+                        part, k, j, :, i * narrow : (i + 1) * narrow
+                    ]
 
 
 def joined(flip, taper, rows, blocks):
@@ -163,14 +162,14 @@
     count = peers // blocks
     whole = pl.pallas_call(
         join_kernel,
-        out_shape=shaped((peers, rows, across), BF),
+        out_shape=shaped((peers, 2, rows // 2, across), BF),
         grid_spec=pltpu.PrefetchScalarGridSpec(
             num_scalar_prefetch=1,
             grid=(blocks,),
             in_specs=[
                 pl.BlockSpec((parts, 2, count, tall, wide), lambda i, flip: (0, 0, i, 0, 0))
             ],
-            out_specs=pl.BlockSpec((count, rows, across), lambda i, flip: (i, 0, 0)),
+            out_specs=pl.BlockSpec((count, 2, rows // 2, across), lambda i, flip: (i, 0, 0, 0)),
         ),
         compiler_params=room(6),
         name="joined",

time: 189 us -> 189 us (level)
  no operation moved by 1% of the time
where the time goes in v5:
time: 189 us; the launch traced here: 188 us
  starting transfers between devices  93.1 us (49%)
  waiting for transfers between devices  57.2 us (30%)
  Pallas kernels  17.1 us (9%)
  between operations  13.9 us (7%)
  local copies, waits for them, and re-layouts  4.64 us (2%)
  other arithmetic  2.22 us (1%)
    ppermute x7, starting transfers between devices, exchange(): weights[step] = lax.ppermute(weights[step], 'mem', pairs)  18.7 us
    ppermute x4, waiting for transfers between devices, neighbours(): from_left = lax.ppermute(last, axis, chain(axis, 1))  17.7 us
    ppermute x4, starting transfers between devices, neighbours(): from_right = lax.ppermute(first, axis, chain(axis, -1))  17.1 us
    all_to_all x1, starting transfers between devices, on_device(): lax.all_to_all(taper_slices(jnp.concatenate([at, flip]), column_taper, ro...  15.5 us
    ppermute x7, waiting for transfers between devices, exchange(): weights[step] = lax.ppermute(weights[step], 'mem', pairs)  14.5 us
    all_gather x1, waiting for transfers between devices, on_device(): row_whole = lax.all_gather(both, 'mem', axis=0, tiled=False)  13.3 us
    all_to_all x1, starting transfers between devices, on_device(): localized = lax.all_to_all(tapered, 'row', 0, 0, tiled=True)  12.2 us
    ppermute x4, starting transfers between devices, neighbours(): from_left = lax.ppermute(last, axis, chain(axis, 1))  10.2 us
  transfers between devices with their start and end apart: 24, of which 13 were waited for; matrix products, arithmetic and copies ran while one was open for 1% of the time, Pallas kernels for 5%

profile of v5, /device:TPU:68, one launch (start us, length us, event | category | flops | bytes accessed | tf_op | source)
XLA Modules:
  0.0 188.2 jit_solution(16621174854957900904)
XLA Ops:
  7.3 2.4 %taper_slices.1 = bf16[32,72,256]{2,1,0:T(8,128)(2,1)} custom-call(s32[2]{0:T(128)S(1)} %pad_add_fusion.which_ref, bf16[64,2048]{1,0:T(8,128)(2,1)} %column_ref.1, bf16[32,1024]{1,0:T(8,128)(2,1)} %row_ref.1), custom_call_target="tpu_custom_call" | custom-call | tf_op jit(solution)/shard_map/taper_slices/pallas_call | solution.py:54
  9.8 15.5 %all-to-all-start = ((bf16[32,72,256]{2,1,0:T(8,128)(2,1)}), bf16[32,72,256]{2,1,0:T(8,128)(2,1)S(1)}, u32[]{:S(2)}, u32[]{:S(2)}) async-start(bf16[32,72,256]{2,1,0:T(8,128)(2,1)} %taper_slices.1), calls=%async_computation | async-start | bytes 2359296 | tf_op jit(solution)/shard_map/all_to_all | solution.py:476
  27.3 1.9 %collective-permute-start.2 = (bf16[5,3,32,128]{3,2,1,0:T(8,128)(2,1)S(1)}, bf16[5,3,32,128]{3,2,1,0:T(8,128)(2,1)S(1)}, u32[]{:S(2)}, u32[]{:S(2)}) collective-permute-start(bf16[5,3,32,128]{3,2,1,0:T(8,128)(2,1)S(1)} %get-tuple-element.49), channel_id=1, source_target_pairs={{0,2},{2,4},{4,6},{6,8},{8,10},{10,12},{12,14},{1,3},{3,5},{5,7},{... | collective-permute-start | bytes 368648 | tf_op jit(solution)/shard_map/ppermute | solution.py:449
  29.2 3.6 %collective-permute-start.1 = (bf16[5,3,32,128]{3,2,1,0:T(8,128)(2,1)S(1)}, bf16[5,3,32,128]{3,2,1,0:T(8,128)(2,1)S(1)}, u32[]{:S(2)}, u32[]{:S(2)}) collective-permute-start(bf16[5,3,32,128]{3,2,1,0:T(8,128)(2,1)S(1)} %get-tuple-element.50), channel_id=1, source_target_pairs={{2,0},{4,2},{6,4},{8,6},{10,8},{12,10},{14,12},{3,1},{5,3},{7,5},{... | collective-permute-start | bytes 368648 | tf_op jit(solution)/shard_map/ppermute | solution.py:450
  38.2 4.3 %collective-permute-start.4 = (bf16[5,3,8,384]{3,2,1,0:T(8,128)(2,1)S(1)}, bf16[5,3,8,384]{3,2,1,0:T(8,128)(2,1)S(1)}, u32[]{:S(2)}, u32[]{:S(2)}) collective-permute-start(bf16[5,3,8,384]{3,2,1,0:T(8,128)(2,1)S(1)} %get-tuple-element.47), channel_id=1, source_target_pairs={{0,16},{16,32},{32,48},{48,64},{64,80},{80,96},{96,112},{112,128},... | collective-permute-start | bytes 276488 | tf_op jit(solution)/shard_map/ppermute | solution.py:449
  42.4 4.6 %collective-permute-start.3 = (bf16[5,3,8,384]{3,2,1,0:T(8,128)(2,1)S(1)}, bf16[5,3,8,384]{3,2,1,0:T(8,128)(2,1)S(1)}, u32[]{:S(2)}, u32[]{:S(2)}) collective-permute-start(bf16[5,3,8,384]{3,2,1,0:T(8,128)(2,1)S(1)} %get-tuple-element.48), channel_id=1, source_target_pairs={{16,0},{32,16},{48,32},{64,48},{80,64},{96,80},{112,96},{128,112},... | collective-permute-start | bytes 276488 | tf_op jit(solution)/shard_map/ppermute | solution.py:450
  47.0 12.3 %collective-permute-done.4 = bf16[5,3,8,384]{3,2,1,0:T(8,128)(2,1)S(1)} collective-permute-done((bf16[5,3,8,384]{3,2,1,0:T(8,128)(2,1)S(1)}, bf16[5,3,8,384]{3,2,1,0:T(8,128)(2,1)S(1)}, u32[]{:S(2)}, u32[]{:S(2)}) %collective-permute-start.4) | collective-permute-done | bytes 92192 | tf_op jit(solution)/shard_map/ppermute | solution.py:449
  59.6 2.9 %all-to-all-done.slices_ref.refs_1_ = bf16[32,72,256]{2,1,0:T(8,128)(2,1)S(1)} async-done(((bf16[32,72,256]{2,1,0:T(8,128)(2,1)}), bf16[32,72,256]{2,1,0:T(8,128)(2,1)S(1)}, u32[]{:S(2)}, u32[]{:S(2)}) %all-to-all-start) | async-done | bytes 1179680 | tf_op jit(solution)/shard_map/all_to_all | solution.py:476
  64.5 3.9 %columns_pass.1._.refs_0_ = bf16[32,3,32,128]{3,2,1,0:T(8,128)(2,1)S(1)} custom-call(bf16[1536,2048]{1,0:T(8,128)(2,1)} %all-gather.4.cloned.1.call-done.refs_0_, bf16[32,72,256]{2,1,0:T(8,128)(2,1)S(1)} %all-to-all-done.slices_ref.refs_1_), custom_call_target="tpu_custom_call" | custom-call | tf_op jit(solution)/shard_map/columns_pass/pallas_call | solution.py:116
  70.1 7.8 %all-to-all-start.1 = ((bf16[32,3,32,128]{3,2,1,0:T(8,128)(2,1)}), bf16[32,3,32,128]{3,2,1,0:T(8,128)(2,1)S(1)}, u32[]{:S(2)}, u32[]{:S(2)}) async-start(bf16[32,3,32,128]{3,2,1,0:T(8,128)(2,1)} %after.4.refs_3_), calls=%async_computation.1 | async-start | bytes 1572864 | tf_op jit(solution)/shard_map/all_to_all | solution.py:502
  78.0 3.2 %collective-permute-start.9 = (bf16[5,3,40,384]{3,2,1,0:T(8,128)(2,1)}, bf16[5,3,40,384]{3,2,1,0:T(8,128)(2,1)S(1)}, u32[]{:S(2)}, u32[]{:S(2)}) collective-permute-start(bf16[5,3,40,384]{3,2,1,0:T(8,128)(2,1)} %after.6), channel_id=1, source_target_pairs={{0,1},{1,0},{2,3},{3,2},{4,5},{5,4},{6,7},{7,6},{8,9},{9,8},{10,11... | collective-permute-start | bytes 1382408 | tf_op jit(solution)/shard_map/ppermute | solution.py:495
  81.2 3.0 %collective-permute-start.6 = (bf16[3,2,3,32,256]{4,3,2,1,0:T(8,128)(2,1)}, bf16[3,2,3,32,256]{4,3,2,1,0:T(8,128)(2,1)}, u32[]{:S(2)}, u32[]{:S(2)}) collective-permute-start(bf16[3,2,3,32,256]{4,3,2,1,0:T(8,128)(2,1)} %get-tuple-element.30), channel_id=1, source_target_pairs={{0,4},{2,6},{4,0},{6,2},{8,12},{10,14},{12,8},{14,10},{1,5},{3,7},... | collective-permute-start | bytes 884744 | tf_op jit(solution)/shard_map/ppermute | solution.py:486
  84.2 1.9 %collective-permute-start.7 = (bf16[3,2,3,32,256]{4,3,2,1,0:T(8,128)(2,1)}, bf16[3,2,3,32,256]{4,3,2,1,0:T(8,128)(2,1)}, u32[]{:S(2)}, u32[]{:S(2)}) collective-permute-start(bf16[3,2,3,32,256]{4,3,2,1,0:T(8,128)(2,1)} %get-tuple-element.31), channel_id=1, source_target_pairs={{0,6},{2,4},{4,2},{6,0},{8,14},{10,12},{12,10},{14,8},{1,7},{3,5},... | collective-permute-start | bytes 884744 | tf_op jit(solution)/shard_map/ppermute | solution.py:486
  86.1 1.9 %collective-permute-start.8 = (bf16[3,2,3,32,256]{4,3,2,1,0:T(8,128)(2,1)}, bf16[3,2,3,32,256]{4,3,2,1,0:T(8,128)(2,1)}, u32[]{:S(2)}, u32[]{:S(2)}) collective-permute-start(bf16[3,2,3,32,256]{4,3,2,1,0:T(8,128)(2,1)} %get-tuple-element.32), channel_id=1, source_target_pairs={{0,12},{2,14},{4,8},{6,10},{8,4},{10,6},{12,0},{14,2},{1,13},{3,15... | collective-permute-start | bytes 884744 | tf_op jit(solution)/shard_map/ppermute | solution.py:486
  88.1 13.3 %all-gather.6.cloned.1.call-done = bf16[16,32,8,256]{3,2,1,0:T(8,128)(2,1)} async-done(((bf16[2,32,8,256]{3,2,1,0:T(8,128)(2,1)}), bf16[16,32,8,256]{3,2,1,0:T(8,128)(2,1)}) %all-gather.6.cloned.1.call-update) | async-done | bytes 2097168 | tf_op jit(solution)/shard_map/all_gather | solution.py:500
  101.4 2.6 %joined.1 = bf16[32,2,16,1024]{3,2,1,0:T(8,128)(2,1)S(1)} custom-call(s32[1]{0:T(128)} %bitcast.flip_ref.refs_0_, bf16[8,2,32,8,256]{4,3,2,1,0:T(8,128)(2,1)} %bitcast.6), custom_call_target="tpu_custom_call" | custom-call | tf_op jit(solution)/shard_map/joined/pallas_call | solution.py:163
  105.5 2.2 %rows_pass.1.refs_3_ = bf16[32,3,32,128]{3,2,1,0:T(8,128)(2,1)} custom-call(bf16[1024,1024]{1,0:T(8,128)(2,1)S(1)} %bitcast.5, bf16[32,3,32,128]{3,2,1,0:T(8,128)(2,1)S(1)} %all-to-all-done.1.fields_ref, bf16[3,2,3,32,256]{4,3,2,1,0:T(8,128)(2,1)} %collective-permute-done.6.refs_0_.refs_4_, ...), custom_call_target="tpu_custom_call" | custom-call | tf_op jit(solution)/shard_map/rows_pass/pallas_call | solution.py:195
  107.7 12.2 %all-to-all-start.2 = ((bf16[32,3,32,128]{3,2,1,0:T(8,128)(2,1)}), bf16[32,3,32,128]{3,2,1,0:T(8,128)(2,1)S(1)}, u32[]{:S(2)}, u32[]{:S(2)}) async-start(bf16[32,3,32,128]{3,2,1,0:T(8,128)(2,1)} %rows_pass.1.refs_3_), calls=%async_computation.2 | async-start | bytes 1572864 | tf_op jit(solution)/shard_map/all_to_all | solution.py:505
  120.0 2.9 %collective-permute-start.10 = (bf16[3,2,3,32,256]{4,3,2,1,0:T(8,128)(2,1)}, bf16[3,2,3,32,256]{4,3,2,1,0:T(8,128)(2,1)S(1)}, u32[]{:S(2)}, u32[]{:S(2)}) collective-permute-start(bf16[3,2,3,32,256]{4,3,2,1,0:T(8,128)(2,1)} %get-tuple-element.37), channel_id=1, source_target_pairs={{0,8},{2,10},{4,12},{6,14},{8,0},{10,2},{12,4},{14,6},{1,9},{3,11}... | collective-permute-start | bytes 884744 | tf_op jit(solution)/shard_map/ppermute | solution.py:486
  122.9 3.2 %collective-permute-start.11 = (bf16[3,2,3,32,256]{4,3,2,1,0:T(8,128)(2,1)}, bf16[3,2,3,32,256]{4,3,2,1,0:T(8,128)(2,1)S(1)}, u32[]{:S(2)}, u32[]{:S(2)}) collective-permute-start(bf16[3,2,3,32,256]{4,3,2,1,0:T(8,128)(2,1)} %get-tuple-element.38), channel_id=1, source_target_pairs={{0,10},{2,8},{4,14},{6,12},{8,2},{10,0},{12,6},{14,4},{1,11},{3,9}... | collective-permute-start | bytes 884744 | tf_op jit(solution)/shard_map/ppermute | solution.py:486
  126.1 3.8 %collective-permute-start.12 = (bf16[3,2,3,32,256]{4,3,2,1,0:T(8,128)(2,1)}, bf16[3,2,3,32,256]{4,3,2,1,0:T(8,128)(2,1)S(1)}, u32[]{:S(2)}, u32[]{:S(2)}) collective-permute-start(bf16[3,2,3,32,256]{4,3,2,1,0:T(8,128)(2,1)} %get-tuple-element.39), channel_id=1, source_target_pairs={{0,14},{2,12},{4,10},{6,8},{8,6},{10,4},{12,2},{14,0},{1,15},{3,13... | collective-permute-start | bytes 884744 | tf_op jit(solution)/shard_map/ppermute | solution.py:486
  130.0 3.8 %collective-permute-done.10.refs_6_ = bf16[3,2,3,32,256]{4,3,2,1,0:T(8,128)(2,1)S(1)} collective-permute-done((bf16[3,2,3,32,256]{4,3,2,1,0:T(8,128)(2,1)}, bf16[3,2,3,32,256]{4,3,2,1,0:T(8,128)(2,1)S(1)}, u32[]{:S(2)}, u32[]{:S(2)}) %collective-permute-start.10) | collective-permute-done | bytes 294944 | tf_op jit(solution)/shard_map/ppermute | solution.py:486
  133.8 2.9 %collective-permute-done.11.refs_7_ = bf16[3,2,3,32,256]{4,3,2,1,0:T(8,128)(2,1)S(1)} collective-permute-done((bf16[3,2,3,32,256]{4,3,2,1,0:T(8,128)(2,1)}, bf16[3,2,3,32,256]{4,3,2,1,0:T(8,128)(2,1)S(1)}, u32[]{:S(2)}, u32[]{:S(2)}) %collective-permute-start.11) | collective-permute-done | bytes 294944 | tf_op jit(solution)/shard_map/ppermute | solution.py:486
  136.7 7.8 %collective-permute-done.12.refs_9_ = bf16[3,2,3,32,256]{4,3,2,1,0:T(8,128)(2,1)S(1)} collective-permute-done((bf16[3,2,3,32,256]{4,3,2,1,0:T(8,128)(2,1)}, bf16[3,2,3,32,256]{4,3,2,1,0:T(8,128)(2,1)S(1)}, u32[]{:S(2)}, u32[]{:S(2)}) %collective-permute-start.12) | collective-permute-done | bytes 294944 | tf_op jit(solution)/shard_map/ppermute | solution.py:486
  148.0 2.1 %collective-permute-start.14 = (bf16[3,3,32,128]{3,2,1,0:T(8,128)(2,1)S(1)}, bf16[3,3,32,128]{3,2,1,0:T(8,128)(2,1)S(1)}, u32[]{:S(2)}, u32[]{:S(2)}) collective-permute-start(bf16[3,3,32,128]{3,2,1,0:T(8,128)(2,1)S(1)} %get-tuple-element.42), channel_id=1, source_target_pairs={{0,2},{2,4},{4,6},{6,8},{8,10},{10,12},{12,14},{1,3},{3,5},{5,7},{... | collective-permute-start | bytes 221192 | tf_op jit(solution)/shard_map/ppermute | solution.py:449
  150.0 3.5 %collective-permute-start.15 = (bf16[3,3,32,128]{3,2,1,0:T(8,128)(2,1)S(1)}, bf16[3,3,32,128]{3,2,1,0:T(8,128)(2,1)S(1)}, u32[]{:S(2)}, u32[]{:S(2)}) collective-permute-start(bf16[3,3,32,128]{3,2,1,0:T(8,128)(2,1)S(1)} %get-tuple-element.43), channel_id=1, source_target_pairs={{2,0},{4,2},{6,4},{8,6},{10,8},{12,10},{14,12},{3,1},{5,3},{7,5},{... | collective-permute-start | bytes 221192 | tf_op jit(solution)/shard_map/ppermute | solution.py:450
  155.5 5.4 %collective-permute-start.16 = (bf16[3,3,8,384]{3,2,1,0:T(8,128)(2,1)S(1)}, bf16[3,3,8,384]{3,2,1,0:T(8,128)(2,1)S(1)}, u32[]{:S(2)}, u32[]{:S(2)}) collective-permute-start(bf16[3,3,8,384]{3,2,1,0:T(8,128)(2,1)S(1)} %get-tuple-element.45), channel_id=1, source_target_pairs={{16,0},{32,16},{48,32},{64,48},{80,64},{96,80},{112,96},{128,112},... | collective-permute-start | bytes 165896 | tf_op jit(solution)/shard_map/ppermute | solution.py:450
  162.9 2.7 %collective-permute-start.13 = (bf16[3,3,32,256]{3,2,1,0:T(8,128)(2,1)S(1)}, bf16[3,3,32,256]{3,2,1,0:T(8,128)(2,1)S(1)}, u32[]{:S(2)}, u32[]{:S(2)}) collective-permute-start(bf16[3,3,32,256]{3,2,1,0:T(8,128)(2,1)S(1)} %get-tuple-element.41.body_ref), channel_id=1, source_target_pairs={{0,1},{1,0},{2,3},{3,2},{4,5},{5,4},{6,7},{7,6},{8,9},{9,8},{10,11... | collective-permute-start | bytes 442376 | tf_op jit(solution)/shard_map/ppermute | solution.py:510
  165.7 5.2 %collective-permute-done.17.previous_ref = bf16[3,3,8,384]{3,2,1,0:T(8,128)(2,1)S(1)} collective-permute-done((bf16[3,3,8,384]{3,2,1,0:T(8,128)(2,1)S(1)}, bf16[3,3,8,384]{3,2,1,0:T(8,128)(2,1)S(1)}, u32[]{:S(2)}, u32[]{:S(2)}) %collective-permute-start.17) | collective-permute-done | bytes 55328 | tf_op jit(solution)/shard_map/ppermute | solution.py:449
  170.9 3.6 %collective-permute-start.18 = (bf16[3,3,56,128]{3,2,1,0:T(8,128)(2,1)S(1)}, bf16[3,3,56,128]{3,2,1,0:T(8,128)(2,1)S(1)}, u32[]{:S(2)}, u32[]{:S(2)}) collective-permute-start(bf16[3,3,56,128]{3,2,1,0:T(8,128)(2,1)S(1)} %frame.1.refs_3_), channel_id=1, source_target_pairs={{0,1},{1,0},{2,3},{3,2},{4,5},{5,4},{6,7},{7,6},{8,9},{9,8},{10,11... | collective-permute-start | bytes 387080 | tf_op jit(solution)/shard_map/ppermute | solution.py:519
  174.5 3.6 %collective-permute-done.18.refs_4_ = bf16[3,3,56,128]{3,2,1,0:T(8,128)(2,1)S(1)} collective-permute-done((bf16[3,3,56,128]{3,2,1,0:T(8,128)(2,1)S(1)}, bf16[3,3,56,128]{3,2,1,0:T(8,128)(2,1)S(1)}, u32[]{:S(2)}, u32[]{:S(2)}) %collective-permute-start.18) | collective-permute-done | bytes 129056 | tf_op jit(solution)/shard_map/ppermute | solution.py:519
  178.2 3.2 %advect.1 = f32[3,3,32,256]{3,2,1,0:T(8,128)} custom-call(s32[1]{0:T(128)} %bitcast.flip_ref.refs_0_, f32[3,3,32,256]{3,2,1,0:T(8,128)S(1)} %get-tuple-element.40.refs_1_, bf16[3,3,32,256]{3,2,1,0:T(8,128)(2,1)S(1)} %collective-permute-done.13.refs_2_, bf16[3,3,56,128]{3,2,1,0:T(8,128)(2,1)S(1)} %frame.1.refs_3_, ...), custom_call_target="tpu_custom_call" | custom-call | tf_op jit(solution)/shard_map/advect/pallas_call | solution.py:421
  (83 shorter events, 20.7 us)
Async XLA Ops:
  6.5 57.9 %all-gather.4.cloned.1.call-start = ((), (), s32[]{:S(2)}) async-start(), calls=%async_computation.3 | async-start | bytes 7077888 | tf_op jit(solution)/shard_map/all_gather | solution.py:473
  9.8 52.7 %all-to-all-start = ((bf16[32,72,256]{2,1,0:T(8,128)(2,1)}), bf16[32,72,256]{2,1,0:T(8,128)(2,1)S(1)}, u32[]{:S(2)}, u32[]{:S(2)}) async-start(bf16[32,72,256]{2,1,0:T(8,128)(2,1)} %taper_slices.1), calls=%async_computation | async-start | bytes 2359296 | tf_op jit(solution)/shard_map/all_to_all | solution.py:476
  25.3 76.1 %all-gather.6.cloned.1.call-start = ((), (), s32[]{:S(2)}) async-start(), calls=%async_computation.4 | async-start | bytes 2359296 | tf_op jit(solution)/shard_map/all_gather | solution.py:500
  27.3 10.8 %collective-permute-start.2 = (bf16[5,3,32,128]{3,2,1,0:T(8,128)(2,1)S(1)}, bf16[5,3,32,128]{3,2,1,0:T(8,128)(2,1)S(1)}, u32[]{:S(2)}, u32[]{:S(2)}) collective-permute-start(bf16[5,3,32,128]{3,2,1,0:T(8,128)(2,1)S(1)} %get-tuple-element.49), channel_id=1, source_target_pairs={{0,2},{2,4},{4,6},{6,8},{8,10},{10,12},{12,14},{1,3},{3,5},{5,7},{... | collective-permute-start | bytes 368648 | tf_op jit(solution)/shard_map/ppermute | solution.py:449
  29.2 8.9 %collective-permute-start.1 = (bf16[5,3,32,128]{3,2,1,0:T(8,128)(2,1)S(1)}, bf16[5,3,32,128]{3,2,1,0:T(8,128)(2,1)S(1)}, u32[]{:S(2)}, u32[]{:S(2)}) collective-permute-start(bf16[5,3,32,128]{3,2,1,0:T(8,128)(2,1)S(1)} %get-tuple-element.50), channel_id=1, source_target_pairs={{2,0},{4,2},{6,4},{8,6},{10,8},{12,10},{14,12},{3,1},{5,3},{7,5},{... | collective-permute-start | bytes 368648 | tf_op jit(solution)/shard_map/ppermute | solution.py:450
  36.1 23.2 %copy-start.10 = (bf16[3,2,3,32,256]{4,3,2,1,0:T(8,128)(2,1)}, bf16[3,2,3,32,256]{4,3,2,1,0:T(8,128)(2,1)S(1)}, u32[]{:S(2)}) copy-start(bf16[3,2,3,32,256]{4,3,2,1,0:T(8,128)(2,1)S(1)} %get-tuple-element.34.refs_0_) | copy-start | bytes 884740
  36.2 23.2 %copy-start.11 = (bf16[3,2,3,32,256]{4,3,2,1,0:T(8,128)(2,1)}, bf16[3,2,3,32,256]{4,3,2,1,0:T(8,128)(2,1)S(1)}, u32[]{:S(2)}) copy-start(bf16[3,2,3,32,256]{4,3,2,1,0:T(8,128)(2,1)S(1)} %get-tuple-element.35.refs_1_) | copy-start | bytes 884740
  36.2 23.4 %copy-start.12 = (bf16[3,2,3,32,256]{4,3,2,1,0:T(8,128)(2,1)}, bf16[3,2,3,32,256]{4,3,2,1,0:T(8,128)(2,1)S(1)}, u32[]{:S(2)}) copy-start(bf16[3,2,3,32,256]{4,3,2,1,0:T(8,128)(2,1)S(1)} %get-tuple-element.36.refs_2_) | copy-start | bytes 884740
  36.2 23.4 %collective-permute-start = (bf16[3,2,3,32,256]{4,3,2,1,0:T(8,128)(2,1)S(1)}, bf16[3,2,3,32,256]{4,3,2,1,0:T(8,128)(2,1)S(1)}, u32[]{:S(2)}, u32[]{:S(2)}) collective-permute-start(bf16[3,2,3,32,256]{4,3,2,1,0:T(8,128)(2,1)S(1)} %get-tuple-element.26), channel_id=1, source_target_pairs={{0,2},{2,0},{4,6},{6,4},{8,10},{10,8},{12,14},{14,12},{1,3},{3,1},... | collective-permute-start | bytes 884744 | tf_op jit(solution)/shard_map/ppermute | solution.py:486
  38.2 21.2 %collective-permute-start.4 = (bf16[5,3,8,384]{3,2,1,0:T(8,128)(2,1)S(1)}, bf16[5,3,8,384]{3,2,1,0:T(8,128)(2,1)S(1)}, u32[]{:S(2)}, u32[]{:S(2)}) collective-permute-start(bf16[5,3,8,384]{3,2,1,0:T(8,128)(2,1)S(1)} %get-tuple-element.47), channel_id=1, source_target_pairs={{0,16},{16,32},{32,48},{48,64},{64,80},{80,96},{96,112},{112,128},... | collective-permute-start | bytes 276488 | tf_op jit(solution)/shard_map/ppermute | solution.py:449
  42.4 16.9 %collective-permute-start.3 = (bf16[5,3,8,384]{3,2,1,0:T(8,128)(2,1)S(1)}, bf16[5,3,8,384]{3,2,1,0:T(8,128)(2,1)S(1)}, u32[]{:S(2)}, u32[]{:S(2)}) collective-permute-start(bf16[5,3,8,384]{3,2,1,0:T(8,128)(2,1)S(1)} %get-tuple-element.48), channel_id=1, source_target_pairs={{16,0},{32,16},{48,32},{64,48},{80,64},{96,80},{112,96},{128,112},... | collective-permute-start | bytes 276488 | tf_op jit(solution)/shard_map/ppermute | solution.py:450
  62.5 6.9 %collective-permute-start.5 = (bf16[32,8,256]{2,1,0:T(8,128)(2,1)S(1)}, bf16[32,8,256]{2,1,0:T(8,128)(2,1)S(1)}, u32[]{:S(2)}, u32[]{:S(2)}) collective-permute-start(bf16[32,8,256]{2,1,0:T(8,128)(2,1)S(1)} %row_part.1.own_ref), channel_id=1, source_target_pairs={{0,1},{1,0},{2,3},{3,2},{4,5},{5,4},{6,7},{7,6},{8,9},{9,8},{10,11... | collective-permute-start | bytes 393224 | tf_op jit(solution)/shard_map/ppermute | solution.py:498
  70.1 35.4 %all-to-all-start.1 = ((bf16[32,3,32,128]{3,2,1,0:T(8,128)(2,1)}), bf16[32,3,32,128]{3,2,1,0:T(8,128)(2,1)S(1)}, u32[]{:S(2)}, u32[]{:S(2)}) async-start(bf16[32,3,32,128]{3,2,1,0:T(8,128)(2,1)} %after.4.refs_3_), calls=%async_computation.1 | async-start | bytes 1572864 | tf_op jit(solution)/shard_map/all_to_all | solution.py:502
  78.0 27.5 %collective-permute-start.9 = (bf16[5,3,40,384]{3,2,1,0:T(8,128)(2,1)}, bf16[5,3,40,384]{3,2,1,0:T(8,128)(2,1)S(1)}, u32[]{:S(2)}, u32[]{:S(2)}) collective-permute-start(bf16[5,3,40,384]{3,2,1,0:T(8,128)(2,1)} %after.6), channel_id=1, source_target_pairs={{0,1},{1,0},{2,3},{3,2},{4,5},{5,4},{6,7},{7,6},{8,9},{9,8},{10,11... | collective-permute-start | bytes 1382408 | tf_op jit(solution)/shard_map/ppermute | solution.py:495
  81.2 24.3 %collective-permute-start.6 = (bf16[3,2,3,32,256]{4,3,2,1,0:T(8,128)(2,1)}, bf16[3,2,3,32,256]{4,3,2,1,0:T(8,128)(2,1)}, u32[]{:S(2)}, u32[]{:S(2)}) collective-permute-start(bf16[3,2,3,32,256]{4,3,2,1,0:T(8,128)(2,1)} %get-tuple-element.30), channel_id=1, source_target_pairs={{0,4},{2,6},{4,0},{6,2},{8,12},{10,14},{12,8},{14,10},{1,5},{3,7},... | collective-permute-start | bytes 884744 | tf_op jit(solution)/shard_map/ppermute | solution.py:486
  84.2 21.3 %collective-permute-start.7 = (bf16[3,2,3,32,256]{4,3,2,1,0:T(8,128)(2,1)}, bf16[3,2,3,32,256]{4,3,2,1,0:T(8,128)(2,1)}, u32[]{:S(2)}, u32[]{:S(2)}) collective-permute-start(bf16[3,2,3,32,256]{4,3,2,1,0:T(8,128)(2,1)} %get-tuple-element.31), channel_id=1, source_target_pairs={{0,6},{2,4},{4,2},{6,0},{8,14},{10,12},{12,10},{14,8},{1,7},{3,5},... | collective-permute-start | bytes 884744 | tf_op jit(solution)/shard_map/ppermute | solution.py:486
  86.1 19.4 %collective-permute-start.8 = (bf16[3,2,3,32,256]{4,3,2,1,0:T(8,128)(2,1)}, bf16[3,2,3,32,256]{4,3,2,1,0:T(8,128)(2,1)}, u32[]{:S(2)}, u32[]{:S(2)}) collective-permute-start(bf16[3,2,3,32,256]{4,3,2,1,0:T(8,128)(2,1)} %get-tuple-element.32), channel_id=1, source_target_pairs={{0,12},{2,14},{4,8},{6,10},{8,4},{10,6},{12,0},{14,2},{1,13},{3,15... | collective-permute-start | bytes 884744 | tf_op jit(solution)/shard_map/ppermute | solution.py:486
  107.7 37.6 %copy-start.6 = (bf16[3,2,3,32,256]{4,3,2,1,0:T(8,128)(2,1)S(1)}, bf16[3,2,3,32,256]{4,3,2,1,0:T(8,128)(2,1)}, u32[]{:S(2)}) copy-start(bf16[3,2,3,32,256]{4,3,2,1,0:T(8,128)(2,1)} %copy-done.5) | copy-start | bytes 884740
  107.7 37.6 %copy-start.17 = (bf16[3,2,3,32,256]{4,3,2,1,0:T(8,128)(2,1)S(1)}, bf16[3,2,3,32,256]{4,3,2,1,0:T(8,128)(2,1)}, u32[]{:S(2)}) copy-start(bf16[3,2,3,32,256]{4,3,2,1,0:T(8,128)(2,1)} %copy-done.16) | copy-start | bytes 884740
  107.7 37.6 %all-to-all-start.2 = ((bf16[32,3,32,128]{3,2,1,0:T(8,128)(2,1)}), bf16[32,3,32,128]{3,2,1,0:T(8,128)(2,1)S(1)}, u32[]{:S(2)}, u32[]{:S(2)}) async-start(bf16[32,3,32,128]{3,2,1,0:T(8,128)(2,1)} %rows_pass.1.refs_3_), calls=%async_computation.2 | async-start | bytes 1572864 | tf_op jit(solution)/shard_map/all_to_all | solution.py:505
  120.0 58.2 %copy-start.4 = (f32[3,3,32,256]{3,2,1,0:T(8,128)S(1)}, f32[3,3,32,256]{3,2,1,0:T(8,128)}, u32[]{:S(2)}) copy-start(f32[3,3,32,256]{3,2,1,0:T(8,128)} %refs_5_.1) | copy-start | bytes 884740
  120.0 58.2 %copy-start.8 = (bf16[5,3,8,384]{3,2,1,0:T(8,128)(2,1)S(1)}, bf16[5,3,8,384]{3,2,1,0:T(8,128)(2,1)}, u32[]{:S(2)}) copy-start(bf16[5,3,8,384]{3,2,1,0:T(8,128)(2,1)} %copy-done.7) | copy-start | bytes 276484
  120.0 58.2 %copy-start.9 = (f32[2,3,32,256]{3,2,1,0:T(8,128)S(1)}, f32[2,3,32,256]{3,2,1,0:T(8,128)}, u32[]{:S(2)}) copy-start(f32[2,3,32,256]{3,2,1,0:T(8,128)} %refs_6_.1) | copy-start | bytes 589828
  120.0 13.8 %collective-permute-start.10 = (bf16[3,2,3,32,256]{4,3,2,1,0:T(8,128)(2,1)}, bf16[3,2,3,32,256]{4,3,2,1,0:T(8,128)(2,1)S(1)}, u32[]{:S(2)}, u32[]{:S(2)}) collective-permute-start(bf16[3,2,3,32,256]{4,3,2,1,0:T(8,128)(2,1)} %get-tuple-element.37), channel_id=1, source_target_pairs={{0,8},{2,10},{4,12},{6,14},{8,0},{10,2},{12,4},{14,6},{1,9},{3,11}... | collective-permute-start | bytes 884744 | tf_op jit(solution)/shard_map/ppermute | solution.py:486
  122.9 13.8 %collective-permute-start.11 = (bf16[3,2,3,32,256]{4,3,2,1,0:T(8,128)(2,1)}, bf16[3,2,3,32,256]{4,3,2,1,0:T(8,128)(2,1)S(1)}, u32[]{:S(2)}, u32[]{:S(2)}) collective-permute-start(bf16[3,2,3,32,256]{4,3,2,1,0:T(8,128)(2,1)} %get-tuple-element.38), channel_id=1, source_target_pairs={{0,10},{2,8},{4,14},{6,12},{8,2},{10,0},{12,6},{14,4},{1,11},{3,9}... | collective-permute-start | bytes 884744 | tf_op jit(solution)/shard_map/ppermute | solution.py:486
  126.1 18.4 %collective-permute-start.12 = (bf16[3,2,3,32,256]{4,3,2,1,0:T(8,128)(2,1)}, bf16[3,2,3,32,256]{4,3,2,1,0:T(8,128)(2,1)S(1)}, u32[]{:S(2)}, u32[]{:S(2)}) collective-permute-start(bf16[3,2,3,32,256]{4,3,2,1,0:T(8,128)(2,1)} %get-tuple-element.39), channel_id=1, source_target_pairs={{0,14},{2,12},{4,10},{6,8},{8,6},{10,4},{12,2},{14,0},{1,15},{3,13... | collective-permute-start | bytes 884744 | tf_op jit(solution)/shard_map/ppermute | solution.py:486
  148.0 5.7 %collective-permute-start.14 = (bf16[3,3,32,128]{3,2,1,0:T(8,128)(2,1)S(1)}, bf16[3,3,32,128]{3,2,1,0:T(8,128)(2,1)S(1)}, u32[]{:S(2)}, u32[]{:S(2)}) collective-permute-start(bf16[3,3,32,128]{3,2,1,0:T(8,128)(2,1)S(1)} %get-tuple-element.42), channel_id=1, source_target_pairs={{0,2},{2,4},{4,6},{6,8},{8,10},{10,12},{12,14},{1,3},{3,5},{5,7},{... | collective-permute-start | bytes 221192 | tf_op jit(solution)/shard_map/ppermute | solution.py:449
  150.0 5.5 %collective-permute-start.15 = (bf16[3,3,32,128]{3,2,1,0:T(8,128)(2,1)S(1)}, bf16[3,3,32,128]{3,2,1,0:T(8,128)(2,1)S(1)}, u32[]{:S(2)}, u32[]{:S(2)}) collective-permute-start(bf16[3,3,32,128]{3,2,1,0:T(8,128)(2,1)S(1)} %get-tuple-element.43), channel_id=1, source_target_pairs={{2,0},{4,2},{6,4},{8,6},{10,8},{12,10},{14,12},{3,1},{5,3},{7,5},{... | collective-permute-start | bytes 221192 | tf_op jit(solution)/shard_map/ppermute | solution.py:450
  155.5 10.1 %collective-permute-start.16 = (bf16[3,3,8,384]{3,2,1,0:T(8,128)(2,1)S(1)}, bf16[3,3,8,384]{3,2,1,0:T(8,128)(2,1)S(1)}, u32[]{:S(2)}, u32[]{:S(2)}) collective-permute-start(bf16[3,3,8,384]{3,2,1,0:T(8,128)(2,1)S(1)} %get-tuple-element.45), channel_id=1, source_target_pairs={{16,0},{32,16},{48,32},{64,48},{80,64},{96,80},{112,96},{128,112},... | collective-permute-start | bytes 165896 | tf_op jit(solution)/shard_map/ppermute | solution.py:450
  161.0 9.9 %collective-permute-start.17 = (bf16[3,3,8,384]{3,2,1,0:T(8,128)(2,1)S(1)}, bf16[3,3,8,384]{3,2,1,0:T(8,128)(2,1)S(1)}, u32[]{:S(2)}, u32[]{:S(2)}) collective-permute-start(bf16[3,3,8,384]{3,2,1,0:T(8,128)(2,1)S(1)} %get-tuple-element.46), channel_id=1, source_target_pairs={{0,16},{16,32},{32,48},{48,64},{64,80},{80,96},{96,112},{112,128},... | collective-permute-start | bytes 165896 | tf_op jit(solution)/shard_map/ppermute | solution.py:449
  162.9 11.6 %collective-permute-start.13 = (bf16[3,3,32,256]{3,2,1,0:T(8,128)(2,1)S(1)}, bf16[3,3,32,256]{3,2,1,0:T(8,128)(2,1)S(1)}, u32[]{:S(2)}, u32[]{:S(2)}) collective-permute-start(bf16[3,3,32,256]{3,2,1,0:T(8,128)(2,1)S(1)} %get-tuple-element.41.body_ref), channel_id=1, source_target_pairs={{0,1},{1,0},{2,3},{3,2},{4,5},{5,4},{6,7},{7,6},{8,9},{9,8},{10,11... | collective-permute-start | bytes 442376 | tf_op jit(solution)/shard_map/ppermute | solution.py:510
  170.9 7.2 %collective-permute-start.18 = (bf16[3,3,56,128]{3,2,1,0:T(8,128)(2,1)S(1)}, bf16[3,3,56,128]{3,2,1,0:T(8,128)(2,1)S(1)}, u32[]{:S(2)}, u32[]{:S(2)}) collective-permute-start(bf16[3,3,56,128]{3,2,1,0:T(8,128)(2,1)S(1)} %frame.1.refs_3_), channel_id=1, source_target_pairs={{0,1},{1,0},{2,3},{3,2},{4,5},{5,4},{6,7},{7,6},{8,9},{9,8},{10,11... | collective-permute-start | bytes 387080 | tf_op jit(solution)/shard_map/ppermute | solution.py:519
  (12 other events, 58.0 us)
Sparse Core Ops, SparseCore 0:
  9.5 50.2 all-gather.3
  70.2 31.1 all-gather.5

commit v6 on v5

--- a/solution.py
+++ b/solution.py
@@ -500,7 +500,7 @@
     row_whole = lax.all_gather(both, "mem", axis=0, tiled=False)
     hold((2, 3, 6), [first_pass])
     arrived = lax.all_to_all(first_pass, "row", 0, 0, tiled=True)
-    tapered = rows_pass(joined(flip, row_whole, row_taper.shape[0], 4), arrived, [*exchange((2, 3, 6)), opposite])
+    tapered = rows_pass(joined(flip, row_whole, row_taper.shape[0], 2), arrived, [*exchange((2, 3, 6)), opposite])
     hold((4, 5, 7), [tapered])
     localized = lax.all_to_all(tapered, "row", 0, 0, tiled=True)
     exchange((4, 5, 7))

time: 189 us -> 189 us (level)
  no operation moved by 1% of the time
where the time goes in v6:
time: 189 us; the launch traced here: 188 us
  starting transfers between devices  93.1 us (49%)
  waiting for transfers between devices  57.9 us (31%)
  Pallas kernels  16.4 us (9%)
  between operations  13.9 us (7%)
  local copies, waits for them, and re-layouts  4.64 us (2%)
  other arithmetic  2.22 us (1%)
    ppermute x7, starting transfers between devices, exchange(): weights[step] = lax.ppermute(weights[step], 'mem', pairs)  18.7 us
    ppermute x4, waiting for transfers between devices, neighbours(): from_left = lax.ppermute(last, axis, chain(axis, 1))  17.7 us
    ppermute x4, starting transfers between devices, neighbours(): from_right = lax.ppermute(first, axis, chain(axis, -1))  17.1 us
    all_to_all x1, starting transfers between devices, on_device(): lax.all_to_all(taper_slices(jnp.concatenate([at, flip]), column_taper, ro...  15.5 us
    ppermute x7, waiting for transfers between devices, exchange(): weights[step] = lax.ppermute(weights[step], 'mem', pairs)  14.5 us
    all_gather x1, waiting for transfers between devices, on_device(): row_whole = lax.all_gather(both, 'mem', axis=0, tiled=False)  13.3 us
    all_to_all x1, starting transfers between devices, on_device(): localized = lax.all_to_all(tapered, 'row', 0, 0, tiled=True)  12.2 us
    ppermute x4, starting transfers between devices, neighbours(): from_left = lax.ppermute(last, axis, chain(axis, 1))  10.2 us
  transfers between devices with their start and end apart: 24, of which 13 were waited for; matrix products, arithmetic and copies ran while one was open for 1% of the time, Pallas kernels for 5%

profile of v6, /device:TPU:68, one launch (start us, length us, event | category | flops | bytes accessed | tf_op | source)
XLA Modules:
  0.0 188.2 jit_solution(3593573707821568685)
XLA Ops:
  7.3 2.4 %taper_slices.1 = bf16[32,72,256]{2,1,0:T(8,128)(2,1)} custom-call(s32[2]{0:T(128)S(1)} %pad_add_fusion.which_ref, bf16[64,2048]{1,0:T(8,128)(2,1)} %column_ref.1, bf16[32,1024]{1,0:T(8,128)(2,1)} %row_ref.1), custom_call_target="tpu_custom_call" | custom-call | tf_op jit(solution)/shard_map/taper_slices/pallas_call | solution.py:54
  9.8 15.5 %all-to-all-start = ((bf16[32,72,256]{2,1,0:T(8,128)(2,1)}), bf16[32,72,256]{2,1,0:T(8,128)(2,1)S(1)}, u32[]{:S(2)}, u32[]{:S(2)}) async-start(bf16[32,72,256]{2,1,0:T(8,128)(2,1)} %taper_slices.1), calls=%async_computation | async-start | bytes 2359296 | tf_op jit(solution)/shard_map/all_to_all | solution.py:476
  27.3 1.9 %collective-permute-start.2 = (bf16[5,3,32,128]{3,2,1,0:T(8,128)(2,1)S(1)}, bf16[5,3,32,128]{3,2,1,0:T(8,128)(2,1)S(1)}, u32[]{:S(2)}, u32[]{:S(2)}) collective-permute-start(bf16[5,3,32,128]{3,2,1,0:T(8,128)(2,1)S(1)} %get-tuple-element.49), channel_id=1, source_target_pairs={{0,2},{2,4},{4,6},{6,8},{8,10},{10,12},{12,14},{1,3},{3,5},{5,7},{... | collective-permute-start | bytes 368648 | tf_op jit(solution)/shard_map/ppermute | solution.py:449
  29.2 3.6 %collective-permute-start.1 = (bf16[5,3,32,128]{3,2,1,0:T(8,128)(2,1)S(1)}, bf16[5,3,32,128]{3,2,1,0:T(8,128)(2,1)S(1)}, u32[]{:S(2)}, u32[]{:S(2)}) collective-permute-start(bf16[5,3,32,128]{3,2,1,0:T(8,128)(2,1)S(1)} %get-tuple-element.50), channel_id=1, source_target_pairs={{2,0},{4,2},{6,4},{8,6},{10,8},{12,10},{14,12},{3,1},{5,3},{7,5},{... | collective-permute-start | bytes 368648 | tf_op jit(solution)/shard_map/ppermute | solution.py:450
  38.2 4.3 %collective-permute-start.4 = (bf16[5,3,8,384]{3,2,1,0:T(8,128)(2,1)S(1)}, bf16[5,3,8,384]{3,2,1,0:T(8,128)(2,1)S(1)}, u32[]{:S(2)}, u32[]{:S(2)}) collective-permute-start(bf16[5,3,8,384]{3,2,1,0:T(8,128)(2,1)S(1)} %get-tuple-element.47), channel_id=1, source_target_pairs={{0,16},{16,32},{32,48},{48,64},{64,80},{80,96},{96,112},{112,128},... | collective-permute-start | bytes 276488 | tf_op jit(solution)/shard_map/ppermute | solution.py:449
  42.4 4.6 %collective-permute-start.3 = (bf16[5,3,8,384]{3,2,1,0:T(8,128)(2,1)S(1)}, bf16[5,3,8,384]{3,2,1,0:T(8,128)(2,1)S(1)}, u32[]{:S(2)}, u32[]{:S(2)}) collective-permute-start(bf16[5,3,8,384]{3,2,1,0:T(8,128)(2,1)S(1)} %get-tuple-element.48), channel_id=1, source_target_pairs={{16,0},{32,16},{48,32},{64,48},{80,64},{96,80},{112,96},{128,112},... | collective-permute-start | bytes 276488 | tf_op jit(solution)/shard_map/ppermute | solution.py:450
  47.0 12.3 %collective-permute-done.4 = bf16[5,3,8,384]{3,2,1,0:T(8,128)(2,1)S(1)} collective-permute-done((bf16[5,3,8,384]{3,2,1,0:T(8,128)(2,1)S(1)}, bf16[5,3,8,384]{3,2,1,0:T(8,128)(2,1)S(1)}, u32[]{:S(2)}, u32[]{:S(2)}) %collective-permute-start.4) | collective-permute-done | bytes 92192 | tf_op jit(solution)/shard_map/ppermute | solution.py:449
  59.6 2.9 %all-to-all-done.slices_ref.refs_1_ = bf16[32,72,256]{2,1,0:T(8,128)(2,1)S(1)} async-done(((bf16[32,72,256]{2,1,0:T(8,128)(2,1)}), bf16[32,72,256]{2,1,0:T(8,128)(2,1)S(1)}, u32[]{:S(2)}, u32[]{:S(2)}) %all-to-all-start) | async-done | bytes 1179680 | tf_op jit(solution)/shard_map/all_to_all | solution.py:476
  64.5 3.9 %columns_pass.1._.refs_0_ = bf16[32,3,32,128]{3,2,1,0:T(8,128)(2,1)S(1)} custom-call(bf16[1536,2048]{1,0:T(8,128)(2,1)} %all-gather.4.cloned.1.call-done.refs_0_, bf16[32,72,256]{2,1,0:T(8,128)(2,1)S(1)} %all-to-all-done.slices_ref.refs_1_), custom_call_target="tpu_custom_call" | custom-call | tf_op jit(solution)/shard_map/columns_pass/pallas_call | solution.py:116
  70.1 7.8 %all-to-all-start.1 = ((bf16[32,3,32,128]{3,2,1,0:T(8,128)(2,1)}), bf16[32,3,32,128]{3,2,1,0:T(8,128)(2,1)S(1)}, u32[]{:S(2)}, u32[]{:S(2)}) async-start(bf16[32,3,32,128]{3,2,1,0:T(8,128)(2,1)} %after.4.refs_3_), calls=%async_computation.1 | async-start | bytes 1572864 | tf_op jit(solution)/shard_map/all_to_all | solution.py:502
  78.0 3.2 %collective-permute-start.9 = (bf16[5,3,40,384]{3,2,1,0:T(8,128)(2,1)}, bf16[5,3,40,384]{3,2,1,0:T(8,128)(2,1)S(1)}, u32[]{:S(2)}, u32[]{:S(2)}) collective-permute-start(bf16[5,3,40,384]{3,2,1,0:T(8,128)(2,1)} %after.6), channel_id=1, source_target_pairs={{0,1},{1,0},{2,3},{3,2},{4,5},{5,4},{6,7},{7,6},{8,9},{9,8},{10,11... | collective-permute-start | bytes 1382408 | tf_op jit(solution)/shard_map/ppermute | solution.py:495
  81.2 3.0 %collective-permute-start.6 = (bf16[3,2,3,32,256]{4,3,2,1,0:T(8,128)(2,1)}, bf16[3,2,3,32,256]{4,3,2,1,0:T(8,128)(2,1)}, u32[]{:S(2)}, u32[]{:S(2)}) collective-permute-start(bf16[3,2,3,32,256]{4,3,2,1,0:T(8,128)(2,1)} %get-tuple-element.30), channel_id=1, source_target_pairs={{0,4},{2,6},{4,0},{6,2},{8,12},{10,14},{12,8},{14,10},{1,5},{3,7},... | collective-permute-start | bytes 884744 | tf_op jit(solution)/shard_map/ppermute | solution.py:486
  84.2 1.9 %collective-permute-start.7 = (bf16[3,2,3,32,256]{4,3,2,1,0:T(8,128)(2,1)}, bf16[3,2,3,32,256]{4,3,2,1,0:T(8,128)(2,1)}, u32[]{:S(2)}, u32[]{:S(2)}) collective-permute-start(bf16[3,2,3,32,256]{4,3,2,1,0:T(8,128)(2,1)} %get-tuple-element.31), channel_id=1, source_target_pairs={{0,6},{2,4},{4,2},{6,0},{8,14},{10,12},{12,10},{14,8},{1,7},{3,5},... | collective-permute-start | bytes 884744 | tf_op jit(solution)/shard_map/ppermute | solution.py:486
  86.1 1.9 %collective-permute-start.8 = (bf16[3,2,3,32,256]{4,3,2,1,0:T(8,128)(2,1)}, bf16[3,2,3,32,256]{4,3,2,1,0:T(8,128)(2,1)}, u32[]{:S(2)}, u32[]{:S(2)}) collective-permute-start(bf16[3,2,3,32,256]{4,3,2,1,0:T(8,128)(2,1)} %get-tuple-element.32), channel_id=1, source_target_pairs={{0,12},{2,14},{4,8},{6,10},{8,4},{10,6},{12,0},{14,2},{1,13},{3,15... | collective-permute-start | bytes 884744 | tf_op jit(solution)/shard_map/ppermute | solution.py:486
  88.1 13.3 %all-gather.6.cloned.1.call-done = bf16[16,32,8,256]{3,2,1,0:T(8,128)(2,1)} async-done(((bf16[2,32,8,256]{3,2,1,0:T(8,128)(2,1)}), bf16[16,32,8,256]{3,2,1,0:T(8,128)(2,1)}) %all-gather.6.cloned.1.call-update) | async-done | bytes 2097168 | tf_op jit(solution)/shard_map/all_gather | solution.py:500
  103.2 2.2 %collective-permute-done.9.refs_3_.refs_9_ = bf16[5,3,40,384]{3,2,1,0:T(8,128)(2,1)S(1)} collective-permute-done((bf16[5,3,40,384]{3,2,1,0:T(8,128)(2,1)}, bf16[5,3,40,384]{3,2,1,0:T(8,128)(2,1)S(1)}, u32[]{:S(2)}, u32[]{:S(2)}) %collective-permute-start.9) | collective-permute-done | bytes 460832 | tf_op jit(solution)/shard_map/ppermute | solution.py:495
  105.5 2.2 %rows_pass.1.refs_3_ = bf16[32,3,32,128]{3,2,1,0:T(8,128)(2,1)} custom-call(bf16[1024,1024]{1,0:T(8,128)(2,1)S(1)} %bitcast.5, bf16[32,3,32,128]{3,2,1,0:T(8,128)(2,1)S(1)} %all-to-all-done.1.fields_ref, bf16[3,2,3,32,256]{4,3,2,1,0:T(8,128)(2,1)} %collective-permute-done.6.refs_0_.refs_4_, ...), custom_call_target="tpu_custom_call" | custom-call | tf_op jit(solution)/shard_map/rows_pass/pallas_call | solution.py:195
  107.7 12.2 %all-to-all-start.2 = ((bf16[32,3,32,128]{3,2,1,0:T(8,128)(2,1)}), bf16[32,3,32,128]{3,2,1,0:T(8,128)(2,1)S(1)}, u32[]{:S(2)}, u32[]{:S(2)}) async-start(bf16[32,3,32,128]{3,2,1,0:T(8,128)(2,1)} %rows_pass.1.refs_3_), calls=%async_computation.2 | async-start | bytes 1572864 | tf_op jit(solution)/shard_map/all_to_all | solution.py:505
  120.0 2.9 %collective-permute-start.10 = (bf16[3,2,3,32,256]{4,3,2,1,0:T(8,128)(2,1)}, bf16[3,2,3,32,256]{4,3,2,1,0:T(8,128)(2,1)S(1)}, u32[]{:S(2)}, u32[]{:S(2)}) collective-permute-start(bf16[3,2,3,32,256]{4,3,2,1,0:T(8,128)(2,1)} %get-tuple-element.37), channel_id=1, source_target_pairs={{0,8},{2,10},{4,12},{6,14},{8,0},{10,2},{12,4},{14,6},{1,9},{3,11}... | collective-permute-start | bytes 884744 | tf_op jit(solution)/shard_map/ppermute | solution.py:486
  122.9 3.2 %collective-permute-start.11 = (bf16[3,2,3,32,256]{4,3,2,1,0:T(8,128)(2,1)}, bf16[3,2,3,32,256]{4,3,2,1,0:T(8,128)(2,1)S(1)}, u32[]{:S(2)}, u32[]{:S(2)}) collective-permute-start(bf16[3,2,3,32,256]{4,3,2,1,0:T(8,128)(2,1)} %get-tuple-element.38), channel_id=1, source_target_pairs={{0,10},{2,8},{4,14},{6,12},{8,2},{10,0},{12,6},{14,4},{1,11},{3,9}... | collective-permute-start | bytes 884744 | tf_op jit(solution)/shard_map/ppermute | solution.py:486
  126.1 3.8 %collective-permute-start.12 = (bf16[3,2,3,32,256]{4,3,2,1,0:T(8,128)(2,1)}, bf16[3,2,3,32,256]{4,3,2,1,0:T(8,128)(2,1)S(1)}, u32[]{:S(2)}, u32[]{:S(2)}) collective-permute-start(bf16[3,2,3,32,256]{4,3,2,1,0:T(8,128)(2,1)} %get-tuple-element.39), channel_id=1, source_target_pairs={{0,14},{2,12},{4,10},{6,8},{8,6},{10,4},{12,2},{14,0},{1,15},{3,13... | collective-permute-start | bytes 884744 | tf_op jit(solution)/shard_map/ppermute | solution.py:486
  130.0 3.8 %collective-permute-done.10.refs_6_ = bf16[3,2,3,32,256]{4,3,2,1,0:T(8,128)(2,1)S(1)} collective-permute-done((bf16[3,2,3,32,256]{4,3,2,1,0:T(8,128)(2,1)}, bf16[3,2,3,32,256]{4,3,2,1,0:T(8,128)(2,1)S(1)}, u32[]{:S(2)}, u32[]{:S(2)}) %collective-permute-start.10) | collective-permute-done | bytes 294944 | tf_op jit(solution)/shard_map/ppermute | solution.py:486
  133.8 2.9 %collective-permute-done.11.refs_7_ = bf16[3,2,3,32,256]{4,3,2,1,0:T(8,128)(2,1)S(1)} collective-permute-done((bf16[3,2,3,32,256]{4,3,2,1,0:T(8,128)(2,1)}, bf16[3,2,3,32,256]{4,3,2,1,0:T(8,128)(2,1)S(1)}, u32[]{:S(2)}, u32[]{:S(2)}) %collective-permute-start.11) | collective-permute-done | bytes 294944 | tf_op jit(solution)/shard_map/ppermute | solution.py:486
  136.7 7.8 %collective-permute-done.12.refs_9_ = bf16[3,2,3,32,256]{4,3,2,1,0:T(8,128)(2,1)S(1)} collective-permute-done((bf16[3,2,3,32,256]{4,3,2,1,0:T(8,128)(2,1)}, bf16[3,2,3,32,256]{4,3,2,1,0:T(8,128)(2,1)S(1)}, u32[]{:S(2)}, u32[]{:S(2)}) %collective-permute-start.12) | collective-permute-done | bytes 294944 | tf_op jit(solution)/shard_map/ppermute | solution.py:486
  148.0 2.1 %collective-permute-start.14 = (bf16[3,3,32,128]{3,2,1,0:T(8,128)(2,1)S(1)}, bf16[3,3,32,128]{3,2,1,0:T(8,128)(2,1)S(1)}, u32[]{:S(2)}, u32[]{:S(2)}) collective-permute-start(bf16[3,3,32,128]{3,2,1,0:T(8,128)(2,1)S(1)} %get-tuple-element.42), channel_id=1, source_target_pairs={{0,2},{2,4},{4,6},{6,8},{8,10},{10,12},{12,14},{1,3},{3,5},{5,7},{... | collective-permute-start | bytes 221192 | tf_op jit(solution)/shard_map/ppermute | solution.py:449
  150.0 3.5 %collective-permute-start.15 = (bf16[3,3,32,128]{3,2,1,0:T(8,128)(2,1)S(1)}, bf16[3,3,32,128]{3,2,1,0:T(8,128)(2,1)S(1)}, u32[]{:S(2)}, u32[]{:S(2)}) collective-permute-start(bf16[3,3,32,128]{3,2,1,0:T(8,128)(2,1)S(1)} %get-tuple-element.43), channel_id=1, source_target_pairs={{2,0},{4,2},{6,4},{8,6},{10,8},{12,10},{14,12},{3,1},{5,3},{7,5},{... | collective-permute-start | bytes 221192 | tf_op jit(solution)/shard_map/ppermute | solution.py:450
  155.5 5.4 %collective-permute-start.16 = (bf16[3,3,8,384]{3,2,1,0:T(8,128)(2,1)S(1)}, bf16[3,3,8,384]{3,2,1,0:T(8,128)(2,1)S(1)}, u32[]{:S(2)}, u32[]{:S(2)}) collective-permute-start(bf16[3,3,8,384]{3,2,1,0:T(8,128)(2,1)S(1)} %get-tuple-element.45), channel_id=1, source_target_pairs={{16,0},{32,16},{48,32},{64,48},{80,64},{96,80},{112,96},{128,112},... | collective-permute-start | bytes 165896 | tf_op jit(solution)/shard_map/ppermute | solution.py:450
  162.9 2.7 %collective-permute-start.13 = (bf16[3,3,32,256]{3,2,1,0:T(8,128)(2,1)S(1)}, bf16[3,3,32,256]{3,2,1,0:T(8,128)(2,1)S(1)}, u32[]{:S(2)}, u32[]{:S(2)}) collective-permute-start(bf16[3,3,32,256]{3,2,1,0:T(8,128)(2,1)S(1)} %get-tuple-element.41.body_ref), channel_id=1, source_target_pairs={{0,1},{1,0},{2,3},{3,2},{4,5},{5,4},{6,7},{7,6},{8,9},{9,8},{10,11... | collective-permute-start | bytes 442376 | tf_op jit(solution)/shard_map/ppermute | solution.py:510
  165.7 5.2 %collective-permute-done.17.previous_ref = bf16[3,3,8,384]{3,2,1,0:T(8,128)(2,1)S(1)} collective-permute-done((bf16[3,3,8,384]{3,2,1,0:T(8,128)(2,1)S(1)}, bf16[3,3,8,384]{3,2,1,0:T(8,128)(2,1)S(1)}, u32[]{:S(2)}, u32[]{:S(2)}) %collective-permute-start.17) | collective-permute-done | bytes 55328 | tf_op jit(solution)/shard_map/ppermute | solution.py:449
  170.9 3.6 %collective-permute-start.18 = (bf16[3,3,56,128]{3,2,1,0:T(8,128)(2,1)S(1)}, bf16[3,3,56,128]{3,2,1,0:T(8,128)(2,1)S(1)}, u32[]{:S(2)}, u32[]{:S(2)}) collective-permute-start(bf16[3,3,56,128]{3,2,1,0:T(8,128)(2,1)S(1)} %frame.1.refs_3_), channel_id=1, source_target_pairs={{0,1},{1,0},{2,3},{3,2},{4,5},{5,4},{6,7},{7,6},{8,9},{9,8},{10,11... | collective-permute-start | bytes 387080 | tf_op jit(solution)/shard_map/ppermute | solution.py:519
  174.5 3.6 %collective-permute-done.18.refs_4_ = bf16[3,3,56,128]{3,2,1,0:T(8,128)(2,1)S(1)} collective-permute-done((bf16[3,3,56,128]{3,2,1,0:T(8,128)(2,1)S(1)}, bf16[3,3,56,128]{3,2,1,0:T(8,128)(2,1)S(1)}, u32[]{:S(2)}, u32[]{:S(2)}) %collective-permute-start.18) | collective-permute-done | bytes 129056 | tf_op jit(solution)/shard_map/ppermute | solution.py:519
  178.2 3.2 %advect.1 = f32[3,3,32,256]{3,2,1,0:T(8,128)} custom-call(s32[1]{0:T(128)} %bitcast.flip_ref.refs_0_, f32[3,3,32,256]{3,2,1,0:T(8,128)S(1)} %get-tuple-element.40.refs_1_, bf16[3,3,32,256]{3,2,1,0:T(8,128)(2,1)S(1)} %collective-permute-done.13.refs_2_, bf16[3,3,56,128]{3,2,1,0:T(8,128)(2,1)S(1)} %frame.1.refs_3_, ...), custom_call_target="tpu_custom_call" | custom-call | tf_op jit(solution)/shard_map/advect/pallas_call | solution.py:421
  (83 shorter events, 21.1 us)
Async XLA Ops:
  6.5 57.9 %all-gather.4.cloned.1.call-start = ((), (), s32[]{:S(2)}) async-start(), calls=%async_computation.3 | async-start | bytes 7077888 | tf_op jit(solution)/shard_map/all_gather | solution.py:473
  9.8 52.7 %all-to-all-start = ((bf16[32,72,256]{2,1,0:T(8,128)(2,1)}), bf16[32,72,256]{2,1,0:T(8,128)(2,1)S(1)}, u32[]{:S(2)}, u32[]{:S(2)}) async-start(bf16[32,72,256]{2,1,0:T(8,128)(2,1)} %taper_slices.1), calls=%async_computation | async-start | bytes 2359296 | tf_op jit(solution)/shard_map/all_to_all | solution.py:476
  25.3 76.1 %all-gather.6.cloned.1.call-start = ((), (), s32[]{:S(2)}) async-start(), calls=%async_computation.4 | async-start | bytes 2359296 | tf_op jit(solution)/shard_map/all_gather | solution.py:500
  27.3 10.8 %collective-permute-start.2 = (bf16[5,3,32,128]{3,2,1,0:T(8,128)(2,1)S(1)}, bf16[5,3,32,128]{3,2,1,0:T(8,128)(2,1)S(1)}, u32[]{:S(2)}, u32[]{:S(2)}) collective-permute-start(bf16[5,3,32,128]{3,2,1,0:T(8,128)(2,1)S(1)} %get-tuple-element.49), channel_id=1, source_target_pairs={{0,2},{2,4},{4,6},{6,8},{8,10},{10,12},{12,14},{1,3},{3,5},{5,7},{... | collective-permute-start | bytes 368648 | tf_op jit(solution)/shard_map/ppermute | solution.py:449
  29.2 8.9 %collective-permute-start.1 = (bf16[5,3,32,128]{3,2,1,0:T(8,128)(2,1)S(1)}, bf16[5,3,32,128]{3,2,1,0:T(8,128)(2,1)S(1)}, u32[]{:S(2)}, u32[]{:S(2)}) collective-permute-start(bf16[5,3,32,128]{3,2,1,0:T(8,128)(2,1)S(1)} %get-tuple-element.50), channel_id=1, source_target_pairs={{2,0},{4,2},{6,4},{8,6},{10,8},{12,10},{14,12},{3,1},{5,3},{7,5},{... | collective-permute-start | bytes 368648 | tf_op jit(solution)/shard_map/ppermute | solution.py:450
  36.1 23.2 %copy-start.10 = (bf16[3,2,3,32,256]{4,3,2,1,0:T(8,128)(2,1)}, bf16[3,2,3,32,256]{4,3,2,1,0:T(8,128)(2,1)S(1)}, u32[]{:S(2)}) copy-start(bf16[3,2,3,32,256]{4,3,2,1,0:T(8,128)(2,1)S(1)} %get-tuple-element.34.refs_0_) | copy-start | bytes 884740
  36.2 23.2 %copy-start.11 = (bf16[3,2,3,32,256]{4,3,2,1,0:T(8,128)(2,1)}, bf16[3,2,3,32,256]{4,3,2,1,0:T(8,128)(2,1)S(1)}, u32[]{:S(2)}) copy-start(bf16[3,2,3,32,256]{4,3,2,1,0:T(8,128)(2,1)S(1)} %get-tuple-element.35.refs_1_) | copy-start | bytes 884740
  36.2 23.4 %copy-start.12 = (bf16[3,2,3,32,256]{4,3,2,1,0:T(8,128)(2,1)}, bf16[3,2,3,32,256]{4,3,2,1,0:T(8,128)(2,1)S(1)}, u32[]{:S(2)}) copy-start(bf16[3,2,3,32,256]{4,3,2,1,0:T(8,128)(2,1)S(1)} %get-tuple-element.36.refs_2_) | copy-start | bytes 884740
  36.2 23.4 %collective-permute-start = (bf16[3,2,3,32,256]{4,3,2,1,0:T(8,128)(2,1)S(1)}, bf16[3,2,3,32,256]{4,3,2,1,0:T(8,128)(2,1)S(1)}, u32[]{:S(2)}, u32[]{:S(2)}) collective-permute-start(bf16[3,2,3,32,256]{4,3,2,1,0:T(8,128)(2,1)S(1)} %get-tuple-element.26), channel_id=1, source_target_pairs={{0,2},{2,0},{4,6},{6,4},{8,10},{10,8},{12,14},{14,12},{1,3},{3,1},... | collective-permute-start | bytes 884744 | tf_op jit(solution)/shard_map/ppermute | solution.py:486
  38.2 21.2 %collective-permute-start.4 = (bf16[5,3,8,384]{3,2,1,0:T(8,128)(2,1)S(1)}, bf16[5,3,8,384]{3,2,1,0:T(8,128)(2,1)S(1)}, u32[]{:S(2)}, u32[]{:S(2)}) collective-permute-start(bf16[5,3,8,384]{3,2,1,0:T(8,128)(2,1)S(1)} %get-tuple-element.47), channel_id=1, source_target_pairs={{0,16},{16,32},{32,48},{48,64},{64,80},{80,96},{96,112},{112,128},... | collective-permute-start | bytes 276488 | tf_op jit(solution)/shard_map/ppermute | solution.py:449
  42.4 16.9 %collective-permute-start.3 = (bf16[5,3,8,384]{3,2,1,0:T(8,128)(2,1)S(1)}, bf16[5,3,8,384]{3,2,1,0:T(8,128)(2,1)S(1)}, u32[]{:S(2)}, u32[]{:S(2)}) collective-permute-start(bf16[5,3,8,384]{3,2,1,0:T(8,128)(2,1)S(1)} %get-tuple-element.48), channel_id=1, source_target_pairs={{16,0},{32,16},{48,32},{64,48},{80,64},{96,80},{112,96},{128,112},... | collective-permute-start | bytes 276488 | tf_op jit(solution)/shard_map/ppermute | solution.py:450
  62.5 6.9 %collective-permute-start.5 = (bf16[32,8,256]{2,1,0:T(8,128)(2,1)S(1)}, bf16[32,8,256]{2,1,0:T(8,128)(2,1)S(1)}, u32[]{:S(2)}, u32[]{:S(2)}) collective-permute-start(bf16[32,8,256]{2,1,0:T(8,128)(2,1)S(1)} %row_part.1.own_ref), channel_id=1, source_target_pairs={{0,1},{1,0},{2,3},{3,2},{4,5},{5,4},{6,7},{7,6},{8,9},{9,8},{10,11... | collective-permute-start | bytes 393224 | tf_op jit(solution)/shard_map/ppermute | solution.py:498
  70.1 35.4 %all-to-all-start.1 = ((bf16[32,3,32,128]{3,2,1,0:T(8,128)(2,1)}), bf16[32,3,32,128]{3,2,1,0:T(8,128)(2,1)S(1)}, u32[]{:S(2)}, u32[]{:S(2)}) async-start(bf16[32,3,32,128]{3,2,1,0:T(8,128)(2,1)} %after.4.refs_3_), calls=%async_computation.1 | async-start | bytes 1572864 | tf_op jit(solution)/shard_map/all_to_all | solution.py:502
  78.0 27.5 %collective-permute-start.9 = (bf16[5,3,40,384]{3,2,1,0:T(8,128)(2,1)}, bf16[5,3,40,384]{3,2,1,0:T(8,128)(2,1)S(1)}, u32[]{:S(2)}, u32[]{:S(2)}) collective-permute-start(bf16[5,3,40,384]{3,2,1,0:T(8,128)(2,1)} %after.6), channel_id=1, source_target_pairs={{0,1},{1,0},{2,3},{3,2},{4,5},{5,4},{6,7},{7,6},{8,9},{9,8},{10,11... | collective-permute-start | bytes 1382408 | tf_op jit(solution)/shard_map/ppermute | solution.py:495
  81.2 24.3 %collective-permute-start.6 = (bf16[3,2,3,32,256]{4,3,2,1,0:T(8,128)(2,1)}, bf16[3,2,3,32,256]{4,3,2,1,0:T(8,128)(2,1)}, u32[]{:S(2)}, u32[]{:S(2)}) collective-permute-start(bf16[3,2,3,32,256]{4,3,2,1,0:T(8,128)(2,1)} %get-tuple-element.30), channel_id=1, source_target_pairs={{0,4},{2,6},{4,0},{6,2},{8,12},{10,14},{12,8},{14,10},{1,5},{3,7},... | collective-permute-start | bytes 884744 | tf_op jit(solution)/shard_map/ppermute | solution.py:486
  84.2 21.3 %collective-permute-start.7 = (bf16[3,2,3,32,256]{4,3,2,1,0:T(8,128)(2,1)}, bf16[3,2,3,32,256]{4,3,2,1,0:T(8,128)(2,1)}, u32[]{:S(2)}, u32[]{:S(2)}) collective-permute-start(bf16[3,2,3,32,256]{4,3,2,1,0:T(8,128)(2,1)} %get-tuple-element.31), channel_id=1, source_target_pairs={{0,6},{2,4},{4,2},{6,0},{8,14},{10,12},{12,10},{14,8},{1,7},{3,5},... | collective-permute-start | bytes 884744 | tf_op jit(solution)/shard_map/ppermute | solution.py:486
  86.1 19.4 %collective-permute-start.8 = (bf16[3,2,3,32,256]{4,3,2,1,0:T(8,128)(2,1)}, bf16[3,2,3,32,256]{4,3,2,1,0:T(8,128)(2,1)}, u32[]{:S(2)}, u32[]{:S(2)}) collective-permute-start(bf16[3,2,3,32,256]{4,3,2,1,0:T(8,128)(2,1)} %get-tuple-element.32), channel_id=1, source_target_pairs={{0,12},{2,14},{4,8},{6,10},{8,4},{10,6},{12,0},{14,2},{1,13},{3,15... | collective-permute-start | bytes 884744 | tf_op jit(solution)/shard_map/ppermute | solution.py:486
  107.7 37.6 %copy-start.6 = (bf16[3,2,3,32,256]{4,3,2,1,0:T(8,128)(2,1)S(1)}, bf16[3,2,3,32,256]{4,3,2,1,0:T(8,128)(2,1)}, u32[]{:S(2)}) copy-start(bf16[3,2,3,32,256]{4,3,2,1,0:T(8,128)(2,1)} %copy-done.5) | copy-start | bytes 884740
  107.7 37.6 %copy-start.17 = (bf16[3,2,3,32,256]{4,3,2,1,0:T(8,128)(2,1)S(1)}, bf16[3,2,3,32,256]{4,3,2,1,0:T(8,128)(2,1)}, u32[]{:S(2)}) copy-start(bf16[3,2,3,32,256]{4,3,2,1,0:T(8,128)(2,1)} %copy-done.16) | copy-start | bytes 884740
  107.7 37.6 %all-to-all-start.2 = ((bf16[32,3,32,128]{3,2,1,0:T(8,128)(2,1)}), bf16[32,3,32,128]{3,2,1,0:T(8,128)(2,1)S(1)}, u32[]{:S(2)}, u32[]{:S(2)}) async-start(bf16[32,3,32,128]{3,2,1,0:T(8,128)(2,1)} %rows_pass.1.refs_3_), calls=%async_computation.2 | async-start | bytes 1572864 | tf_op jit(solution)/shard_map/all_to_all | solution.py:505
  120.0 58.2 %copy-start.4 = (f32[3,3,32,256]{3,2,1,0:T(8,128)S(1)}, f32[3,3,32,256]{3,2,1,0:T(8,128)}, u32[]{:S(2)}) copy-start(f32[3,3,32,256]{3,2,1,0:T(8,128)} %refs_5_.1) | copy-start | bytes 884740
  120.0 58.2 %copy-start.8 = (bf16[5,3,8,384]{3,2,1,0:T(8,128)(2,1)S(1)}, bf16[5,3,8,384]{3,2,1,0:T(8,128)(2,1)}, u32[]{:S(2)}) copy-start(bf16[5,3,8,384]{3,2,1,0:T(8,128)(2,1)} %copy-done.7) | copy-start | bytes 276484
  120.0 58.2 %copy-start.9 = (f32[2,3,32,256]{3,2,1,0:T(8,128)S(1)}, f32[2,3,32,256]{3,2,1,0:T(8,128)}, u32[]{:S(2)}) copy-start(f32[2,3,32,256]{3,2,1,0:T(8,128)} %refs_6_.1) | copy-start | bytes 589828
  120.0 13.8 %collective-permute-start.10 = (bf16[3,2,3,32,256]{4,3,2,1,0:T(8,128)(2,1)}, bf16[3,2,3,32,256]{4,3,2,1,0:T(8,128)(2,1)S(1)}, u32[]{:S(2)}, u32[]{:S(2)}) collective-permute-start(bf16[3,2,3,32,256]{4,3,2,1,0:T(8,128)(2,1)} %get-tuple-element.37), channel_id=1, source_target_pairs={{0,8},{2,10},{4,12},{6,14},{8,0},{10,2},{12,4},{14,6},{1,9},{3,11}... | collective-permute-start | bytes 884744 | tf_op jit(solution)/shard_map/ppermute | solution.py:486
  122.9 13.8 %collective-permute-start.11 = (bf16[3,2,3,32,256]{4,3,2,1,0:T(8,128)(2,1)}, bf16[3,2,3,32,256]{4,3,2,1,0:T(8,128)(2,1)S(1)}, u32[]{:S(2)}, u32[]{:S(2)}) collective-permute-start(bf16[3,2,3,32,256]{4,3,2,1,0:T(8,128)(2,1)} %get-tuple-element.38), channel_id=1, source_target_pairs={{0,10},{2,8},{4,14},{6,12},{8,2},{10,0},{12,6},{14,4},{1,11},{3,9}... | collective-permute-start | bytes 884744 | tf_op jit(solution)/shard_map/ppermute | solution.py:486
  126.1 18.4 %collective-permute-start.12 = (bf16[3,2,3,32,256]{4,3,2,1,0:T(8,128)(2,1)}, bf16[3,2,3,32,256]{4,3,2,1,0:T(8,128)(2,1)S(1)}, u32[]{:S(2)}, u32[]{:S(2)}) collective-permute-start(bf16[3,2,3,32,256]{4,3,2,1,0:T(8,128)(2,1)} %get-tuple-element.39), channel_id=1, source_target_pairs={{0,14},{2,12},{4,10},{6,8},{8,6},{10,4},{12,2},{14,0},{1,15},{3,13... | collective-permute-start | bytes 884744 | tf_op jit(solution)/shard_map/ppermute | solution.py:486
  148.0 5.7 %collective-permute-start.14 = (bf16[3,3,32,128]{3,2,1,0:T(8,128)(2,1)S(1)}, bf16[3,3,32,128]{3,2,1,0:T(8,128)(2,1)S(1)}, u32[]{:S(2)}, u32[]{:S(2)}) collective-permute-start(bf16[3,3,32,128]{3,2,1,0:T(8,128)(2,1)S(1)} %get-tuple-element.42), channel_id=1, source_target_pairs={{0,2},{2,4},{4,6},{6,8},{8,10},{10,12},{12,14},{1,3},{3,5},{5,7},{... | collective-permute-start | bytes 221192 | tf_op jit(solution)/shard_map/ppermute | solution.py:449
  150.0 5.5 %collective-permute-start.15 = (bf16[3,3,32,128]{3,2,1,0:T(8,128)(2,1)S(1)}, bf16[3,3,32,128]{3,2,1,0:T(8,128)(2,1)S(1)}, u32[]{:S(2)}, u32[]{:S(2)}) collective-permute-start(bf16[3,3,32,128]{3,2,1,0:T(8,128)(2,1)S(1)} %get-tuple-element.43), channel_id=1, source_target_pairs={{2,0},{4,2},{6,4},{8,6},{10,8},{12,10},{14,12},{3,1},{5,3},{7,5},{... | collective-permute-start | bytes 221192 | tf_op jit(solution)/shard_map/ppermute | solution.py:450
  155.5 10.1 %collective-permute-start.16 = (bf16[3,3,8,384]{3,2,1,0:T(8,128)(2,1)S(1)}, bf16[3,3,8,384]{3,2,1,0:T(8,128)(2,1)S(1)}, u32[]{:S(2)}, u32[]{:S(2)}) collective-permute-start(bf16[3,3,8,384]{3,2,1,0:T(8,128)(2,1)S(1)} %get-tuple-element.45), channel_id=1, source_target_pairs={{16,0},{32,16},{48,32},{64,48},{80,64},{96,80},{112,96},{128,112},... | collective-permute-start | bytes 165896 | tf_op jit(solution)/shard_map/ppermute | solution.py:450
  161.0 9.9 %collective-permute-start.17 = (bf16[3,3,8,384]{3,2,1,0:T(8,128)(2,1)S(1)}, bf16[3,3,8,384]{3,2,1,0:T(8,128)(2,1)S(1)}, u32[]{:S(2)}, u32[]{:S(2)}) collective-permute-start(bf16[3,3,8,384]{3,2,1,0:T(8,128)(2,1)S(1)} %get-tuple-element.46), channel_id=1, source_target_pairs={{0,16},{16,32},{32,48},{48,64},{64,80},{80,96},{96,112},{112,128},... | collective-permute-start | bytes 165896 | tf_op jit(solution)/shard_map/ppermute | solution.py:449
  162.9 11.6 %collective-permute-start.13 = (bf16[3,3,32,256]{3,2,1,0:T(8,128)(2,1)S(1)}, bf16[3,3,32,256]{3,2,1,0:T(8,128)(2,1)S(1)}, u32[]{:S(2)}, u32[]{:S(2)}) collective-permute-start(bf16[3,3,32,256]{3,2,1,0:T(8,128)(2,1)S(1)} %get-tuple-element.41.body_ref), channel_id=1, source_target_pairs={{0,1},{1,0},{2,3},{3,2},{4,5},{5,4},{6,7},{7,6},{8,9},{9,8},{10,11... | collective-permute-start | bytes 442376 | tf_op jit(solution)/shard_map/ppermute | solution.py:510
  170.9 7.2 %collective-permute-start.18 = (bf16[3,3,56,128]{3,2,1,0:T(8,128)(2,1)S(1)}, bf16[3,3,56,128]{3,2,1,0:T(8,128)(2,1)S(1)}, u32[]{:S(2)}, u32[]{:S(2)}) collective-permute-start(bf16[3,3,56,128]{3,2,1,0:T(8,128)(2,1)S(1)} %frame.1.refs_3_), channel_id=1, source_target_pairs={{0,1},{1,0},{2,3},{3,2},{4,5},{5,4},{6,7},{7,6},{8,9},{9,8},{10,11... | collective-permute-start | bytes 387080 | tf_op jit(solution)/shard_map/ppermute | solution.py:519
  (12 other events, 58.0 us)
Sparse Core Ops, SparseCore 0:
  9.5 50.2 all-gather.3
  70.2 31.1 all-gather.5
